TPU v7x, 32 devices: a whole 2x2x4 slice. The times are simulated.
32 devices in a mesh: fsdp: 8 (over y, x, core), tp: 4 (over z).
Axes of the slice: x: 2, y: 2, z: 4, core: 2. Of those that a mesh axis runs over, the one named last changes fastest.
Arguments:
- layer_input: bfloat16 [24576, 512], P(('fsdp', 'tp')), may hold values from -6 to 6
- segment_ids: int32 [24, 1024], P('fsdp'), may hold values from 0 to 15, never falling along the last dimension, each value on 1 to 512 neighbouring positions
- valid_mask: int32 [24576], P(('fsdp', 'tp')), may hold values from 0 to 1, as said below
- teacher: bfloat16 [24576, 512], P(('fsdp', 'tp')), may hold values from -6 to 6
- cotangent: bfloat16 [24576, 512], P(('fsdp', 'tp')), may hold values from -6 to 6
- ln1_gain: bfloat16 [512], P('fsdp'), may hold values from 0.099609375 to 1.8984375
- ln1_bias: bfloat16 [512], P('fsdp'), may hold values from -1.75 to 1.75
- w_q: bfloat16 [512, 512], P('fsdp', 'tp'), may hold values from -0.25 to 0.25
- w_k: bfloat16 [512, 512], P('fsdp', 'tp'), may hold values from -0.25 to 0.25
- w_v: bfloat16 [512, 512], P('fsdp', 'tp'), may hold values from -0.25 to 0.25
- b_q: bfloat16 [8, 64], P('tp', 'fsdp'), may hold values from -3 to 3
- b_v: bfloat16 [8, 64], P('tp', 'fsdp'), may hold values from -3 to 3
- w_o: bfloat16 [512, 512], P('tp', 'fsdp'), may hold values from -1 to 1
- b_o: bfloat16 [512], P('fsdp'), may hold values from -3 to 3
- ln2_gain: bfloat16 [512], P('fsdp'), may hold values from 0.099609375 to 1.8984375
- ln2_bias: bfloat16 [512], P('fsdp'), may hold values from -1.75 to 1.75
- w_up: bfloat16 [512, 2048], P('fsdp', 'tp'), may hold values from -0.25 to 0.25
- b_up: bfloat16 [32, 64], P('tp', 'fsdp'), may hold values from -3 to 3
- w_down: bfloat16 [2048, 512], P('tp', 'fsdp'), may hold values from -0.25 to 0.25
- b_down: bfloat16 [512], P('fsdp'), may hold values from -3 to 3
Outputs:
- layer_out: bfloat16 [24576, 512], P(('fsdp', 'tp'))
- loss: float32 [], replicated
- grad_layer_input: float32 [24576, 512], P(('fsdp', 'tp'))
- grad_ln1_gain: float32 [512], P('fsdp')
- grad_ln1_bias: float32 [512], P('fsdp')
- grad_w_q: float32 [512, 512], P('fsdp', 'tp')
- grad_w_k: float32 [512, 512], P('fsdp', 'tp')
- grad_w_v: float32 [512, 512], P('fsdp', 'tp')
- grad_b_q: float32 [8, 64], P('tp', 'fsdp')
- grad_b_v: float32 [8, 64], P('tp', 'fsdp')
- grad_w_o: float32 [512, 512], P('tp', 'fsdp')
- grad_b_o: float32 [512], P('fsdp')
- grad_ln2_gain: float32 [512], P('fsdp')
- grad_ln2_bias: float32 [512], P('fsdp')
- grad_w_up: float32 [512, 2048], P('fsdp', 'tp')
- grad_b_up: float32 [32, 64], P('tp', 'fsdp')
- grad_w_down: float32 [2048, 512], P('tp', 'fsdp')
- grad_b_down: float32 [512], P('fsdp')
Inputs may be any that keep to these rules, and one draw needn't show every extreme that they name: `segment_ids`: in each sequence the ids never fall, each document holds 1 to 512 positions, and one holds exactly 512. `valid_mask`: the first token of every sequence is 1.
All inputs are finite; a program needn't handle non-finite values.
Results may differ from a plain program's by a relative error of at most 0.014.
Values may be sent and summed in bfloat16 or wider, within the bound.
No kernel may reach another device: no remote copies, remote signals or barrier semaphores. Data moves between devices by JAX's collectives and lax.ppermute only.
A program may use at most 128 MiB of HBM per device.

v0:
```python
import functools

import jax
import jax.numpy as jnp
from jax import lax
from jax.experimental import pallas as pl
from jax.experimental.pallas import tpu as pltpu
from jax.sharding import PartitionSpec as P

D = 512
H = 8
HD = 64
LEN = 1024
HALO = 512
PAIR = 2 * HD
NEG = -1e30
SCALE = HD ** (-0.5)
F32 = jnp.float32
BF16 = jnp.bfloat16
MIB = 1 << 20

CONTRACT_LAST = (((1,), (1,)), ((), ()))


def dot(a, b):
    return jnp.dot(a, b, preferred_element_type=F32)


def dot_t(a, b):
    return lax.dot_general(a, b, CONTRACT_LAST, preferred_element_type=F32)


def normalize(x):
    center = x - jnp.mean(x, axis=-1, keepdims=True)
    rstd = lax.rsqrt(jnp.mean(center * center, axis=-1, keepdims=True) + 1e-05)
    return center * rstd, rstd


def norm_pull(g, gain, xhat, rstd):
    gx = g * gain
    return rstd * (
        gx
        - jnp.mean(gx, axis=-1, keepdims=True)
        - xhat * jnp.mean(gx * xhat, axis=-1, keepdims=True)
    )


def fold(x):
    return jnp.sum(x.reshape(x.shape[0] // 8, 8, x.shape[1]), axis=0)


def rows_of(start, size, unit=128):
    return pl.ds(pl.multiple_of(start, unit), size)


def forward_kernel(
    qb, x_ref, vec_ref, w_ref, idr_ref, idc_ref, n_ref, q_ref, k_ref, v_ref, o_ref, lse_ref, bias_ref, stat_ref
):
    ext, own = x_ref.shape[0], o_ref.shape[0]
    window = HALO + qb

    def project(i, carry):
        rows = rows_of(i * 128, 128)
        xhat, _ = normalize(x_ref[rows, :].astype(F32))
        n1 = (xhat * vec_ref[0:1, :] + vec_ref[1:2, :]).astype(BF16)
        n_ref[rows, :] = n1
        k_ref[rows, :] = dot(n1, w_ref[:, D : 2 * D]).astype(BF16)
        v_ref[rows, :] = (dot(n1, w_ref[:, 2 * D : 3 * D]) + vec_ref[3:4, :]).astype(BF16)
        return carry

    lax.fori_loop(0, ext // 128, project, 0)

    def project_q(i, carry):
        rows = rows_of(i * 128, 128)
        q = dot(n_ref[rows_of(HALO + i * 128, 128), :], w_ref[:, 0:D]) + vec_ref[2:3, :]
        q_ref[rows, :] = q.astype(BF16) * jnp.asarray(SCALE, BF16)
        return carry

    lax.fori_loop(0, own // 128, project_q, 0)

    def query_block(i, carry):
        first = i * qb
        key = lax.broadcasted_iota(jnp.int32, (qb, window), 1)
        query = lax.broadcasted_iota(jnp.int32, (qb, window), 0)
        same = idc_ref[rows_of(HALO + first, qb), :] == idr_ref[:, rows_of(first, window)]
        bias_ref[...] = jnp.where(same & (key <= query + HALO), 0.0, NEG)

        def pair(g, inner):
            lanes = rows_of(g * PAIR, PAIR)
            lane = lax.broadcasted_iota(jnp.int32, (qb, PAIR), 1)
            keys = k_ref[rows_of(first, window), lanes]
            values = v_ref[rows_of(first, window), lanes]
            both = q_ref[rows_of(first, qb), lanes]
            got = None
            for h in range(2):
                mine = (lane < HD) if h == 0 else (lane >= HD)
                s = dot_t(jnp.where(mine, both, jnp.zeros_like(both)), keys) + bias_ref[...]
                top = jnp.max(s, axis=-1, keepdims=True)
                p = jnp.exp(s - top)
                total = jnp.sum(p, axis=-1, keepdims=True)
                o = dot(p.astype(BF16), values) / total
                got = o if h == 0 else jnp.where(mine, o, got)
                stat_ref[...] = jnp.where(lane == 2 * g + h, top + jnp.log(total), stat_ref[...])
            o_ref[rows_of(first, qb), lanes] = got.astype(BF16)
            return inner

        lax.fori_loop(0, D // PAIR, pair, 0)
        lse_ref[:, rows_of(first, qb)] = jnp.transpose(stat_ref[...])[0:H, :]
        return carry

    stat_ref[...] = jnp.zeros_like(stat_ref)
    lax.fori_loop(0, own // qb, query_block, 0)


def attention_forward(x_ext, vecs, w_qkv, id_row, id_col, own):
    ext = x_ext.shape[0]
    qb = 256 if own % 256 == 0 else 128
    shapes = (
        jax.ShapeDtypeStruct((ext, D), BF16),
        jax.ShapeDtypeStruct((own, D), BF16),
        jax.ShapeDtypeStruct((ext, D), BF16),
        jax.ShapeDtypeStruct((ext, D), BF16),
        jax.ShapeDtypeStruct((own, D), BF16),
        jax.ShapeDtypeStruct((H, own), F32),
    )
    return pl.pallas_call(
        functools.partial(forward_kernel, qb),
        out_shape=shapes,
        scratch_shapes=[pltpu.VMEM((qb, HALO + qb), F32), pltpu.VMEM((qb, 128), F32)],
        compiler_params=pltpu.CompilerParams(vmem_limit_bytes=48 * MIB),
        name="attention_forward",
    )(x_ext, vecs, w_qkv, id_row, id_col)


def middle_kernel(
    rb,
    scale_ref,
    x_ref,
    o_ref,
    teacher_ref,
    cot_ref,
    mask_ref,
    vec_ref,
    bup_ref,
    wo_ref,
    wup_ref,
    wdn_ref,
    out_ref,
    gh_ref,
    go_ref,
    delta_ref,
    gwo_ref,
    gwup_ref,
    gwdn_ref,
    small_ref,
    gbup_ref,
    slope_ref,
    hid_ref,
    gpre_ref,
    n2t_ref,
    gmlpt_ref,
    gattnt_ref,
):
    own = x_ref.shape[0]
    ff = wup_ref.shape[1]
    chunk = 512
    small_ref[...] = jnp.zeros_like(small_ref)
    head_of = lax.broadcasted_iota(jnp.int32, (D, 128), 0) // HD
    pick = (head_of == lax.broadcasted_iota(jnp.int32, (D, 128), 1)).astype(BF16)

    def block(i, carry):
        rows = rows_of(i * rb, rb)
        out_bias, gain, offset, down_bias = (vec_ref[j : j + 1, :] for j in range(4))
        h1 = x_ref[rows, :].astype(F32) + dot_t(o_ref[rows, :], wo_ref[...]) + out_bias
        xhat, rstd = normalize(h1)
        n2 = xhat * gain + offset
        n2_low = n2.astype(BF16)
        n2t_ref[:, rows] = jnp.transpose(n2).astype(BF16)
        for c in range(0, ff, chunk):
            pre = dot(n2_low, wup_ref[:, c : c + chunk]) + bup_ref[:, c : c + chunk]
            s = jax.nn.sigmoid(1.702 * pre)
            value = pre * s
            hid_ref[rows, c : c + chunk] = value.astype(BF16)
            slope_ref[:, c : c + chunk] = s + 1.702 * value * (1.0 - s)
        out = h1 + dot_t(hid_ref[rows, :], wdn_ref[...]) + down_bias
        out_ref[rows, :] = out.astype(BF16)
        valid = mask_ref[rows, :]
        diff = (out - teacher_ref[rows, :].astype(F32)) * valid
        g_out = cot_ref[rows, :].astype(F32) + scale_ref[0, 0] * diff
        small_ref[0:8, :] += fold(g_out)
        small_ref[8:16, :] += fold(diff * diff)
        g_mlp = g_out.astype(BF16)
        gmlpt_ref[:, rows] = jnp.transpose(g_out).astype(BF16)
        for c in range(0, ff, chunk):
            g_hid = dot(g_mlp, wdn_ref[:, c : c + chunk])
            gpre_ref[rows, c : c + chunk] = (g_hid * slope_ref[:, c : c + chunk]).astype(BF16)
        g_n2 = dot_t(gpre_ref[rows, :], wup_ref[...])
        small_ref[16:24, :] += fold(g_n2 * xhat)
        small_ref[24:32, :] += fold(g_n2)
        g_h1 = g_out + norm_pull(g_n2, gain, xhat, rstd)
        gh_ref[rows, :] = g_h1
        small_ref[32:40, :] += fold(g_h1)
        gattnt_ref[:, rows] = jnp.transpose(g_h1).astype(BF16)
        g_o = dot(g_h1.astype(BF16), wo_ref[...]).astype(BF16)
        go_ref[rows, :] = g_o
        product = g_o.astype(F32) * o_ref[rows, :].astype(F32)
        high = product.astype(BF16)
        low = (product - high.astype(F32)).astype(BF16)
        delta_ref[:, rows] = jnp.transpose(dot(high, pick) + dot(low, pick))[0:H, :]
        return carry

    lax.fori_loop(0, own // rb, block, 0)
    ones = jnp.ones((8, own), BF16)

    def grads(i, carry):
        cols = rows_of(i * chunk, chunk)
        gwdn_ref[:, cols] = dot(gmlpt_ref[...], hid_ref[:, cols]).astype(BF16)
        gwup_ref[:, cols] = dot(n2t_ref[...], gpre_ref[:, cols]).astype(BF16)
        gbup_ref[:, cols] = dot(ones, gpre_ref[:, cols])
        return carry

    lax.fori_loop(0, ff // chunk, grads, 0)
    gwo_ref[...] = dot(gattnt_ref[...], o_ref[...]).astype(BF16)


def middle(scale, x, o, teacher, cot, mask, vecs, b_up, w_o, w_up, w_dn):
    own, ff = x.shape[0], w_up.shape[1]
    rb = 256 if own % 256 == 0 else 128
    shapes = (
        jax.ShapeDtypeStruct((own, D), BF16),
        jax.ShapeDtypeStruct((own, D), F32),
        jax.ShapeDtypeStruct((own, D), BF16),
        jax.ShapeDtypeStruct((H, own), F32),
        jax.ShapeDtypeStruct((D, D), BF16),
        jax.ShapeDtypeStruct((D, ff), BF16),
        jax.ShapeDtypeStruct((D, ff), BF16),
        jax.ShapeDtypeStruct((40, D), F32),
        jax.ShapeDtypeStruct((8, ff), F32),
    )
    whole = pl.BlockSpec(memory_space=pltpu.VMEM)
    return pl.pallas_call(
        functools.partial(middle_kernel, rb),
        out_shape=shapes,
        in_specs=[pl.BlockSpec(memory_space=pltpu.SMEM)] + [whole] * 10,
        out_specs=[whole] * len(shapes),
        scratch_shapes=[
            pltpu.VMEM((rb, ff), F32),
            pltpu.VMEM((own, ff), BF16),
            pltpu.VMEM((own, ff), BF16),
            pltpu.VMEM((D, own), BF16),
            pltpu.VMEM((D, own), BF16),
            pltpu.VMEM((D, own), BF16),
        ],
        compiler_params=pltpu.CompilerParams(vmem_limit_bytes=56 * MIB),
        name="middle",
    )(scale, x, o, teacher, cot, mask, vecs, b_up, w_o, w_up, w_dn)


def backward_kernel(
    qb,
    q_ref,
    k_ref,
    v_ref,
    go_ref,
    lse_ref,
    delta_ref,
    idr_ref,
    idc_ref,
    n_ref,
    x_ref,
    w_ref,
    gn_halo_ref,
    gn_ref,
    gw_ref,
    small_ref,
    bias_ref,
    kt_ref,
    nt_ref,
    dqt_ref,
    dk_ref,
    dv_ref,
    g_ref,
):
    ext, own = k_ref.shape[0], q_ref.shape[0]
    window = HALO + qb
    dk_ref[...] = jnp.zeros_like(dk_ref)
    dv_ref[...] = jnp.zeros_like(dv_ref)
    small_ref[...] = jnp.zeros_like(small_ref)

    def turn(i, carry):
        rows = rows_of(i * 128, 128)
        kt_ref[:, rows] = jnp.transpose(k_ref[rows, :].astype(F32)).astype(BF16)
        nt_ref[:, rows] = jnp.transpose(n_ref[rows, :].astype(F32)).astype(BF16)
        return carry

    lax.fori_loop(0, ext // 128, turn, 0)

    def query_block(i, carry):
        first = i * qb
        key = lax.broadcasted_iota(jnp.int32, (window, qb), 0)
        query = lax.broadcasted_iota(jnp.int32, (window, qb), 1)
        same = idc_ref[rows_of(first, window), :] == idr_ref[:, rows_of(HALO + first, qb)]
        bias_ref[...] = jnp.where(same & (key <= query + HALO), 0.0, NEG)

        def pair(g, inner):
            lanes = rows_of(g * PAIR, PAIR)
            lane = lax.broadcasted_iota(jnp.int32, (qb, PAIR), 1)
            keys = k_ref[rows_of(first, window), lanes]
            values = v_ref[rows_of(first, window), lanes]
            both_q = q_ref[rows_of(first, qb), lanes]
            both_g = go_ref[rows_of(first, qb), lanes]
            all_lse = lse_ref[:, rows_of(first, qb)]
            all_delta = delta_ref[:, rows_of(first, qb)]
            line = lax.broadcasted_iota(jnp.int32, (H, qb), 0)
            dk, dv = None, None
            for h in range(2):
                head = 2 * g + h
                mine = (lane < HD) if h == 0 else (lane >= HD)
                q = jnp.where(mine, both_q, jnp.zeros_like(both_q))
                g_o = jnp.where(mine, both_g, jnp.zeros_like(both_g))
                lse = jnp.sum(jnp.where(line == head, all_lse, 0.0), axis=0, keepdims=True)
                delta = jnp.sum(jnp.where(line == head, all_delta, 0.0), axis=0, keepdims=True)
                p = jnp.exp(dot_t(keys, q) + bias_ref[...] - lse)
                ds = (p * (dot_t(values, g_o) - delta)).astype(BF16)
                dv_h = dot(p.astype(BF16), g_o)
                dk_h = dot(ds, q)
                dk, dv = (dk_h, dv_h) if h == 0 else (dk + dk_h, dv + dv_h)
                dqt_ref[rows_of(head * HD, HD, HD), rows_of(first, qb)] = dot(
                    kt_ref[rows_of(head * HD, HD, HD), rows_of(first, window)], ds
                )
            dk_ref[rows_of(first, window), lanes] += dk
            dv_ref[rows_of(first, window), lanes] += dv
            return inner

        lax.fori_loop(0, D // PAIR, pair, 0)
        return carry

    lax.fori_loop(0, own // qb, query_block, 0)

    def gather(i, carry):
        rows = rows_of(i * 128, 128)
        g_ref[rows, D : 2 * D] = dk_ref[rows, :].astype(BF16)
        g_ref[rows, 2 * D : 3 * D] = dv_ref[rows, :].astype(BF16)
        return carry

    lax.fori_loop(0, ext // 128, gather, 0)

    def gather_q(i, carry):
        cols = rows_of(i * 128, 128)
        g_ref[rows_of(HALO + i * 128, 128), 0:D] = (jnp.transpose(dqt_ref[:, cols]) * SCALE).astype(BF16)
        return carry

    lax.fori_loop(0, own // 128, gather_q, 0)

    def norms(rows, g_n1):
        xhat, _ = normalize(x_ref[rows, :].astype(F32))
        small_ref[0:8, :] += fold(g_n1 * xhat)
        small_ref[8:16, :] += fold(g_n1)

    def pull_halo(i, carry):
        rows = rows_of(i * 128, 128)
        g_n1 = dot_t(g_ref[rows, D : 3 * D], w_ref[:, D : 3 * D])
        gn_halo_ref[rows, :] = g_n1.astype(BF16)
        norms(rows, g_n1)
        return carry

    lax.fori_loop(0, HALO // 128, pull_halo, 0)

    def pull_own(i, carry):
        rows = rows_of(HALO + i * 128, 128)
        g_n1 = dot_t(g_ref[rows, :], w_ref[...])
        gn_ref[rows_of(i * 128, 128), :] = g_n1
        norms(rows, g_n1)
        return carry

    lax.fori_loop(0, own // 128, pull_own, 0)
    gw_ref[:, 0:D] = dot(nt_ref[:, HALO:], g_ref[HALO:, 0:D]).astype(BF16)
    gw_ref[:, D : 2 * D] = dot(nt_ref[...], g_ref[:, D : 2 * D]).astype(BF16)
    gw_ref[:, 2 * D : 3 * D] = dot(nt_ref[...], g_ref[:, 2 * D : 3 * D]).astype(BF16)
    small_ref[16:24, :] = dot(jnp.ones((8, own), BF16), g_ref[HALO:, 0:D])
    small_ref[24:32, :] = dot(jnp.ones((8, ext), BF16), g_ref[:, 2 * D : 3 * D])


def attention_backward(q, k, v, g_o, lse, delta, id_row, id_col, n1, x_ext, w_qkv):
    ext, own = k.shape[0], q.shape[0]
    qb = 256 if own % 256 == 0 else 128
    shapes = (
        jax.ShapeDtypeStruct((HALO, D), BF16),
        jax.ShapeDtypeStruct((own, D), F32),
        jax.ShapeDtypeStruct((D, 3 * D), BF16),
        jax.ShapeDtypeStruct((32, D), F32),
    )
    return pl.pallas_call(
        functools.partial(backward_kernel, qb),
        out_shape=shapes,
        scratch_shapes=[
            pltpu.VMEM((HALO + qb, qb), F32),
            pltpu.VMEM((D, ext), BF16),
            pltpu.VMEM((D, ext), BF16),
            pltpu.VMEM((D, own), F32),
            pltpu.VMEM((ext, D), F32),
            pltpu.VMEM((ext, D), F32),
            pltpu.VMEM((ext, 3 * D), BF16),
        ],
        compiler_params=pltpu.CompilerParams(vmem_limit_bytes=56 * MIB),
        name="attention_backward",
    )(q, k, v, g_o, lse, delta, id_row, id_col, n1, x_ext, w_qkv)


def finish_kernel(x_ref, gn_ref, gh_ref, vec_ref, out_ref):
    def block(i, carry):
        rows = rows_of(i * 128, 128)
        xhat, rstd = normalize(x_ref[rows, :].astype(F32))
        out_ref[rows, :] = gh_ref[rows, :] + norm_pull(gn_ref[rows, :], vec_ref[0:1, :], xhat, rstd)
        return carry

    lax.fori_loop(0, x_ref.shape[0] // 128, block, 0)


def finish(x, g_n1, g_h1, vecs):
    return pl.pallas_call(
        finish_kernel,
        out_shape=jax.ShapeDtypeStruct(x.shape, F32),
        compiler_params=pltpu.CompilerParams(vmem_limit_bytes=32 * MIB),
        name="finish",
    )(x, g_n1, g_h1, vecs)


def hops(rows):
    plan, left, step = [], HALO, 1
    while left > 0:
        take = min(rows, left)
        plan.append((step, take))
        left, step = left - take, step + 1
    return plan


def local(
    layer_input,
    segment_ids,
    valid_mask,
    teacher,
    cotangent,
    ln1_gain,
    ln1_bias,
    w_q,
    w_k,
    w_v,
    b_q,
    b_v,
    w_o,
    b_o,
    ln2_gain,
    ln2_bias,
    w_up,
    b_up,
    w_down,
    b_down,
):
    fsdp_size = lax.axis_size("fsdp")
    tensor_size = lax.axis_size("tp")
    place = lax.axis_index("tp")
    own = layer_input.shape[0]
    tokens_all = own * fsdp_size * tensor_size
    rows_d = w_q.shape[0]
    cols_h, cols_f = w_q.shape[1], w_up.shape[1]

    parts = []
    for step, take in hops(own):
        route = [(i, i + step) for i in range(tensor_size - step)]
        parts.insert(0, lax.ppermute(layer_input[own - take :], "tp", route))
    x_ext = jnp.concatenate(parts + [layer_input], axis=0)
    ids = segment_ids + LEN * jnp.arange(segment_ids.shape[0], dtype=jnp.int32)[:, None]
    ids = jnp.concatenate([jnp.full((HALO,), -1, jnp.int32), ids.reshape(-1)])
    ids = lax.dynamic_slice_in_dim(ids, place * own, HALO + own)
    id_row, id_col = ids[None, :], ids[:, None]

    pack = jnp.concatenate([w_q, w_k, w_v, w_o.T, w_up, w_down.T], axis=1)
    count = jnp.sum(valid_mask)
    count_high = count // 256
    vectors = jnp.concatenate([ln1_gain, ln1_bias, b_o, ln2_gain, ln2_bias, b_down])
    heads = jnp.concatenate([b_q.reshape(-1), b_v.reshape(-1), b_up.reshape(-1)])
    digits = jnp.stack([count_high, count - 256 * count_high]).astype(BF16)
    small = jnp.concatenate([vectors, heads, digits])
    width = pack.shape[1]
    lines = -(-small.shape[0] // width)
    small = jnp.pad(small, (0, lines * width - small.shape[0])).reshape(lines, width)
    shard = jnp.concatenate([pack, small], axis=0)
    every = lax.all_gather(lax.all_gather(shard, "tp", axis=0), "fsdp", axis=0)
    big = every[:, :, :rows_d, :]

    def columns(start, size):
        part = big[:, :, :, start : start + size]
        return part.transpose(0, 2, 1, 3).reshape(fsdp_size * rows_d, tensor_size * size)

    w_qkv = jnp.concatenate([columns(j * cols_h, cols_h) for j in range(3)], axis=1)
    w_ot = columns(3 * cols_h, cols_h)
    w_up_all = columns(4 * cols_h, cols_f)
    w_dn_all = columns(4 * cols_h + cols_f, cols_f)
    few = every[:, :, rows_d:, :].reshape(fsdp_size, tensor_size, -1).astype(F32)
    six = few[:, 0, : 6 * rows_d].reshape(fsdp_size, 6, rows_d).transpose(1, 0, 2).reshape(6, D)
    at = 6 * rows_d

    def by_head(start, shape):
        size = shape[0] * shape[1]
        part = few[:, :, start : start + size].reshape((fsdp_size, tensor_size) + shape)
        return part.transpose(1, 2, 0, 3).reshape(1, -1)

    bq_all = by_head(at, b_q.shape)
    at += b_q.size
    bv_all = by_head(at, b_v.shape)
    at += b_v.size
    bup_all = by_head(at, b_up.shape)
    at += b_up.size
    valid_total = 256.0 * jnp.sum(few[:, :, at]) + jnp.sum(few[:, :, at + 1])

    vec_one = jnp.concatenate([six[0:2], bq_all, bv_all], axis=0)
    vec_two = jnp.stack([six[2], six[3], six[4], six[5]])
    n1, q, k, v, o, lse = attention_forward(x_ext, vec_one, w_qkv, id_row, id_col, own)
    scale = (tokens_all / valid_total).reshape(1, 1)
    mask = valid_mask.astype(F32)[:, None]
    layer_out, g_h1, g_o, delta, g_wo, g_wup, g_wdn, small_two, g_bup = middle(
        scale, layer_input, o, teacher, cotangent, mask, vec_two, bup_all, w_ot, w_up_all, w_dn_all
    )
    gn_halo, gn_own, g_qkv, small_one = attention_backward(
        q, k, v, g_o, lse, delta, id_row, id_col, n1, x_ext, w_qkv
    )

    total = gn_own
    left = HALO
    for step, take in hops(own):
        route = [(i + step, i) for i in range(tensor_size - step)]
        part = lax.ppermute(gn_halo[left - take : left], "tp", route).astype(F32)
        total = total + jnp.pad(part, ((own - take, 0), (0, 0)))
        left -= take
    grad_input = finish(layer_input, total, g_h1, vec_one)

    def split(grad, size):
        return grad.reshape(fsdp_size, rows_d, tensor_size, size).transpose(0, 2, 1, 3)

    g_pack = jnp.concatenate(
        [split(g_qkv[:, j * D : (j + 1) * D], cols_h) for j in range(3)]
        + [split(g_wo, cols_h), split(g_wup, cols_f), split(g_wdn, cols_f)],
        axis=3,
    )
    ones = [small_one[8 * j : 8 * j + 8].sum(0) for j in range(2)] + [small_one[16], small_one[24]]
    twos = [small_two[8 * j : 8 * j + 8].sum(0) for j in range(5)]
    loss_part = 0.5 / D * jnp.sum(twos[1]) / valid_total
    six_grads = jnp.stack([ones[0], ones[1], twos[4], twos[2], twos[3], twos[0]])
    six_grads = six_grads.reshape(6, fsdp_size, 1, rows_d).transpose(1, 2, 0, 3)
    six_grads = jnp.broadcast_to(
        six_grads.reshape(fsdp_size, 1, -1), (fsdp_size, tensor_size, 6 * rows_d)
    )

    def heads_of(grad, shape):
        part = grad.reshape((tensor_size, shape[0], fsdp_size, shape[1]))
        return part.transpose(2, 0, 1, 3).reshape(fsdp_size, tensor_size, -1)

    loss_high = loss_part.astype(BF16).astype(F32)
    losses = jnp.broadcast_to(
        jnp.stack([loss_high, loss_part - loss_high]), (fsdp_size, tensor_size, 2)
    )
    g_small = jnp.concatenate(
        [
            six_grads,
            heads_of(ones[2], b_q.shape),
            heads_of(ones[3], b_v.shape),
            heads_of(g_bup[0], b_up.shape),
            losses,
        ],
        axis=2,
    ).astype(BF16)
    g_small = jnp.pad(g_small, ((0, 0), (0, 0), (0, lines * width - g_small.shape[2])))
    g_all = jnp.concatenate([g_pack, g_small.reshape(fsdp_size, tensor_size, lines, width)], axis=2)
    mine = lax.psum_scatter(g_all, "fsdp", scatter_dimension=0, tiled=False)
    mine = lax.psum_scatter(mine, "tp", scatter_dimension=0, tiled=False).astype(F32)
    g_mat, g_vec = mine[:rows_d], mine[rows_d:].reshape(-1)
    c3, c4 = 3 * cols_h, 4 * cols_h
    six_out = g_vec[: 6 * rows_d].reshape(6, rows_d)
    at = 6 * rows_d
    grad_bq = g_vec[at : at + b_q.size].reshape(b_q.shape)
    at += b_q.size
    grad_bv = g_vec[at : at + b_v.size].reshape(b_v.shape)
    at += b_v.size
    grad_bup = g_vec[at : at + b_up.size].reshape(b_up.shape)
    at += b_up.size
    loss = g_vec[at] + g_vec[at + 1]
    return (
        layer_out,
        loss,
        grad_input,
        six_out[0],
        six_out[1],
        g_mat[:, 0:cols_h],
        g_mat[:, cols_h : 2 * cols_h],
        g_mat[:, 2 * cols_h : c3],
        grad_bq,
        grad_bv,
        g_mat[:, c3:c4].T,
        six_out[2],
        six_out[3],
        six_out[4],
        g_mat[:, c4 : c4 + cols_f],
        grad_bup,
        g_mat[:, c4 + cols_f :].T,
        six_out[5],
    )


ROWS = D // 8
EXTRA = 8
COLS = D // 4
FFC = 512
WA = 3 * COLS
WF = COLS + 2 * FFC
TALL = D + 16
ALL = (0, 1, 2, 3)
PIECES_A = ((0, ALL), (2, ALL), (4, ALL), (6, ALL), (1, ALL[0:2]), (1, ALL[2:4]), (3, ALL), (5, ALL), (7, ALL))
SMALL = pl.CostEstimate(flops=1, bytes_accessed=1, transcendentals=0)


def about(us):
    return pl.CostEstimate(flops=us * 1000000, bytes_accessed=us * 3300000, transcendentals=0)


ANY = pl.BlockSpec(memory_space=pl.ANY)
VMEM = pl.BlockSpec(memory_space=pltpu.VMEM)
FAR = pl.BlockSpec(memory_space=pl.ANY)


def params(mib):
    return pltpu.CompilerParams(vmem_limit_bytes=mib * MIB)


def lane_of(shape):
    return lax.broadcasted_iota(jnp.int32, shape, len(shape) - 1)


def pack_kernel(
    wq_ref, wk_ref, wv_ref, wo_ref, wup_ref, wdn_ref, g1, b1, bo, g2, b2, bd, bq, bv, bup, mask_ref, a_ref, f_ref
):
    me = lax.axis_index("fsdp")
    a_ref[0:ROWS, 0:COLS] = wq_ref[...]
    a_ref[0:ROWS, COLS : 2 * COLS] = wk_ref[...]
    a_ref[0:ROWS, 2 * COLS : 3 * COLS] = wv_ref[...]
    f_ref[:, 0:COLS] = wo_ref[...]
    f_ref[:, COLS : COLS + FFC] = wup_ref[...]
    f_ref[:, COLS + FFC :] = wdn_ref[...]
    count = jnp.sum(mask_ref[...].astype(F32)).reshape(1, 1)
    high = jnp.floor(count / 256.0)
    lane = lane_of((1, 128))
    digits = jnp.where(lane == 0, high, jnp.where(lane == 1, count - 256.0 * high, 0.0))
    vectors = [r[...].astype(F32).reshape(1, ROWS) for r in (g1, b1, bo, g2, b2, bd)]
    rows = [jnp.concatenate([v, v], axis=1) for v in vectors] + [digits, jnp.zeros((1, 128), F32)]
    a_ref[ROWS:, 0:128] = jnp.concatenate(rows, axis=0).astype(BF16)

    def spread(ref):
        block = ref[...].astype(F32)
        count, piece = block.shape
        lanes = count * HD
        lane = lane_of((1, lanes))
        row = jnp.zeros((1, lanes), F32)
        for i in range(count):
            for j in range(piece):
                at = i * HD + me * piece + j
                row = jnp.where(lane == at, block[i : i + 1, j : j + 1], row)
        return row

    ups = spread(bup)
    rows = [spread(bq), spread(bv)] + [ups[:, 128 * j : 128 * j + 128] for j in range(4)]
    rows.append(jnp.zeros((2, 128), F32))
    a_ref[ROWS:, 128:256] = jnp.concatenate(rows, axis=0).astype(BF16)
    a_ref[ROWS:, 256:384] = jnp.zeros((EXTRA, 128), BF16)


def pack_weights(args):
    return pl.pallas_call(
        pack_kernel,
        out_shape=(
            jax.ShapeDtypeStruct((ROWS + EXTRA, WA), BF16),
            jax.ShapeDtypeStruct((ROWS, WF), BF16),
        ),
        compiler_params=params(60),
        name="pack_weights",
    )(*args)


def project_kernel(
    tokens_all, x_ref, idc_ref, p0, p1, p2, p3, p4, p5, p6, p7, p8,
    q_ref, k_ref, v_ref, kt_ref, nt_ref, w_ref, vec_ref, bup_ref, scale_ref, head_ref, ext_ref, sem
):
    me, place = lax.axis_index("fsdp"), lax.axis_index("tp")
    pieces = (p0, p1, p2, p3, p4, p5, p6, p7, p8)

    def each(act):
        for ref, (mask, steps) in zip(pieces, PIECES_A):
            owner = lax.bitwise_xor(me, mask)
            for i, s in enumerate(steps):
                tp = lax.bitwise_and(place - s + 4, 3)
                act(ref.at[i], 4 * mask + s, owner, tp)

    def start_ext(ref, slot, owner, tp):
        pltpu.make_async_copy(ref.at[pl.ds(ROWS, EXTRA), :], ext_ref.at[slot], sem.at[0]).start()

    def start_w(ref, slot, owner, tp):
        pltpu.make_async_copy(
            ref.at[pl.ds(0, ROWS), :],
            w_ref.at[rows_of(owner * ROWS, ROWS, ROWS), rows_of(tp * WA, WA)],
            sem.at[1],
        ).start()

    each(start_ext)
    each(start_w)
    pltpu.make_async_copy(ext_ref, ext_ref, sem.at[0]).wait()
    lane = lane_of((EXTRA, D))
    vectors = jnp.zeros((EXTRA, D), F32)
    total = jnp.zeros((EXTRA, 128), F32)
    for j in range(8):
        block = ext_ref[4 * j, :, 0:128].astype(F32)
        wide = jnp.concatenate([block] * 4, axis=1)
        vectors = jnp.where(lane // ROWS == lax.bitwise_xor(me, j), wide, vectors)
        for s in range(4):
            total += ext_ref[4 * j + s, :, 0:128].astype(F32)
    vec_ref[...] = vectors
    valid = 256.0 * total[6:7, 0:1] + total[6:7, 1:2]
    scale_ref[...] = jnp.concatenate(
        [jnp.broadcast_to(tokens_all / valid, (4, 128)), jnp.broadcast_to(0.5 / D / valid, (4, 128))], axis=0
    )
    for s in range(4):
        tp = lax.bitwise_and(place - s + 4, 3)
        block = jnp.zeros((EXTRA, 128), F32)
        for j in range(8):
            block += ext_ref[4 * j + s, :, 128:256].astype(F32)
        head_ref[:, rows_of(tp * COLS, COLS)] = block
        for i in range(4):
            bup_ref[:, rows_of(tp * FFC + 128 * i, 128)] = jnp.broadcast_to(block[2 + i : 3 + i], (8, 128))
    pltpu.make_async_copy(w_ref, w_ref, sem.at[1]).wait()

    def own_rows(i, carry):
        rows = rows_of(i * 128, 128)
        n1 = first_norm(x_ref[rows, :], vectors, me, nt_ref, rows)
        made = dot(n1, w_ref[...])
        spare_q, spare_k, spare_v = spare_lanes(idc_ref[rows_of(HALO + i * 128, 128), :])
        for t in range(4):
            lanes = slice(t * COLS, (t + 1) * COLS)
            q = (made[:, t * WA : t * WA + COLS] + head_ref[0:1, lanes]).astype(BF16)
            keep_heads(q_ref, rows, t, q * jnp.asarray(SCALE, BF16), spare_q)
            keep_keys(made[:, t * WA + COLS : (t + 1) * WA], head_ref, k_ref, v_ref, kt_ref, rows, t, spare_k, spare_v)
        return carry

    lax.fori_loop(0, x_ref.shape[0] // 128, own_rows, 0)


DOCS = 48
TERMS = 3


def spare_lanes(ids):
    shape = (ids.shape[0], PAIR)
    at = lax.bitwise_and(lane_of(shape), HD - 1)
    same = at == ids
    ones = jnp.where((at >= DOCS) & (at < DOCS + TERMS), 1.0, 0.0)
    spare_q = jnp.where(same & (at < DOCS), 1.0, 0.0).astype(BF16)
    spare_k = jnp.where(at < DOCS, jnp.where(same, 0.0, NEG), ones).astype(BF16)
    return spare_q, spare_k, ones.astype(BF16)


def three_terms(x):
    high = x.astype(BF16)
    rest = x - high.astype(F32)
    middle = rest.astype(BF16)
    return high, middle, (rest - middle.astype(F32)).astype(BF16)


def keep_heads(ref, rows, pair, value, spare):
    lane = lane_of(value.shape)
    for h in range(2):
        at = (2 * pair + h) * PAIR
        mine = (lane < HD) if h == 0 else (lane >= HD)
        ref[rows, at : at + PAIR] = jnp.where(mine, value, spare)


def first_norm(x, vectors, me, nt_ref, rows):
    xhat, _ = normalize(x.astype(F32))
    n1 = xhat * vectors[0:1] + vectors[1:2]
    turned = jnp.transpose(n1).astype(BF16)
    for i in range(8):
        slot = lax.bitwise_xor(me, i)
        nt_ref[rows_of(slot * ROWS, ROWS, ROWS), rows] = turned[ROWS * i : ROWS * (i + 1)]
    nt_ref[D:, rows] = jnp.ones((TALL - D, x.shape[0]), BF16)
    return n1.astype(BF16)


def keep_keys(made, head_ref, k_ref, v_ref, kt_ref, rows, t, spare_k, spare_v):
    lanes = slice(t * COLS, (t + 1) * COLS)
    k = made[:, 0:COLS]
    keep_heads(k_ref, rows, t, k.astype(BF16), spare_k)
    kt_ref[lanes, rows] = jnp.transpose(k).astype(BF16)
    keep_heads(v_ref, rows, t, (made[:, COLS:] + head_ref[1:2, lanes]).astype(BF16), spare_v)


def project(x, id_col, pieces, tokens_all):
    own = x.shape[0]
    shapes = (
        jax.ShapeDtypeStruct((own, 2 * D), BF16),
        jax.ShapeDtypeStruct((own, 2 * D), BF16),
        jax.ShapeDtypeStruct((own, 2 * D), BF16),
        jax.ShapeDtypeStruct((D, own), BF16),
        jax.ShapeDtypeStruct((TALL, own), BF16),
        jax.ShapeDtypeStruct((D, 4 * WA), BF16),
        jax.ShapeDtypeStruct((EXTRA, D), F32),
        jax.ShapeDtypeStruct((8, 4 * FFC), F32),
        jax.ShapeDtypeStruct((8, 128), F32),
        jax.ShapeDtypeStruct((EXTRA, D), F32),
    )
    return pl.pallas_call(
        functools.partial(project_kernel, float(tokens_all)),
        out_shape=shapes,
        in_specs=[VMEM, VMEM] + [FAR] * 9,
        out_specs=[VMEM] * len(shapes),
        scratch_shapes=[pltpu.VMEM((32, EXTRA, WA), BF16), pltpu.SemaphoreType.DMA((2,))],
        compiler_params=params(6),
        cost_estimate=SMALL,
        name="project",
    )(x, id_col, *pieces)


def project_halo_kernel(x_ref, idc_ref, w_ref, vec_ref, head_ref, k_ref, v_ref, kt_ref, nt_ref):
    me = lax.axis_index("fsdp")

    def halo_rows(i, carry):
        rows = rows_of(i * 128, 128)
        n1 = first_norm(x_ref[rows, :], vec_ref[...], me, nt_ref, rows)
        _, spare_k, spare_v = spare_lanes(idc_ref[rows, :])
        for t in range(4):
            made = dot(n1, w_ref[:, t * WA + COLS : (t + 1) * WA])
            keep_keys(made, head_ref, k_ref, v_ref, kt_ref, rows, t, spare_k, spare_v)
        return carry

    lax.fori_loop(0, HALO // 128, halo_rows, 0)


def project_halo(x, id_col, w, vec, head):
    shape = jax.ShapeDtypeStruct((HALO, 2 * D), BF16)
    turned, tall = (jax.ShapeDtypeStruct((size, HALO), BF16) for size in (D, TALL))
    return pl.pallas_call(
        project_halo_kernel,
        out_shape=(shape, shape, turned, tall),
        compiler_params=params(6),
        cost_estimate=SMALL,
        name="project_halo",
    )(x, id_col, w, vec, head)


QB = 256


def causal(by_rows):
    key = lax.broadcasted_iota(jnp.int32, (QB, QB), 1 if by_rows else 0)
    query = lax.broadcasted_iota(jnp.int32, (QB, QB), 0 if by_rows else 1)
    return jnp.where(key <= query, 0.0, NEG)


def staged(units, stages, lag=1, beside=()):
    steps = len(units) + lag * (len(stages) - 1)
    for n in range(steps):
        for depth, stage in enumerate(stages):
            if 0 <= n - lag * depth < len(units):
                stage(units[n - lag * depth])
        if n < len(beside):
            beside[n]()
    for extra in beside[steps:]:
        extra()


def attend_heads(heads, bias_ref):
    lane = lane_of((QB, PAIR))
    at = lax.bitwise_and(lane, HD - 1)

    def score(one):
        q = one["q"][one["rows"], one["lanes"]]
        one["s"] = []
        for keys, _, where, last in one["parts"]:
            s = dot_t(q, keys[where, one["lanes"]])
            one["s"].append(s + bias_ref[...] if last else s)

    def soften(one):
        one["top"] = functools.reduce(jnp.maximum, [jnp.max(s, axis=-1, keepdims=True) for s in one["s"]])
        one["p"] = [jnp.exp(s - one["top"]).astype(BF16) for s in one.pop("s")]

    def attend(one):
        total = None
        for p, (_, values, where, _) in zip(one.pop("p"), one["parts"]):
            part = dot(p, values[where, one["lanes"]])
            total = part if total is None else total + part
        first = (HD if one["h"] == 0 else 0) + DOCS
        weight = total[:, first : first + 1]
        mine = (lane < HD) if one["h"] == 0 else (lane >= HD)
        q = one["q"][one["rows"], one["lanes"]]
        for i, term in enumerate(three_terms(-(one["top"] + jnp.log(weight)))):
            q = jnp.where((at == DOCS + i) & ~mine, jnp.broadcast_to(term, q.shape), q)
        one["take"](one["h"], (total / weight).astype(BF16), q)

    staged(heads, (score, soften, attend), 2)


def keep_attended(o_ref, qa_ref, rows, pair):
    lane = lane_of((QB, PAIR))

    def take(h, o, q):
        lanes = rows_of(pair * PAIR, PAIR)
        qa_ref[rows, head_lanes(pair, h)] = q
        o_ref[rows, lanes] = o if h == 0 else jnp.where(lane < HD, o_ref[rows, lanes], o)

    return take


def head_lanes(pair, h):
    return rows_of((2 * pair + h) * PAIR, PAIR)


def each_two(count, act):
    def step(i, carry):
        act((2 * i, 2 * i + 1))
        return carry

    lax.fori_loop(0, count, step, 0)


def attend_far_kernel(q_ref, k_ref, v_ref, o_ref, qa_ref, bias_ref):
    bias_ref[...] = causal(True)
    parts = ((k_ref, v_ref, slice(0, HALO), False), (k_ref, v_ref, slice(HALO, HALO + QB), True))

    def two(pairs):
        heads = []
        for pair in pairs:
            take = keep_attended(o_ref, qa_ref, slice(0, QB), pair)
            for h in range(2):
                heads.append(
                    dict(q=q_ref, rows=slice(HALO, HALO + QB), lanes=head_lanes(pair, h), h=h, parts=parts, take=take)
                )
        attend_heads(heads, bias_ref)

    each_two(2, two)


def attend_far(q, k, v):
    return pl.pallas_call(
        attend_far_kernel,
        out_shape=(jax.ShapeDtypeStruct((QB, D), BF16), jax.ShapeDtypeStruct((QB, 2 * D), BF16)),
        in_specs=[VMEM] * 3,
        out_specs=[VMEM] * 2,
        scratch_shapes=[pltpu.VMEM((QB, QB), F32)],
        compiler_params=params(8),
        cost_estimate=SMALL,
        name="attend_far",
    )(q, k, v)


def near_parts(halo, own):
    return (
        ((*halo, slice(0, HALO), False), (*own, slice(0, QB), True)),
        ((*halo, slice(QB, HALO), False), (*own, slice(0, QB), False), (*own, slice(QB, HALO), True)),
    )


def attend_near_kernel(q_ref, kh_ref, ko_ref, vh_ref, vo_ref, o_ref, qa_ref, bias_ref):
    bias_ref[...] = causal(True)

    def two(pairs):
        heads = []
        for pair in pairs:
            for i, parts in enumerate(near_parts((kh_ref, vh_ref), (ko_ref, vo_ref))):
                rows = slice(i * QB, (i + 1) * QB)
                take = keep_attended(o_ref, qa_ref, rows, pair)
                for h in range(2):
                    heads.append(dict(q=q_ref, rows=rows, lanes=head_lanes(pair, h), h=h, parts=parts, take=take))
        attend_heads(heads, bias_ref)

    each_two(2, two)


def attend_near(q, k_halo, k, v_halo, v):
    return pl.pallas_call(
        attend_near_kernel,
        out_shape=(jax.ShapeDtypeStruct((HALO, D), BF16), jax.ShapeDtypeStruct((HALO, 2 * D), BF16)),
        in_specs=[VMEM] * 5,
        out_specs=[VMEM] * 2,
        scratch_shapes=[pltpu.VMEM((QB, QB), F32)],
        compiler_params=params(8),
        cost_estimate=SMALL,
        name="attend_near",
    )(q, k_halo, k, v_halo, v)


PIECES_F = ((0, (0,)), (0, (1,)), (0, (2,)), (0, (3,)), (2, (0, 1, 2, 3)), (4, (0, 1, 2, 3)), (6, (0, 1)), (6, (2, 3)))


def central_kernel(
    rb, x_ref, oa_ref, oc_ref, teacher_ref, cot_ref, mask_ref, vec_ref, bup_ref, scale_ref,
    *rest
):
    pieces = rest[:16]
    (
    out_ref, gh_ref, ga_ref, theirs_ref, mine_ref, small_ref, gbup_ref,
    wo_ref, wup_ref, wdn_ref, slope_ref, hid_ref, gpre_ref, n2t_ref, gmlpt_ref, gattnt_ref, place_ref, o_ref,
    h1_ref, xhat_ref, n2_ref, gmlp_ref, sem
    ) = rest[16:]
    me, place = lax.axis_index("fsdp"), lax.axis_index("tp")
    own, ff = x_ref.shape[0], 4 * FFC
    parts = ((wo_ref, 0, COLS), (wup_ref, COLS, FFC), (wdn_ref, COLS + FFC, FFC))
    for n, (dst, start, size) in enumerate(parts):
        for j, ref in enumerate(pieces):
            mask, steps = PIECES_F[j % 8]
            owner = lax.bitwise_xor(me, mask + j // 8)
            for i, s in enumerate(steps):
                tp = lax.bitwise_and(place - s + 4, 3)
                pltpu.make_async_copy(
                    ref.at[i, :, pl.ds(start, size)],
                    dst.at[rows_of(owner * ROWS, ROWS, ROWS), rows_of(tp * size, size)],
                    sem.at[n],
                ).start()
    small_ref[...] = jnp.zeros_like(small_ref)
    head_of = lax.broadcasted_iota(jnp.int32, (D, 128), 0) // HD
    pick = (head_of == lax.broadcasted_iota(jnp.int32, (D, 128), 1)).astype(BF16)
    out_bias, gain, offset, down_bias = (vec_ref[j : j + 1, :] for j in range(2, 6))
    n2t_ref[D:, :] = jnp.ones((TALL - D, own), BF16)
    source = lax.broadcasted_iota(jnp.int32, (TERMS * 128, H * PAIR), 0)
    target = lax.broadcasted_iota(jnp.int32, (TERMS * 128, H * PAIR), 1)
    head, term = target // PAIR, lax.bitwise_and(target, HD - 1) - DOCS
    outside = (lax.bitwise_and(target, PAIR - 1) >= HD) == (lax.bitwise_and(head, 1) == 0)
    placed = outside & (lax.bitwise_and(source, 127) == head) & (source // 128 == term)
    place_ref[...] = jnp.where(placed, 1.0, 0.0).astype(BF16)
    o_ref[0:HALO, :] = oa_ref[...]
    o_ref[HALO:, :] = oc_ref[...]

    def turn(dst, rows, value):
        turned = jnp.transpose(value).astype(BF16)
        for i in range(8):
            slot = lax.bitwise_xor(me, i)
            dst[rows_of(slot * ROWS, ROWS, ROWS), rows] = turned[ROWS * i : ROWS * (i + 1)]

    def arrived(n):
        pltpu.make_async_copy(parts[n][0], parts[n][0], sem.at[n]).wait()

    blocks = [dict(rows=slice(i * rb, (i + 1) * rb)) for i in range(own // rb)]

    def attention_out(one):
        one["attn"] = dot_t(o_ref[one["rows"], :], wo_ref[...])

    def second_norm(one):
        rows = one["rows"]
        h1 = x_ref[rows, :].astype(F32) + one.pop("attn") + out_bias
        xhat, rstd = normalize(h1)
        n2 = xhat * gain + offset
        h1_ref[rows, :] = h1
        xhat_ref[rows, :] = xhat
        one["rstd"] = rstd
        n2_ref[rows, :] = n2.astype(BF16)
        turn(n2t_ref, rows, n2)

    arrived(0)
    staged(blocks, (attention_out, second_norm))
    arrived(1)

    def by_columns(stages):
        def step(c, carry):
            cols = rows_of(c * FFC, FFC)
            staged([dict(rows=one["rows"], cols=cols) for one in blocks], stages)
            return carry

        lax.fori_loop(0, 4, step, 0)

    def up(one):
        one["pre"] = dot(n2_ref[one["rows"], :], wup_ref[:, one["cols"]]) + bup_ref[0:1, one["cols"]]

    def gelu(one):
        pre = one.pop("pre")
        s = jax.nn.sigmoid(1.702 * pre)
        value = pre * s
        hid_ref[one["rows"], one["cols"]] = value.astype(BF16)
        slope_ref[one["rows"], one["cols"]] = s * (1.702 * (pre - value) + 1.0)

    by_columns((up, gelu))
    arrived(2)

    def down(one):
        one["mlp"] = dot_t(hid_ref[one["rows"], :], wdn_ref[...])

    def output(one):
        rows = one["rows"]
        out = h1_ref[rows, :] + one.pop("mlp") + down_bias
        out_ref[rows, :] = out.astype(BF16)
        diff = (out - teacher_ref[rows, :].astype(F32)) * mask_ref[rows, :]
        g_out = cot_ref[rows, :].astype(F32) + scale_ref[0:1, 0:1] * diff
        gh_ref[rows, :] = g_out
        small_ref[0:8, :] += fold(g_out)
        small_ref[8:16, :] += fold(diff * diff)
        gmlp_ref[rows, :] = g_out.astype(BF16)
        turn(gmlpt_ref, rows, g_out)

    staged(blocks, (down, output))

    def hidden(one):
        one["g"] = dot(gmlp_ref[one["rows"], :], wdn_ref[:, one["cols"]])

    def slope(one):
        g_pre = one.pop("g") * slope_ref[one["rows"], one["cols"]]
        gpre_ref[one["rows"], one["cols"]] = g_pre.astype(BF16)

    by_columns((hidden, slope))

    def into_norm(one):
        one["g"] = dot_t(gpre_ref[one["rows"], :], wup_ref[...])

    def pull_norm(one):
        rows, g_n2, xhat = one["rows"], one.pop("g"), xhat_ref[one["rows"], :]
        small_ref[16:24, :] += fold(g_n2 * xhat)
        small_ref[24:32, :] += fold(g_n2)
        g_h1 = gh_ref[rows, :] + norm_pull(g_n2, gain, xhat, one.pop("rstd"))
        gh_ref[rows, :] = g_h1
        small_ref[32:40, :] += fold(g_h1)
        turn(gattnt_ref, rows, g_h1)
        one["go"] = dot(g_h1.astype(BF16), wo_ref[...]).astype(BF16)

    def pull_out(one):
        rows, g_o = one["rows"], one.pop("go")
        product = g_o.astype(F32) * o_ref[rows, :].astype(F32)
        high = product.astype(BF16)
        low = (product - high.astype(F32)).astype(BF16)
        terms = jnp.concatenate(three_terms(-(dot(high, pick) + dot(low, pick))), axis=1)
        spare = dot(terms, place_ref[...]).astype(BF16)
        lane = lane_of((rb, PAIR))
        for n in range(H):
            mine = (lane < HD) if n % 2 == 0 else (lane >= HD)
            pair = g_o[:, (n // 2) * PAIR : (n // 2 + 1) * PAIR]
            ga_ref[rows, n * PAIR : (n + 1) * PAIR] = jnp.where(mine, pair, spare[:, n * PAIR : (n + 1) * PAIR])

    def keep(grad, s, start, size):
        low = grad.astype(BF16)
        for r in range(8):
            dst = theirs_ref if r % 2 else mine_ref
            dst[r // 2, s, :, start : start + size] = low[ROWS * r : ROWS * (r + 1)]

    def their(s, size):
        return rows_of(lax.bitwise_and(place + s, 3) * size, size)

    def by_down(s):
        keep(dot(gmlpt_ref[...], hid_ref[:, their(s, FFC)]), s, COLS + FFC, FFC)

    staged(
        blocks, (into_norm, pull_norm, pull_out), beside=[functools.partial(by_down, s) for s in range(4)]
    )
    for s in range(4):
        total = dot(n2t_ref[...], gpre_ref[:, their(s, FFC)])
        gbup_ref[:, their(s, FFC)] = total[D : D + 8]
        keep(total, s, COLS, FFC)
        keep(dot(gattnt_ref[...], o_ref[:, their(s, COLS)]), s, 0, COLS)


def central(x, o_near, o_far, teacher, cot, mask, vec, bup, scale, pieces):
    own = x.shape[0]
    rb = 256
    shapes = (
        jax.ShapeDtypeStruct((own, D), BF16),
        jax.ShapeDtypeStruct((own, D), F32),
        jax.ShapeDtypeStruct((own, 2 * D), BF16),
        jax.ShapeDtypeStruct((4, 4, ROWS, WF), BF16),
        jax.ShapeDtypeStruct((4, 4, ROWS, WF), BF16),
        jax.ShapeDtypeStruct((40, D), F32),
        jax.ShapeDtypeStruct((8, 4 * FFC), F32),
    )
    return pl.pallas_call(
        functools.partial(central_kernel, rb),
        out_shape=shapes,
        in_specs=[VMEM] * 9 + [FAR] * 16,
        out_specs=[VMEM] * len(shapes),
        scratch_shapes=[
            pltpu.VMEM((D, D), BF16),
            pltpu.VMEM((D, 4 * FFC), BF16),
            pltpu.VMEM((D, 4 * FFC), BF16),
            pltpu.VMEM((own, 4 * FFC), F32),
            pltpu.VMEM((own, 4 * FFC), BF16),
            pltpu.VMEM((own, 4 * FFC), BF16),
            pltpu.VMEM((TALL, own), BF16),
            pltpu.VMEM((D, own), BF16),
            pltpu.VMEM((D, own), BF16),
            pltpu.VMEM((TERMS * 128, H * PAIR), BF16),
            pltpu.VMEM((own, D), BF16),
            pltpu.VMEM((own, D), F32),
            pltpu.VMEM((own, D), F32),
            pltpu.VMEM((own, D), BF16),
            pltpu.VMEM((own, D), BF16),
            pltpu.SemaphoreType.DMA((3,)),
        ],
        compiler_params=params(30),
        cost_estimate=SMALL,
        name="central",
    )(x, o_near, o_far, teacher, cot, mask, vec, bup, scale, *pieces)


def pull_units(units, bias_ref):
    lane = lane_of((QB, PAIR))

    def mask(x, h):
        return jnp.where((lane < HD) if h == 0 else (lane >= HD), x, jnp.zeros_like(x))

    def score(one):
        keys, values, _, where, _ = one["part"]
        one["s"] = dot_t(keys[where, one["lanes"]], one["q"][one["rows"], one["qlanes"]])
        one["d"] = dot_t(values[where, one["lanes"]], one["g"][one["grows"], one["lanes"]])

    def soften(one):
        s = one.pop("s")
        p = jnp.exp(s + bias_ref[...] if one["part"][4] else s)
        one["p"], one["ds"] = p.astype(BF16), (p * one.pop("d")).astype(BF16)

    def finish(one):
        _, _, keys_t, where, last = one["part"]
        h, sums = one["h"], one["sums"]
        part = dot(keys_t[one["tlanes"], where], one["ds"])
        sums[h] = part if h not in sums else sums[h] + part
        if h == 0:
            sums["before"] = one
            return
        two = (sums.pop("before"), one)
        q = jnp.concatenate([mask(u["q"][u["rows"], u["qlanes"]], u["h"]) for u in two], axis=0)
        g = jnp.concatenate([mask(u["g"][u["grows"], u["lanes"]], u["h"]) for u in two], axis=0)
        dk = dot(jnp.concatenate([u.pop("ds") for u in two], axis=1), q)
        dv = dot(jnp.concatenate([u.pop("p") for u in two], axis=1), g)
        one["take"](dk, dv)
        if last:
            both = jnp.concatenate([sums[0], sums[1]], axis=0)
            one["take_q"]((jnp.transpose(both) * SCALE).astype(BF16))

    staged(units, (score, soften, finish), 2)


def block_units(q_ref, rows, q_pair, g_ref, grows, pair, parts, takes, take_q):
    sums, units = {}, []
    for part, take in zip(parts, takes):
        for h in range(2):
            units.append(
                dict(
                    q=q_ref, rows=rows, qlanes=head_lanes(q_pair, h), g=g_ref, grows=grows, lanes=head_lanes(pair, h), h=h,
                    part=part, tlanes=rows_of((2 * pair + h) * HD, HD, HD), take=take, take_q=take_q, sums=sums,
                )
            )
    return units


def pull_near_kernel(base, q_ref, g_ref, kh_ref, ko_ref, vh_ref, vo_ref, kth_ref, kto_ref, gh_ref, gq_ref, part_ref, bias_ref, late_ref):
    bias_ref[...] = causal(False)
    halo, own = (kh_ref, vh_ref, kth_ref), (ko_ref, vo_ref, kto_ref)

    def one(pair, carry):
        lanes = (rows_of(2 * pair * PAIR, PAIR), rows_of((2 * pair + 1) * PAIR, PAIR))

        def halo_first(*grads):
            for at, d in zip(lanes, grads):
                gh_ref[0:QB, at] = d[0:QB].astype(BF16)
                late_ref[:, at] = d[QB:]

        def halo_second(*grads):
            for at, d in zip(lanes, grads):
                gh_ref[QB:, at] = (late_ref[:, at] + d).astype(BF16)

        def own_first(*grads):
            for at, d in zip(lanes, grads):
                part_ref[0:QB, at] = d

        def own_more(*grads):
            for at, d in zip(lanes, grads):
                part_ref[0:QB, at] += d

        def own_last(*grads):
            for at, d in zip(lanes, grads):
                part_ref[QB:, at] = d

        units, takes = [], ((halo_first, own_first), (halo_second, own_more, own_last))
        for i, parts in enumerate(near_parts(halo, own)):
            rows = slice(i * QB, (i + 1) * QB)

            def take_q(dq, rows=rows):
                gq_ref[rows, rows_of(pair * PAIR, PAIR)] = dq

            units += block_units(q_ref, rows, base + pair, g_ref, rows, base + pair, parts, takes[i], take_q)
        pull_units(units, bias_ref)
        return carry

    lax.fori_loop(0, 2, one, 0)


def pull_near(base, qa, ga, k_halo, k, v_halo, v, kt_halo, kt):
    return pl.pallas_call(
        functools.partial(pull_near_kernel, base),
        out_shape=(
            jax.ShapeDtypeStruct((HALO, D), BF16),
            jax.ShapeDtypeStruct((HALO, D // 2), BF16),
            jax.ShapeDtypeStruct((HALO, D), F32),
        ),
        in_specs=[VMEM] * 8,
        out_specs=[VMEM] * 3,
        scratch_shapes=[pltpu.VMEM((QB, QB), F32), pltpu.VMEM((QB, D), F32)],
        compiler_params=params(10),
        cost_estimate=SMALL,
        name="pull_near",
    )(qa, ga, k_halo, k, v_halo, v, kt_halo, kt)


def pull_far_kernel(q_ref, go_ref, k_ref, v_ref, kt_ref, qa_ref, qb_ref, pa_ref, pb_ref, g_ref, bias_ref):
    bias_ref[...] = causal(False)
    refs = (k_ref, v_ref, kt_ref)
    parts = ((*refs, slice(0, HALO), False), (*refs, slice(HALO, HALO + QB), True))

    def two(inside, carry):
        units = []
        for half, near_q, near_part in ((0, qa_ref, pa_ref), (1, qb_ref, pb_ref)):
            pair = 2 * half + inside
            lanes = tuple(rows_of(pair * WA + n * COLS, COLS) for n in range(3))
            within = tuple(rows_of((2 * inside + n) * PAIR, PAIR) for n in range(2))
            g_ref[0:HALO, lanes[0]] = near_q[:, rows_of(inside * PAIR, PAIR)]

            def older(*grads, lanes=lanes, within=within, near_part=near_part):
                for n, d in enumerate(grads):
                    g_ref[0:HALO, lanes[n + 1]] = (near_part[:, within[n]] + d).astype(BF16)

            def newest(*grads, lanes=lanes):
                for n, d in enumerate(grads):
                    g_ref[HALO:, lanes[n + 1]] = d.astype(BF16)

            def take_q(dq, lanes=lanes):
                g_ref[HALO:, lanes[0]] = dq

            own = slice(HALO, HALO + QB)
            units += block_units(q_ref, slice(0, QB), pair, go_ref, own, pair, parts, (older, newest), take_q)
        pull_units(units, bias_ref)
        return carry

    lax.fori_loop(0, 2, two, 0)


def pull_far(qa, ga, k, v, kt, gq_near, gq_more, part_near, part_more):
    own = k.shape[0]
    return pl.pallas_call(
        pull_far_kernel,
        out_shape=jax.ShapeDtypeStruct((own, 4 * WA), BF16),
        in_specs=[VMEM] * 9,
        out_specs=VMEM,
        scratch_shapes=[pltpu.VMEM((QB, QB), F32)],
        compiler_params=params(10),
        cost_estimate=SMALL,
        name="pull_far",
    )(qa, ga, k, v, kt, gq_near, gq_more, part_near, part_more)


def norm_sums(small_ref, x, g_n1):
    xhat, _ = normalize(x.astype(F32))
    small_ref[0:8, :] += fold(g_n1 * xhat)
    small_ref[8:16, :] += fold(g_n1)


def halo_back_kernel(ga_ref, gb_ref, w_ref, x_ref, out_ref, small_ref):
    small_ref[...] = jnp.zeros_like(small_ref)

    def pull(one):
        total = None
        for t in range(4):
            g = (ga_ref, gb_ref)[t // 2][one["rows"], (t % 2) * 2 * COLS : (t % 2 + 1) * 2 * COLS]
            part = dot_t(g, w_ref[:, t * WA + COLS : (t + 1) * WA])
            total = part if total is None else total + part
        one["g"] = total

    def norms(one):
        g_n1 = one.pop("g")
        out_ref[one["rows"], :] = g_n1.astype(BF16)
        norm_sums(small_ref, x_ref[one["rows"], :], g_n1)

    staged([dict(rows=slice(i * QB, (i + 1) * QB)) for i in range(HALO // QB)], (pull, norms))


def halo_back(g_near, g_more, w, halo):
    return pl.pallas_call(
        halo_back_kernel,
        out_shape=(jax.ShapeDtypeStruct((HALO, D), BF16), jax.ShapeDtypeStruct((16, D), F32)),
        compiler_params=params(6),
        cost_estimate=SMALL,
        name="halo_back",
    )(g_near, g_more, w, halo)


def own_back_kernel(
    x_ref, ga_ref, gb_ref, g_ref, nth_ref, nto_ref, w_ref, small_halo, small_two, gbup_ref, scale_ref,
    gn_ref, theirs_ref, mine_ref, small_ref, gh_ref
):
    me, place = lax.axis_index("fsdp"), lax.axis_index("tp")
    own = x_ref.shape[0]
    small_ref[...] = small_halo[...]
    gh_ref[:, 0:D] = ga_ref[...]
    gh_ref[:, D:] = gb_ref[...]

    def pull(one):
        one["g"] = dot_t(g_ref[one["rows"], :], w_ref[...])

    def norms(one):
        g_n1 = one.pop("g")
        gn_ref[one["rows"], :] = g_n1
        norm_sums(small_ref, x_ref[one["rows"], :], g_n1)

    staged([dict(rows=slice(i * QB, (i + 1) * QB)) for i in range(own // QB)], (pull, norms))
    sums = lambda ref, j: jnp.sum(ref[8 * j : 8 * j + 8, :], axis=0, keepdims=True)
    loss = jnp.sum(sums(small_two, 1), axis=1, keepdims=True) * scale_ref[4:5, 0:1]
    vectors = jnp.concatenate(
        [sums(small_ref, 0), sums(small_ref, 1), sums(small_two, 4), sums(small_two, 2), sums(small_two, 3),
         sums(small_two, 0), jnp.zeros((2, D), F32)],
        axis=0,
    )
    high = loss.astype(BF16).astype(F32)
    row, lane = lax.broadcasted_iota(jnp.int32, (EXTRA, 128), 0), lane_of((EXTRA, 128))

    def grads(s, carry):
        tp = lax.bitwise_and(place + s, 3)
        g_own = g_ref[:, rows_of(tp * WA, WA)]
        g_halo = gh_ref[:, rows_of(tp * 2 * COLS, 2 * COLS)]
        total = dot(nto_ref[...], g_own)
        more = dot(nth_ref[...], g_halo)
        total = jnp.concatenate([total[:, 0:COLS], total[:, COLS:] + more], axis=1)
        low, sums = total[0:D].astype(BF16), total[D : D + 1]
        ups = gbup_ref[0:1, rows_of(tp * FFC, FFC)]
        mids = jnp.concatenate(
            [sums[:, 0:COLS], sums[:, 2 * COLS :]]
            + [ups[:, 128 * j : 128 * j + 128] for j in range(4)]
            + [jnp.zeros((2, 128), F32)],
            axis=0,
        ).astype(BF16)
        for r in range(8):
            dst = theirs_ref if r % 2 else mine_ref
            dst[r // 2, s, 0:ROWS, :] = low[ROWS * r : ROWS * (r + 1)]
            dst[r // 2, s, ROWS:, 128:256] = mids
        return carry

    lax.fori_loop(0, 4, grads, 0)
    for r in range(8):
        owner = lax.bitwise_xor(me, r)
        block = pltpu.roll(vectors, lax.rem(D - owner * ROWS, D), 1)[:, 0:128]
        block = jnp.where((row == 6) & (lane == 0), high, block)
        block = jnp.where((row == 6) & (lane == 1), loss - high, block).astype(BF16)
        dst = theirs_ref if r % 2 else mine_ref
        for s in range(4):
            dst[r // 2, s, ROWS:, 0:128] = block
            dst[r // 2, s, ROWS:, 256:384] = jnp.zeros((EXTRA, 128), BF16)


def own_back(x, g_near, g_more, g_own, nt_halo, nt, w, small_halo, small_two, gbup, scale):
    own = x.shape[0]
    send = jax.ShapeDtypeStruct((4, 4, ROWS + EXTRA, WA), BF16)
    return pl.pallas_call(
        own_back_kernel,
        out_shape=(jax.ShapeDtypeStruct((own, D), F32), send, send),
        scratch_shapes=[pltpu.VMEM((16, D), F32), pltpu.VMEM((HALO, 2 * D), BF16)],
        compiler_params=params(10),
        cost_estimate=SMALL,
        name="own_back",
    )(x, g_near, g_more, g_own, nt_halo, nt, w, small_halo, small_two, gbup, scale)


def close_kernel(x_ref, gn_ref, back_ref, gh_ref, vec_ref, out_ref):
    own = x_ref.shape[0]

    def block(at, extra):
        rows = rows_of(at, 128)
        xhat, rstd = normalize(x_ref[rows, :].astype(F32))
        g_n1 = gn_ref[rows, :] + extra
        out_ref[rows, :] = gh_ref[rows, :] + norm_pull(g_n1, vec_ref[0:1, :], xhat, rstd)

    def first(i, carry):
        block(i * 128, 0.0)
        return carry

    def second(i, carry):
        block(own - HALO + i * 128, back_ref[rows_of(i * 128, 128), :].astype(F32))
        return carry

    lax.fori_loop(0, (own - HALO) // 128, first, 0)
    lax.fori_loop(0, HALO // 128, second, 0)


def close(x, g_n1, back, g_h1, vec):
    return pl.pallas_call(
        close_kernel,
        out_shape=jax.ShapeDtypeStruct(x.shape, F32),
        compiler_params=params(8),
        cost_estimate=SMALL,
        name="close",
    )(x, g_n1, back, g_h1, vec)


def unpack_f_kernel(k_ref, r1, r2, r3, wo_ref, wup_ref, wdn_ref):
    total = (k_ref[0].astype(F32) + r1[...].astype(F32)) + (r2[...].astype(F32) + r3[...].astype(F32))
    wo_ref[...] = total[:, 0:COLS]
    wup_ref[...] = total[:, COLS : COLS + FFC]
    wdn_ref[...] = total[:, COLS + FFC :]


def unpack_f(k, r1, r2, r3):
    return pl.pallas_call(
        unpack_f_kernel,
        out_shape=(
            jax.ShapeDtypeStruct((ROWS, COLS), F32),
            jax.ShapeDtypeStruct((ROWS, FFC), F32),
            jax.ShapeDtypeStruct((ROWS, FFC), F32),
        ),
        compiler_params=params(6),
        name="unpack_f",
    )(k, r1, r2, r3)


def unpack_a_kernel(k_ref, r1, r2, r3, wq_ref, wk_ref, wv_ref, bq_ref, bv_ref, bup_ref, loss_ref, *vec_refs):
    me = lax.axis_index("fsdp")
    total = (k_ref[0].astype(F32) + r1[...].astype(F32)) + (r2[...].astype(F32) + r3[...].astype(F32))
    wq_ref[...] = total[0:ROWS, 0:COLS]
    wk_ref[...] = total[0:ROWS, COLS : 2 * COLS]
    wv_ref[...] = total[0:ROWS, 2 * COLS :]
    for j, ref in enumerate(vec_refs):
        ref[...] = total[ROWS + j, 0:ROWS]
    loss_ref[...] = total[ROWS + 6 : ROWS + 7, 0:1] + total[ROWS + 6 : ROWS + 7, 1:2]
    mids = pltpu.roll(total[ROWS:, 128:256], lax.rem(128 - me * 8, 128), 1)
    for i in range(2):
        bq_ref[i : i + 1, :] = mids[0:1, i * HD : i * HD + 8]
        bv_ref[i : i + 1, :] = mids[1:2, i * HD : i * HD + 8]
    for i in range(8):
        at = (i % 2) * HD
        bup_ref[i : i + 1, :] = mids[2 + i // 2 : 3 + i // 2, at : at + 8]


def unpack_a(k, r1, r2, r3):
    small = jax.ShapeDtypeStruct((ROWS, COLS), F32)
    return pl.pallas_call(
        unpack_a_kernel,
        out_shape=(
            small,
            small,
            small,
            jax.ShapeDtypeStruct((2, 8), F32),
            jax.ShapeDtypeStruct((2, 8), F32),
            jax.ShapeDtypeStruct((8, 8), F32),
            jax.ShapeDtypeStruct((1, 1), F32),
            *[jax.ShapeDtypeStruct((ROWS,), F32)] * 6,
        ),
        compiler_params=params(6),
        name="unpack_a",
    )(k, r1, r2, r3)


def to_mask(x, mask):
    return lax.ppermute(x, "fsdp", [(i, i ^ mask) for i in range(8)])


def to_step(x, step):
    return lax.ppermute(x, "tp", [(i, (i + step) % 4) for i in range(4)])


def add(a, b):
    return (a.astype(F32) + b.astype(F32)).astype(BF16)


def after(values, others):
    return lax.optimization_barrier((values, others))[0]


def local_fast(
    layer_input, segment_ids, valid_mask, teacher, cotangent, ln1_gain, ln1_bias, w_q, w_k, w_v, b_q, b_v,
    w_o, b_o, ln2_gain, ln2_bias, w_up, b_up, w_down, b_down
):
    place = lax.axis_index("tp")
    own = layer_input.shape[0]
    tokens_all = own * lax.axis_size("fsdp") * lax.axis_size("tp")

    shard_a, shard_f = pack_weights(
        (w_q, w_k, w_v, w_o.T, w_up, w_down.T, ln1_gain, ln1_bias, b_o, ln2_gain, ln2_bias, b_down, b_q, b_v, b_up,
         valid_mask)
    )
    steps_a = [shard_a] + [to_step(shard_a, s) for s in (1, 2, 3)]
    line_a = jnp.stack(steps_a)
    steps_f = [shard_f] + [to_step(shard_f, s) for s in (1, 2, 3)]
    over_f = [to_mask(x, 1) for x in steps_f]
    near_a = [to_mask(line_a, m) for m in (2, 4, 6)]
    halves_a = after([jnp.stack(steps_a[0:2]), jnp.stack(steps_a[2:4])], steps_f)
    over_a = [to_mask(a, 1) for a in halves_a]
    line_f = jnp.stack(after(steps_f, (over_a, near_a)))
    pieces_a = [line_a] + near_a + over_a + [to_mask(a, 1) for a in near_a]
    halo = lax.ppermute(layer_input[own - HALO :], "tp", [(i, i + 1) for i in range(3)])
    f_x, f_y = to_mask(line_f, 2), to_mask(line_f, 4)

    ids = segment_ids + 16 * jnp.arange(segment_ids.shape[0], dtype=jnp.int32)[:, None]
    ids = jnp.concatenate([jnp.full((HALO,), -1, jnp.int32), ids.reshape(-1)])
    id_col = lax.dynamic_slice_in_dim(ids, place * own, HALO + own)[:, None]
    mask = valid_mask.astype(F32)[:, None]

    q, k, v, kt, nt, w_all, vec, bup, scale, head = project(after(layer_input, over_f), id_col, pieces_a, tokens_all)
    o_far, qa_far = attend_far(q, k, v)
    f_x, f_y = after((f_x, f_y), o_far)
    halo = after(halo, o_far)
    f_xy = [to_mask(f_y[0:2], 2), to_mask(f_x[2:4], 4)]
    k_halo, v_halo, kt_halo, nt_halo = project_halo(halo, id_col, w_all, vec, head)
    o_near, qa_near = attend_near(q, k_halo, k, v_halo, v)
    near_f = [f_x, f_y] + after(f_xy, o_near)
    pieces_f = [x[None] for x in steps_f] + near_f + [x[None] for x in over_f] + [to_mask(a, 1) for a in near_f]
    layer_out, g_h1, ga, theirs_f, mine_f, small_two, gbup = central(
        layer_input, o_near, o_far, teacher, cotangent, mask, vec, bup, scale, pieces_f
    )

    def near(base, qa, ga):
        return pull_near(base, qa, ga, k_halo, k, v_halo, v, kt_halo, kt)

    g_near, gq_near, part_near = near(0, qa_near, ga)
    half = add(after(mine_f, g_near), to_mask(theirs_f, 1))
    from_x, from_y = to_mask(half[3, 0:2], 2), to_mask(half[3, 2:4], 4)
    g_more, gq_more, part_more = near(2, after(qa_near, half), ga)
    gn_halo, small_halo = halo_back(g_near, g_more, w_all, halo)
    back = lax.ppermute(gn_halo, "tp", [(i + 1, i) for i in range(3)])
    from_x, from_y = after((from_x, from_y), gn_halo)
    for_x = jnp.concatenate([half[1, 0:2], add(half[1, 2:4], from_y)])
    for_y = jnp.concatenate([add(half[2, 0:2], from_x), half[2, 2:4]])
    got_x, got_y = to_mask(for_x, 2), to_mask(for_y, 4)
    g_own = pull_far(after(qa_far, (for_x, for_y)), ga, k, v, kt, gq_near, gq_more, part_near, part_more)
    gn_own, theirs_a, mine_a = own_back(
        layer_input, g_near, g_more, g_own, nt_halo, nt, w_all, small_halo, small_two, gbup, scale
    )
    got_x, got_y = after((got_x, got_y), gn_own)
    line = (half[0].astype(F32) + got_x.astype(F32) + got_y.astype(F32)).astype(BF16)
    grad_wo, grad_wup, grad_wdn = unpack_f(line, *[to_step(line[s], s) for s in (1, 2, 3)])

    half = add(mine_a, to_mask(after(theirs_a, back), 1))
    from_x, from_y, from_xy = (to_mask(half[m], 2 * m) for m in (1, 2, 3))
    line = (half[0].astype(F32) + from_x.astype(F32) + from_y.astype(F32) + from_xy.astype(F32)).astype(BF16)
    grad_wq, grad_wk, grad_wv, grad_bq, grad_bv, grad_bup, loss, *six = unpack_a(
        line, *[to_step(line[s], s) for s in (1, 2, 3)]
    )
    grad_input = close(layer_input, gn_own, back, g_h1, vec)
    return (
        layer_out, loss.reshape(()), grad_input, six[0], six[1], grad_wq, grad_wk, grad_wv, grad_bq, grad_bv, grad_wo.T, six[2],
        six[3], six[4], grad_wup, grad_bup, grad_wdn.T, six[5]
    )


def solution(mesh):
    tokens = P(("fsdp", "tp"), None)
    rows, crossed, heads = P("fsdp"), P("fsdp", "tp"), P("tp", "fsdp")
    placed = (
        tokens,
        P("fsdp", None),
        P(("fsdp", "tp")),
        tokens,
        tokens,
        rows,
        rows,
        crossed,
        crossed,
        crossed,
        heads,
        heads,
        heads,
        rows,
        rows,
        rows,
        crossed,
        heads,
        heads,
        rows,
    )
    given = (
        tokens,
        P(),
        tokens,
        rows,
        rows,
        crossed,
        crossed,
        crossed,
        heads,
        heads,
        heads,
        rows,
        rows,
        rows,
        crossed,
        heads,
        heads,
        rows,
    )
    sizes = (mesh.shape["fsdp"], mesh.shape["tp"])
    body = local_fast if sizes == (8, 4) else local
    return jax.shard_map(body, mesh=mesh, in_specs=placed, out_specs=given, check_vma=False)
```

profile of v0, /device:TPU:0, one launch (start us, length us, event | category | flops | bytes accessed | tf_op | source)
XLA Modules:
  0.0 145.4 jit_solution(14928300327967910142)
XLA Ops:
  0.7 1.9 %pack_weights.1 = (bf16[72,384]{1,0:T(8,128)(2,1)}, bf16[64,1152]{1,0:T(8,128)(2,1)}) custom-call(bf16[64,128]{1,0:T(8,128)(2,1)} %wq_ref.1, bf16[64,128]{1,0:T(8,128)(2,1)} %wk_ref.1, bf16[64,128]{1,0:T(8,128)(2,1)} %wv_ref.1, bf16[64,128]{1,0:T(8,128)(2,1)} %bitcast.88, bf16[64,512]{1,0:T(8,128)(2,1)} %wup_ref.1, bf16[64,512]{1,0:T(8,128)(2,1)} %bitcast.87, ...), custom_call_target="tpu_custom_call" | custom-call | tf_op jit(solution)/shard_map/pack_weights/pallas_call | solution.py:677
  2.6 5.0 %collective-permute-start.9 = (bf16[72,384]{1,0:T(8,128)(2,1)}, bf16[72,384]{1,0:T(8,128)(2,1)S(1)}, u32[]{:S(2)}, u32[]{:S(2)}) collective-permute-start(bf16[72,384]{1,0:T(8,128)(2,1)} %get-tuple-element.94), channel_id=1, source_target_pairs={{0,3},{1,0},{2,1},{3,2},{4,7},{5,4},{6,5},{7,6},{8,11},{9,8},{10,9... | collective-permute-start | bytes 165896 | tf_op jit(solution)/shard_map/ppermute | solution.py:1560
  8.6 2.8 %collective-permute-start.5 = (bf16[64,1152]{1,0:T(8,128)(2,1)}, bf16[64,1152]{1,0:T(8,128)(2,1)S(1)}, u32[]{:S(2)}, u32[]{:S(2)}) collective-permute-start(bf16[64,1152]{1,0:T(8,128)(2,1)} %get-tuple-element.110), channel_id=1, source_target_pairs={{0,3},{1,0},{2,1},{3,2},{4,7},{5,4},{6,5},{7,6},{8,11},{9,8},{10,9... | collective-permute-start | bytes 442376 | tf_op jit(solution)/shard_map/ppermute | solution.py:1560
  16.1 2.5 %collective-permute-start.12 = (bf16[4,72,384]{2,1,0:T(8,128)(2,1)S(1)}, bf16[4,72,384]{2,1,0:T(8,128)(2,1)S(1)}, u32[]{:S(2)}, u32[]{:S(2)}) collective-permute-start(bf16[4,72,384]{2,1,0:T(8,128)(2,1)S(1)} %pad_maximum_fusion.3.p0), channel_id=1, source_target_pairs={{0,24},{4,28},{8,16},{12,20},{16,8},{20,12},{24,0},{28,4},{1,25},{... | collective-permute-start | bytes 663560 | tf_op jit(solution)/shard_map/ppermute | solution.py:1556
  19.7 6.5 %collective-permute-done.3 = bf16[64,1152]{1,0:T(8,128)(2,1)S(1)} collective-permute-done((bf16[64,1152]{1,0:T(8,128)(2,1)}, bf16[64,1152]{1,0:T(8,128)(2,1)S(1)}, u32[]{:S(2)}, u32[]{:S(2)}) %collective-permute-start.3) | collective-permute-done | bytes 147488 | tf_op jit(solution)/shard_map/ppermute | solution.py:1560
  29.3 1.8 %pad_maximum_fusion = bf16[4,64,1152]{2,1,0:T(8,128)(2,1)} fusion(bf16[1,64,1152]{2,1,0:T(8,128)(2,1)S(1)} %bitcast.69, bf16[1,64,1152]{2,1,0:T(8,128)(2,1)S(1)} %bitcast.71, bf16[1,64,1152]{2,1,0:T(8,128)(2,1)S(1)} %bitcast.73, bf16[1,64,1152]{2,1,0:T(8,128)(2,1)} %bitcast.67), kind=kLoop, calls=%fused_computation.6 | loop fusion | flops 884736 | bytes 1179648 | tf_op jit(solution)/shard_map/stack | solution.py:1590
  31.2 1.5 %collective-permute-start.20 = (bf16[4,64,1152]{2,1,0:T(8,128)(2,1)}, bf16[4,64,1152]{2,1,0:T(8,128)(2,1)S(1)}, u32[]{:S(2)}, u32[]{:S(2)}) collective-permute-start(bf16[4,64,1152]{2,1,0:T(8,128)(2,1)} %pad_maximum_fusion), channel_id=1, source_target_pairs={{0,16},{4,20},{8,24},{12,28},{16,0},{20,4},{24,8},{28,12},{1,17},{... | collective-permute-start | bytes 1769480 | tf_op jit(solution)/shard_map/ppermute | solution.py:1556
  32.7 1.5 %collective-permute-start.19 = (bf16[4,64,1152]{2,1,0:T(8,128)(2,1)}, bf16[4,64,1152]{2,1,0:T(8,128)(2,1)S(1)}, u32[]{:S(2)}, u32[]{:S(2)}) collective-permute-start(bf16[4,64,1152]{2,1,0:T(8,128)(2,1)} %pad_maximum_fusion), channel_id=1, source_target_pairs={{0,8},{4,12},{8,0},{12,4},{16,24},{20,28},{24,16},{28,20},{1,9},{5... | collective-permute-start | bytes 1769480 | tf_op jit(solution)/shard_map/ppermute | solution.py:1556
  36.5 3.1 %collective-permute-start.18 = (bf16[512,512]{1,0:T(8,128)(2,1)}, bf16[512,512]{1,0:T(8,128)(2,1)S(1)}, u32[]{:S(2)}, u32[]{:S(2)}) collective-permute-start(bf16[512,512]{1,0:T(8,128)(2,1)} %slice.60), channel_id=1, source_target_pairs={{0,1},{1,2},{2,3},{4,5},{5,6},{6,7},{8,9},{9,10},{10,11},{12,13},{... | collective-permute-start | bytes 1572872 | tf_op jit(solution)/shard_map/ppermute | solution.py:1592
  45.7 5.3 %project.1 = (bf16[768,1024]{1,0:T(8,128)(2,1)S(1)}, bf16[768,1024]{1,0:T(8,128)(2,1)S(1)}, bf16[768,1024]{1,0:T(8,128)(2,1)S(1)}, bf16[512,768]{1,0:T(8,128)(2,...) custom-call(bf16[768,512]{1,0:T(8,128)(2,1)S(1)} %copy-done, ...), custom_call_target="tpu_custom_call" | custom-call | flops 1 | bytes 1 | tf_op jit(solution)/shard_map/project/pallas_call | solution.py:816
  51.0 3.0 %attend_far.1 = (bf16[256,512]{1,0:T(8,128)(2,1)S(1)}, bf16[256,1024]{1,0:T(8,128)(2,1)S(1)}) custom-call(bf16[768,1024]{1,0:T(8,128)(2,1)S(1)} %get-tuple-element.97.q_ref, bf16[768,1024]{1,0:T(8,128)(2,1)S(1)} %get-tuple-element.98.k_ref.ko_ref, bf16[768,1024]{1,0:T(8,128)(2,1)S(1)} %get-tuple-element.99.v_ref.vo_ref), custom_call_target="tpu_custom_call" | custom-call | flops 1 | bytes 1 | tf_op jit(solution)/shard_map/attend_far/pallas_call | solution.py:948
  55.7 2.3 %project_halo.1 = (bf16[512,1024]{1,0:T(8,128)(2,1)S(1)}, bf16[512,1024]{1,0:T(8,128)(2,1)S(1)}, bf16[512,512]{1,0:T(8,128)(2,1)S(1)}, bf16[528,512]{1,0:T(8,128)(2,1)S(1)}) custom-call(bf16[512,512]{1,0:T(8,128)(2,1)S(1)} %collective-permute-done.18.x_ref, s32[1280,1]{1,0:T(8,128)S(1)} %broadcast_in_dim.42.idc_ref, ...), custom_call_target="tpu_custom_call" | custom-call | flops 1 | bytes 1 | tf_op jit(solution)/shard_map/project_halo/pallas_call | solution.py:846
  58.2 6.2 %attend_near.1 = (bf16[512,512]{1,0:T(8,128)(2,1)S(1)}, bf16[512,1024]{1,0:T(8,128)(2,1)S(1)}) custom-call(bf16[768,1024]{1,0:T(8,128)(2,1)S(1)} %get-tuple-element.97.q_ref, bf16[512,1024]{1,0:T(8,128)(2,1)S(1)} %get-tuple-element.105.kh_ref, bf16[768,1024]{1,0:T(8,128)(2,1)S(1)} %get-tuple-element.98.k_ref.ko_ref, ...), custom_call_target="tpu_custom_call" | custom-call | flops 1 | bytes 1 | tf_op jit(solution)/shard_map/attend_near/pallas_call | solution.py:984
  66.6 19.2 %central.1 = (bf16[768,512]{1,0:T(8,128)(2,1)}, f32[768,512]{1,0:T(8,128)S(1)}, bf16[768,1024]{1,0:T(8,128)(2,1)S(1)}, bf16[4,4,64,1152]{3,2,1,0:T(8,128)(2,1)S(...) custom-call(bf16[768,512]{1,0:T(8,128)(2,1)S(1)} %copy-done, ...), custom_call_target="tpu_custom_call" | custom-call | flops 1 | bytes 1 | tf_op jit(solution)/shard_map/central/pallas_call | solution.py:1173
  86.0 4.4 %pull_near.2 = (bf16[512,512]{1,0:T(8,128)(2,1)S(1)}, bf16[512,256]{1,0:T(8,128)(2,1)S(1)}, f32[512,512]{1,0:T(8,128)S(1)}) custom-call(bf16[512,1024]{1,0:T(8,128)(2,1)S(1)} %get-tuple-element.127.q_ref, bf16[768,1024]{1,0:T(8,128)(2,1)S(1)} %get-tuple-element.120.g_ref.go_ref, bf16[512,1024]{1,0:T(8,128)(2,1)S(1)} %get-tuple-element.105.kh_ref, ...), custom_call_target="tpu_custom_call" | custom-call | flops 1 | bytes 1 | tf_op jit(solution)/shard_map/pull_near/pallas_call | solution.py:1295
  91.2 1.6 %collective-permute-start.29 = (bf16[2,64,1152]{2,1,0:T(8,128)(2,1)S(1)}, bf16[2,64,1152]{2,1,0:T(8,128)(2,1)S(1)}, u32[]{:S(2)}, u32[]{:S(2)}) collective-permute-start(bf16[2,64,1152]{2,1,0:T(8,128)(2,1)S(1)} %get-tuple-element.169), channel_id=1, source_target_pairs={{0,16},{4,20},{8,24},{12,28},{16,0},{20,4},{24,8},{28,12},{1,17},{... | collective-permute-start | bytes 884744 | tf_op jit(solution)/shard_map/ppermute | solution.py:1556
  92.9 1.4 collective-permute-start.28
  94.3 4.6 %pull_near.3 = (bf16[512,512]{1,0:T(8,128)(2,1)S(1)}, bf16[512,256]{1,0:T(8,128)(2,1)S(1)}, f32[512,512]{1,0:T(8,128)S(1)}) custom-call(bf16[512,1024]{1,0:T(8,128)(2,1)S(1)} %get-tuple-element.127.q_ref, bf16[768,1024]{1,0:T(8,128)(2,1)S(1)} %get-tuple-element.120.g_ref.go_ref, bf16[512,1024]{1,0:T(8,128)(2,1)S(1)} %get-tuple-element.105.kh_ref, ...), custom_call_target="tpu_custom_call" | custom-call | flops 1 | bytes 1 | tf_op jit(solution)/shard_map/pull_near/pallas_call | solution.py:1295
  99.7 1.3 collective-permute-start.30
  102.1 1.5 %collective-permute-start.38 = (bf16[4,64,1152]{2,1,0:T(8,128)(2,1)S(1)}, bf16[4,64,1152]{2,1,0:T(8,128)(2,1)S(1)}, u32[]{:S(2)}, u32[]{:S(2)}) collective-permute-start(bf16[4,64,1152]{2,1,0:T(8,128)(2,1)S(1)} %pad_maximum_fusion.1), channel_id=1, source_target_pairs={{0,8},{4,12},{8,0},{12,4},{16,24},{20,28},{24,16},{28,20},{1,9},{5... | collective-permute-start | bytes 1769480 | tf_op jit(solution)/shard_map/ppermute | solution.py:1556
  104.3 4.4 %pull_far.1.g_ref = bf16[768,1536]{1,0:T(8,128)(2,1)S(1)} custom-call(bf16[256,1024]{1,0:T(8,128)(2,1)S(1)} %get-tuple-element.133.q_ref, bf16[768,1024]{1,0:T(8,128)(2,1)S(1)} %get-tuple-element.120.g_ref.go_ref, bf16[768,1024]{1,0:T(8,128)(2,1)S(1)} %get-tuple-element.98.k_ref.ko_ref, bf16[768,1024]{1,0:T(8,128)(2,1)S(1)} %get-tuple-element.99.v_ref.vo_ref, ...), custom_call_target="tpu_custom_call" | custom-call | flops 1 | bytes 1 | tf_op jit(solution)/shard_map/pull_far/pallas_call | solution.py:1345
  108.7 4.7 %own_back.1 = (f32[768,512]{1,0:T(8,128)S(1)}, bf16[4,4,72,384]{3,2,1,0:T(8,128)(2,1)S(1)}, bf16[4,4,72,384]{3,2,1,0:T(8,128)(2,1)S(1)}) custom-call(bf16[768,512]{1,0:T(8,128)(2,1)S(1)} %copy-done, bf16[512,512]{1,0:T(8,128)(2,1)S(1)} %get-tuple-element.123.ga_ref, bf16[512,512]{1,0:T(8,128)(2,1)S(1)} %get-tuple-element.128.gb_ref, ...), custom_call_target="tpu_custom_call" | custom-call | flops 1 | bytes 1 | tf_op jit(solution)/shard_map/own_back/pallas_call | solution.py:1457
  113.4 4.3 %collective-permute-done.30.back_ref = bf16[512,512]{1,0:T(8,128)(2,1)S(1)} collective-permute-done((bf16[512,512]{1,0:T(8,128)(2,1)S(1)}, bf16[512,512]{1,0:T(8,128)(2,1)S(1)}, u32[]{:S(2)}, u32[]{:S(2)}) %collective-permute-start.30) | collective-permute-done | bytes 524320 | tf_op jit(solution)/shard_map/ppermute | solution.py:1621
  118.1 1.9 %collective-permute-done.31 = bf16[4,4,72,384]{3,2,1,0:T(8,128)(2,1)S(1)} collective-permute-done((bf16[4,4,72,384]{3,2,1,0:T(8,128)(2,1)S(1)}, bf16[4,4,72,384]{3,2,1,0:T(8,128)(2,1)S(1)}, u32[]{:S(2)}, u32[]{:S(2)}) %collective-permute-start.31) | collective-permute-done | bytes 884768 | tf_op jit(solution)/shard_map/ppermute | solution.py:1556
  120.4 1.3 collective-permute-start.32
  121.7 1.5 %collective-permute-start.34 = (bf16[4,72,384]{2,1,0:T(8,128)(2,1)S(1)}, bf16[4,72,384]{2,1,0:T(8,128)(2,1)S(1)}, u32[]{:S(2)}, u32[]{:S(2)}) collective-permute-start(bf16[4,72,384]{2,1,0:T(8,128)(2,1)S(1)} %get-tuple-element.173), channel_id=1, source_target_pairs={{0,24},{4,28},{8,16},{12,20},{16,8},{20,12},{24,0},{28,4},{1,25},{... | collective-permute-start | bytes 663560 | tf_op jit(solution)/shard_map/ppermute | solution.py:1556
  124.0 3.1 %collective-permute-start.42 = (bf16[64,1152]{1,0:T(8,128)(2,1)S(1)}, bf16[64,1152]{1,0:T(8,128)(2,1)S(1)}, u32[]{:S(2)}, u32[]{:S(2)}) collective-permute-start(bf16[64,1152]{1,0:T(8,128)(2,1)S(1)} %get-tuple-element.175), channel_id=1, source_target_pairs={{0,3},{1,0},{2,1},{3,2},{4,7},{5,4},{6,5},{7,6},{8,11},{9,8},{10,9... | collective-permute-start | bytes 442376 | tf_op jit(solution)/shard_map/ppermute | solution.py:1560
  128.7 2.5 %collective-permute-start.40 = (bf16[64,1152]{1,0:T(8,128)(2,1)S(1)}, bf16[64,1152]{1,0:T(8,128)(2,1)S(1)}, u32[]{:S(2)}, u32[]{:S(2)}) collective-permute-start(bf16[64,1152]{1,0:T(8,128)(2,1)S(1)} %get-tuple-element.177), channel_id=1, source_target_pairs={{0,1},{1,2},{2,3},{3,0},{4,5},{5,6},{6,7},{7,4},{8,9},{9,10},{10,1... | collective-permute-start | bytes 442376 | tf_op jit(solution)/shard_map/ppermute | solution.py:1560
  131.2 2.3 %collective-permute-done.34 = bf16[4,72,384]{2,1,0:T(8,128)(2,1)S(1)} collective-permute-done((bf16[4,72,384]{2,1,0:T(8,128)(2,1)S(1)}, bf16[4,72,384]{2,1,0:T(8,128)(2,1)S(1)}, u32[]{:S(2)}, u32[]{:S(2)}) %collective-permute-start.34) | collective-permute-done | bytes 221216 | tf_op jit(solution)/shard_map/ppermute | solution.py:1556
  133.5 1.4 collective-permute-done.33
  135.9 2.4 %collective-permute-start.36 = (bf16[72,384]{1,0:T(8,128)(2,1)S(1)}, bf16[72,384]{1,0:T(8,128)(2,1)S(1)}, u32[]{:S(2)}, u32[]{:S(2)}) collective-permute-start(bf16[72,384]{1,0:T(8,128)(2,1)S(1)} %get-tuple-element.179), channel_id=1, source_target_pairs={{0,2},{1,3},{2,0},{3,1},{4,6},{5,7},{6,4},{7,5},{8,10},{9,11},{10,... | collective-permute-start | bytes 165896 | tf_op jit(solution)/shard_map/ppermute | solution.py:1560
  139.5 3.0 %close.1 = f32[768,512]{1,0:T(8,128)} custom-call(bf16[768,512]{1,0:T(8,128)(2,1)S(1)} %copy-done, f32[768,512]{1,0:T(8,128)S(1)} %get-tuple-element.147.gn_ref, bf16[512,512]{1,0:T(8,128)(2,1)S(1)} %collective-permute-done.30.back_ref, f32[768,512]{1,0:T(8,128)S(1)} %get-tuple-element.148.gh_ref, f32[8,512]{1,0:T(8,128)S(1)} %get-tuple-element.103.vec_ref), custom_call_target="tpu_custom_call" | custom-call | flops 1 | bytes 1 | tf_op jit(solution)/shard_map/close/pallas_call | solution.py:1489
  (129 shorter events, 33.8 us)
Async XLA Ops:
  2.6 10.0 %collective-permute-start.9 = (bf16[72,384]{1,0:T(8,128)(2,1)}, bf16[72,384]{1,0:T(8,128)(2,1)S(1)}, u32[]{:S(2)}, u32[]{:S(2)}) collective-permute-start(bf16[72,384]{1,0:T(8,128)(2,1)} %get-tuple-element.94), channel_id=1, source_target_pairs={{0,3},{1,0},{2,1},{3,2},{4,7},{5,4},{6,5},{7,6},{8,11},{9,8},{10,9... | collective-permute-start | bytes 165896 | tf_op jit(solution)/shard_map/ppermute | solution.py:1560
  7.6 6.2 %collective-permute-start.8 = (bf16[72,384]{1,0:T(8,128)(2,1)}, bf16[72,384]{1,0:T(8,128)(2,1)S(1)}, u32[]{:S(2)}, u32[]{:S(2)}) collective-permute-start(bf16[72,384]{1,0:T(8,128)(2,1)} %get-tuple-element.94), channel_id=1, source_target_pairs={{0,2},{1,3},{2,0},{3,1},{4,6},{5,7},{6,4},{7,5},{8,10},{9,11},{10,... | collective-permute-start | bytes 165896 | tf_op jit(solution)/shard_map/ppermute | solution.py:1560
  7.6 6.8 %collective-permute-start.7 = (bf16[72,384]{1,0:T(8,128)(2,1)}, bf16[72,384]{1,0:T(8,128)(2,1)S(1)}, u32[]{:S(2)}, u32[]{:S(2)}) collective-permute-start(bf16[72,384]{1,0:T(8,128)(2,1)} %get-tuple-element.94), channel_id=1, source_target_pairs={{0,1},{1,2},{2,3},{3,0},{4,5},{5,6},{6,7},{7,4},{8,9},{9,10},{10,1... | collective-permute-start | bytes 165896 | tf_op jit(solution)/shard_map/ppermute | solution.py:1560
  8.6 10.5 %collective-permute-start.5 = (bf16[64,1152]{1,0:T(8,128)(2,1)}, bf16[64,1152]{1,0:T(8,128)(2,1)S(1)}, u32[]{:S(2)}, u32[]{:S(2)}) collective-permute-start(bf16[64,1152]{1,0:T(8,128)(2,1)} %get-tuple-element.110), channel_id=1, source_target_pairs={{0,3},{1,0},{2,1},{3,2},{4,7},{5,4},{6,5},{7,6},{8,11},{9,8},{10,9... | collective-permute-start | bytes 442376 | tf_op jit(solution)/shard_map/ppermute | solution.py:1560
  11.5 14.7 %collective-permute-start.3 = (bf16[64,1152]{1,0:T(8,128)(2,1)}, bf16[64,1152]{1,0:T(8,128)(2,1)S(1)}, u32[]{:S(2)}, u32[]{:S(2)}) collective-permute-start(bf16[64,1152]{1,0:T(8,128)(2,1)} %get-tuple-element.110), channel_id=1, source_target_pairs={{0,2},{1,3},{2,0},{3,1},{4,6},{5,7},{6,4},{7,5},{8,10},{9,11},{10,... | collective-permute-start | bytes 442376 | tf_op jit(solution)/shard_map/ppermute | solution.py:1560
  12.6 13.6 %collective-permute-start.1 = (bf16[64,1152]{1,0:T(8,128)(2,1)}, bf16[64,1152]{1,0:T(8,128)(2,1)S(1)}, u32[]{:S(2)}, u32[]{:S(2)}) collective-permute-start(bf16[64,1152]{1,0:T(8,128)(2,1)} %get-tuple-element.110), channel_id=1, source_target_pairs={{0,1},{1,2},{2,3},{3,0},{4,5},{5,6},{6,7},{7,4},{8,9},{9,10},{10,1... | collective-permute-start | bytes 442376 | tf_op jit(solution)/shard_map/ppermute | solution.py:1560
  16.1 13.2 %collective-permute-start.12 = (bf16[4,72,384]{2,1,0:T(8,128)(2,1)S(1)}, bf16[4,72,384]{2,1,0:T(8,128)(2,1)S(1)}, u32[]{:S(2)}, u32[]{:S(2)}) collective-permute-start(bf16[4,72,384]{2,1,0:T(8,128)(2,1)S(1)} %pad_maximum_fusion.3.p0), channel_id=1, source_target_pairs={{0,24},{4,28},{8,16},{12,20},{16,8},{20,12},{24,0},{28,4},{1,25},{... | collective-permute-start | bytes 663560 | tf_op jit(solution)/shard_map/ppermute | solution.py:1556
  18.6 10.7 %collective-permute-start.11 = (bf16[4,72,384]{2,1,0:T(8,128)(2,1)S(1)}, bf16[4,72,384]{2,1,0:T(8,128)(2,1)}, u32[]{:S(2)}, u32[]{:S(2)}) collective-permute-start(bf16[4,72,384]{2,1,0:T(8,128)(2,1)S(1)} %pad_maximum_fusion.3.p0), channel_id=1, source_target_pairs={{0,16},{4,20},{8,24},{12,28},{16,0},{20,4},{24,8},{28,12},{1,17},{... | collective-permute-start | bytes 663560 | tf_op jit(solution)/shard_map/ppermute | solution.py:1556
  19.2 10.2 %collective-permute-start.10 = (bf16[4,72,384]{2,1,0:T(8,128)(2,1)S(1)}, bf16[4,72,384]{2,1,0:T(8,128)(2,1)}, u32[]{:S(2)}, u32[]{:S(2)}) collective-permute-start(bf16[4,72,384]{2,1,0:T(8,128)(2,1)S(1)} %pad_maximum_fusion.3.p0), channel_id=1, source_target_pairs={{0,8},{4,12},{8,0},{12,4},{16,24},{20,28},{24,16},{28,20},{1,9},{5... | collective-permute-start | bytes 663560 | tf_op jit(solution)/shard_map/ppermute | solution.py:1556
  28.2 6.0 %collective-permute-start = (bf16[64,1152]{1,0:T(8,128)(2,1)}, bf16[64,1152]{1,0:T(8,128)(2,1)S(1)}, u32[]{:S(2)}, u32[]{:S(2)}) collective-permute-start(bf16[64,1152]{1,0:T(8,128)(2,1)} %get-tuple-element.110), channel_id=1, source_target_pairs={{0,4},{4,0},{8,12},{12,8},{16,20},{20,16},{24,28},{28,24},{1,5},{5... | collective-permute-start | bytes 442376 | tf_op jit(solution)/shard_map/ppermute | solution.py:1556
  31.2 22.8 %collective-permute-start.20 = (bf16[4,64,1152]{2,1,0:T(8,128)(2,1)}, bf16[4,64,1152]{2,1,0:T(8,128)(2,1)S(1)}, u32[]{:S(2)}, u32[]{:S(2)}) collective-permute-start(bf16[4,64,1152]{2,1,0:T(8,128)(2,1)} %pad_maximum_fusion), channel_id=1, source_target_pairs={{0,16},{4,20},{8,24},{12,28},{16,0},{20,4},{24,8},{28,12},{1,17},{... | collective-permute-start | bytes 1769480 | tf_op jit(solution)/shard_map/ppermute | solution.py:1556
  32.7 21.3 %collective-permute-start.19 = (bf16[4,64,1152]{2,1,0:T(8,128)(2,1)}, bf16[4,64,1152]{2,1,0:T(8,128)(2,1)S(1)}, u32[]{:S(2)}, u32[]{:S(2)}) collective-permute-start(bf16[4,64,1152]{2,1,0:T(8,128)(2,1)} %pad_maximum_fusion), channel_id=1, source_target_pairs={{0,8},{4,12},{8,0},{12,4},{16,24},{20,28},{24,16},{28,20},{1,9},{5... | collective-permute-start | bytes 1769480 | tf_op jit(solution)/shard_map/ppermute | solution.py:1556
  34.2 6.1 %collective-permute-start.17 = (bf16[4,72,384]{2,1,0:T(8,128)(2,1)S(1)}, bf16[4,72,384]{2,1,0:T(8,128)(2,1)S(1)}, u32[]{:S(2)}, u32[]{:S(2)}) collective-permute-start(bf16[4,72,384]{2,1,0:T(8,128)(2,1)S(1)} %collective-permute-done.12.p3), channel_id=1, source_target_pairs={{0,4},{4,0},{8,12},{12,8},{16,20},{20,16},{24,28},{28,24},{1,5},{5... | collective-permute-start | bytes 663560 | tf_op jit(solution)/shard_map/ppermute | solution.py:1556
  36.5 19.2 %collective-permute-start.18 = (bf16[512,512]{1,0:T(8,128)(2,1)}, bf16[512,512]{1,0:T(8,128)(2,1)S(1)}, u32[]{:S(2)}, u32[]{:S(2)}) collective-permute-start(bf16[512,512]{1,0:T(8,128)(2,1)} %slice.60), channel_id=1, source_target_pairs={{0,1},{1,2},{2,3},{4,5},{5,6},{6,7},{8,9},{9,10},{10,11},{12,13},{... | collective-permute-start | bytes 1572872 | tf_op jit(solution)/shard_map/ppermute | solution.py:1592
  54.1 10.4 %collective-permute-start.21 = (bf16[2,64,1152]{2,1,0:T(8,128)(2,1)S(1)}, bf16[2,64,1152]{2,1,0:T(8,128)(2,1)S(1)}, u32[]{:S(2)}, u32[]{:S(2)}) collective-permute-start(bf16[2,64,1152]{2,1,0:T(8,128)(2,1)S(1)} %slice.61), channel_id=1, source_target_pairs={{0,8},{4,12},{8,0},{12,4},{16,24},{20,28},{24,16},{28,20},{1,9},{5... | collective-permute-start | bytes 884744 | tf_op jit(solution)/shard_map/ppermute | solution.py:1556
  54.7 9.7 %collective-permute-start.22 = (bf16[2,64,1152]{2,1,0:T(8,128)(2,1)S(1)}, bf16[2,64,1152]{2,1,0:T(8,128)(2,1)S(1)}, u32[]{:S(2)}, u32[]{:S(2)}) collective-permute-start(bf16[2,64,1152]{2,1,0:T(8,128)(2,1)S(1)} %slice.62), channel_id=1, source_target_pairs={{0,16},{4,20},{8,24},{12,28},{16,0},{20,4},{24,8},{28,12},{1,17},{... | collective-permute-start | bytes 884744 | tf_op jit(solution)/shard_map/ppermute | solution.py:1556
  55.2 10.0 %collective-permute-start.23 = (bf16[4,64,1152]{2,1,0:T(8,128)(2,1)S(1)}, bf16[4,64,1152]{2,1,0:T(8,128)(2,1)S(1)}, u32[]{:S(2)}, u32[]{:S(2)}) collective-permute-start(bf16[4,64,1152]{2,1,0:T(8,128)(2,1)S(1)} %collective-permute-done.19.rest_4_), channel_id=1, source_target_pairs={{0,4},{4,0},{8,12},{12,8},{16,20},{20,16},{24,28},{28,24},{1,5},{5... | collective-permute-start | bytes 1769480 | tf_op jit(solution)/shard_map/ppermute | solution.py:1556
  55.2 10.0 %collective-permute-start.24 = (bf16[4,64,1152]{2,1,0:T(8,128)(2,1)S(1)}, bf16[4,64,1152]{2,1,0:T(8,128)(2,1)S(1)}, u32[]{:S(2)}, u32[]{:S(2)}) collective-permute-start(bf16[4,64,1152]{2,1,0:T(8,128)(2,1)S(1)} %collective-permute-done.20.rest_5_), channel_id=1, source_target_pairs={{0,4},{4,0},{8,12},{12,8},{16,20},{20,16},{24,28},{28,24},{1,5},{5... | collective-permute-start | bytes 1769480 | tf_op jit(solution)/shard_map/ppermute | solution.py:1556
  91.2 9.8 %collective-permute-start.29 = (bf16[2,64,1152]{2,1,0:T(8,128)(2,1)S(1)}, bf16[2,64,1152]{2,1,0:T(8,128)(2,1)S(1)}, u32[]{:S(2)}, u32[]{:S(2)}) collective-permute-start(bf16[2,64,1152]{2,1,0:T(8,128)(2,1)S(1)} %get-tuple-element.169), channel_id=1, source_target_pairs={{0,16},{4,20},{8,24},{12,28},{16,0},{20,4},{24,8},{28,12},{1,17},{... | collective-permute-start | bytes 884744 | tf_op jit(solution)/shard_map/ppermute | solution.py:1556
  92.9 9.0 %collective-permute-start.28 = (bf16[2,64,1152]{2,1,0:T(8,128)(2,1)S(1)}, bf16[2,64,1152]{2,1,0:T(8,128)(2,1)S(1)}, u32[]{:S(2)}, u32[]{:S(2)}) collective-permute-start(bf16[2,64,1152]{2,1,0:T(8,128)(2,1)S(1)} %get-tuple-element.170), channel_id=1, source_target_pairs={{0,8},{4,12},{8,0},{12,4},{16,24},{20,28},{24,16},{28,20},{1,9},{5... | collective-permute-start | bytes 884744 | tf_op jit(solution)/shard_map/ppermute | solution.py:1556
  99.7 17.9 %collective-permute-start.30 = (bf16[512,512]{1,0:T(8,128)(2,1)S(1)}, bf16[512,512]{1,0:T(8,128)(2,1)S(1)}, u32[]{:S(2)}, u32[]{:S(2)}) collective-permute-start(bf16[512,512]{1,0:T(8,128)(2,1)S(1)} %get-tuple-element.130), channel_id=1, source_target_pairs={{1,0},{2,1},{3,2},{5,4},{6,5},{7,6},{9,8},{10,9},{11,10},{13,12},{... | collective-permute-start | bytes 1572872 | tf_op jit(solution)/shard_map/ppermute | solution.py:1621
  102.1 15.6 %collective-permute-start.38 = (bf16[4,64,1152]{2,1,0:T(8,128)(2,1)S(1)}, bf16[4,64,1152]{2,1,0:T(8,128)(2,1)S(1)}, u32[]{:S(2)}, u32[]{:S(2)}) collective-permute-start(bf16[4,64,1152]{2,1,0:T(8,128)(2,1)S(1)} %pad_maximum_fusion.1), channel_id=1, source_target_pairs={{0,8},{4,12},{8,0},{12,4},{16,24},{20,28},{24,16},{28,20},{1,9},{5... | collective-permute-start | bytes 1769480 | tf_op jit(solution)/shard_map/ppermute | solution.py:1556
  103.7 14.3 %collective-permute-start.39 = (bf16[4,64,1152]{2,1,0:T(8,128)(2,1)S(1)}, bf16[4,64,1152]{2,1,0:T(8,128)(2,1)S(1)}, u32[]{:S(2)}, u32[]{:S(2)}) collective-permute-start(bf16[4,64,1152]{2,1,0:T(8,128)(2,1)S(1)} %pad_maximum_fusion.2), channel_id=1, source_target_pairs={{0,16},{4,20},{8,24},{12,28},{16,0},{20,4},{24,8},{28,12},{1,17},{... | collective-permute-start | bytes 1769480 | tf_op jit(solution)/shard_map/ppermute | solution.py:1556
  120.4 8.3 %collective-permute-start.32 = (bf16[4,72,384]{2,1,0:T(8,128)(2,1)S(1)}, bf16[4,72,384]{2,1,0:T(8,128)(2,1)S(1)}, u32[]{:S(2)}, u32[]{:S(2)}) collective-permute-start(bf16[4,72,384]{2,1,0:T(8,128)(2,1)S(1)} %get-tuple-element.172), channel_id=1, source_target_pairs={{0,8},{4,12},{8,0},{12,4},{16,24},{20,28},{24,16},{28,20},{1,9},{5... | collective-permute-start | bytes 663560 | tf_op jit(solution)/shard_map/ppermute | solution.py:1556
  121.7 11.8 %collective-permute-start.34 = (bf16[4,72,384]{2,1,0:T(8,128)(2,1)S(1)}, bf16[4,72,384]{2,1,0:T(8,128)(2,1)S(1)}, u32[]{:S(2)}, u32[]{:S(2)}) collective-permute-start(bf16[4,72,384]{2,1,0:T(8,128)(2,1)S(1)} %get-tuple-element.173), channel_id=1, source_target_pairs={{0,24},{4,28},{8,16},{12,20},{16,8},{20,12},{24,0},{28,4},{1,25},{... | collective-permute-start | bytes 663560 | tf_op jit(solution)/shard_map/ppermute | solution.py:1556
  123.2 11.6 %collective-permute-start.33 = (bf16[4,72,384]{2,1,0:T(8,128)(2,1)S(1)}, bf16[4,72,384]{2,1,0:T(8,128)(2,1)S(1)}, u32[]{:S(2)}, u32[]{:S(2)}) collective-permute-start(bf16[4,72,384]{2,1,0:T(8,128)(2,1)S(1)} %get-tuple-element.174), channel_id=1, source_target_pairs={{0,16},{4,20},{8,24},{12,28},{16,0},{20,4},{24,8},{28,12},{1,17},{... | collective-permute-start | bytes 663560 | tf_op jit(solution)/shard_map/ppermute | solution.py:1556
  124.0 14.3 %collective-permute-start.42 = (bf16[64,1152]{1,0:T(8,128)(2,1)S(1)}, bf16[64,1152]{1,0:T(8,128)(2,1)S(1)}, u32[]{:S(2)}, u32[]{:S(2)}) collective-permute-start(bf16[64,1152]{1,0:T(8,128)(2,1)S(1)} %get-tuple-element.175), channel_id=1, source_target_pairs={{0,3},{1,0},{2,1},{3,2},{4,7},{5,4},{6,5},{7,6},{8,11},{9,8},{10,9... | collective-permute-start | bytes 442376 | tf_op jit(solution)/shard_map/ppermute | solution.py:1560
  127.1 15.6 %collective-permute-start.41 = (bf16[64,1152]{1,0:T(8,128)(2,1)S(1)}, bf16[64,1152]{1,0:T(8,128)(2,1)S(1)}, u32[]{:S(2)}, u32[]{:S(2)}) collective-permute-start(bf16[64,1152]{1,0:T(8,128)(2,1)S(1)} %get-tuple-element.176), channel_id=1, source_target_pairs={{0,2},{1,3},{2,0},{3,1},{4,6},{5,7},{6,4},{7,5},{8,10},{9,11},{10,... | collective-permute-start | bytes 442376 | tf_op jit(solution)/shard_map/ppermute | solution.py:1560
  128.7 14.0 %collective-permute-start.40 = (bf16[64,1152]{1,0:T(8,128)(2,1)S(1)}, bf16[64,1152]{1,0:T(8,128)(2,1)S(1)}, u32[]{:S(2)}, u32[]{:S(2)}) collective-permute-start(bf16[64,1152]{1,0:T(8,128)(2,1)S(1)} %get-tuple-element.177), channel_id=1, source_target_pairs={{0,1},{1,2},{2,3},{3,0},{4,5},{5,6},{6,7},{7,4},{8,9},{9,10},{10,1... | collective-permute-start | bytes 442376 | tf_op jit(solution)/shard_map/ppermute | solution.py:1560
  135.0 8.5 %collective-permute-start.37 = (bf16[72,384]{1,0:T(8,128)(2,1)S(1)}, bf16[72,384]{1,0:T(8,128)(2,1)S(1)}, u32[]{:S(2)}, u32[]{:S(2)}) collective-permute-start(bf16[72,384]{1,0:T(8,128)(2,1)S(1)} %get-tuple-element.178), channel_id=1, source_target_pairs={{0,3},{1,0},{2,1},{3,2},{4,7},{5,4},{6,5},{7,6},{8,11},{9,8},{10,9... | collective-permute-start | bytes 165896 | tf_op jit(solution)/shard_map/ppermute | solution.py:1560
  135.9 8.6 %collective-permute-start.36 = (bf16[72,384]{1,0:T(8,128)(2,1)S(1)}, bf16[72,384]{1,0:T(8,128)(2,1)S(1)}, u32[]{:S(2)}, u32[]{:S(2)}) collective-permute-start(bf16[72,384]{1,0:T(8,128)(2,1)S(1)} %get-tuple-element.179), channel_id=1, source_target_pairs={{0,2},{1,3},{2,0},{3,1},{4,6},{5,7},{6,4},{7,5},{8,10},{9,11},{10,... | collective-permute-start | bytes 165896 | tf_op jit(solution)/shard_map/ppermute | solution.py:1560
  138.3 6.3 %collective-permute-start.35 = (bf16[72,384]{1,0:T(8,128)(2,1)S(1)}, bf16[72,384]{1,0:T(8,128)(2,1)S(1)}, u32[]{:S(2)}, u32[]{:S(2)}) collective-permute-start(bf16[72,384]{1,0:T(8,128)(2,1)S(1)} %get-tuple-element.180), channel_id=1, source_target_pairs={{0,1},{1,2},{2,3},{3,0},{4,5},{5,6},{6,7},{7,4},{8,9},{9,10},{10,1... | collective-permute-start | bytes 165896 | tf_op jit(solution)/shard_map/ppermute | solution.py:1560
  (29 other events, 169.4 us)
where the time goes:
time: 146 us; the launch traced here: 145 us
  Pallas kernels  61.5 us (42%)
  starting transfers between devices  45.1 us (31%)
  waiting for transfers between devices  24.9 us (17%)
  local copies, waits for them, and re-layouts  7.61 us (5%)
  other arithmetic  5.18 us (4%)
    ppermute x12, starting transfers between devices, to_step(): return lax.ppermute(x, 'tp', [(i, (i + step) % 4) for i in range(4)])  20.9 us
    ppermute x29, starting transfers between devices, to_mask(): return lax.ppermute(x, 'fsdp', [(i, i ^ mask) for i in range(8)])  19.8 us
    pallas_call x1, Pallas kernels, central(): pl.pallas_call(functools.partial(central_kernel, rb), out_shape=shapes, i...  19.2 us
    ppermute x29, waiting for transfers between devices, to_mask(): return lax.ppermute(x, 'fsdp', [(i, i ^ mask) for i in range(8)])  10.9 us
    ppermute x12, waiting for transfers between devices, to_step(): return lax.ppermute(x, 'tp', [(i, (i + step) % 4) for i in range(4)])  9.65 us
    pallas_call x2, Pallas kernels, pull_near(): pl.pallas_call(functools.partial(pull_near_kernel, base), out_shape=(jax....  8.99 us
    pallas_call x1, Pallas kernels, attend_near(): pl.pallas_call(attend_near_kernel, out_shape=(jax.ShapeDtypeStruct((HALO,...  6.25 us
    unnamed x36, local copies, waits for them, and re-layouts  6.05 us
  transfers between devices with their start and end apart: 43, of which 18 were waited for; matrix products, arithmetic and copies ran while one was open for 4% of the time, Pallas kernels for 27%

commit v1 on v0

--- a/solution.py
+++ b/solution.py
@@ -687,7 +687,7 @@
 
 def project_kernel(
     tokens_all, x_ref, idc_ref, p0, p1, p2, p3, p4, p5, p6, p7, p8,
-    q_ref, k_ref, v_ref, kt_ref, nt_ref, w_ref, vec_ref, bup_ref, scale_ref, head_ref, ext_ref, sem
+    q_ref, k_ref, v_ref, kt_ref, nt_ref, w_ref, vec_ref, bup_ref, scale_ref, head_ref, ext_ref, n_ref, sem
 ):
     me, place = lax.axis_index("fsdp"), lax.axis_index("tp")
     pieces = (p0, p1, p2, p3, p4, p5, p6, p7, p8)
@@ -734,21 +734,28 @@
         head_ref[:, rows_of(tp * COLS, COLS)] = block
         for i in range(4):
             bup_ref[:, rows_of(tp * FFC + 128 * i, 128)] = jnp.broadcast_to(block[2 + i : 3 + i], (8, 128))
-    pltpu.make_async_copy(w_ref, w_ref, sem.at[1]).wait()
-
-    def own_rows(i, carry):
-        rows = rows_of(i * 128, 128)
-        n1 = first_norm(x_ref[rows, :], vectors, me, nt_ref, rows)
-        made = dot(n1, w_ref[...])
-        spare_q, spare_k, spare_v = spare_lanes(idc_ref[rows_of(HALO + i * 128, 128), :])
+
+    def norm(i, carry):
+        rows = rows_of(i * QB, QB)
+        n_ref[rows, :] = first_norm(x_ref[rows, :], vectors, me, nt_ref, rows)
+        return carry
+
+    def product(one):
+        one["made"] = dot(n_ref[one["rows"], :], w_ref[...])
+
+    def keep(one):
+        rows, made = one["rows"], one.pop("made")
+        spare_q, spare_k, spare_v = spare_lanes(idc_ref[slice(HALO + rows.start, HALO + rows.stop), :])
         for t in range(4):
             lanes = slice(t * COLS, (t + 1) * COLS)
             q = (made[:, t * WA : t * WA + COLS] + head_ref[0:1, lanes]).astype(BF16)
             keep_heads(q_ref, rows, t, q * jnp.asarray(SCALE, BF16), spare_q)
             keep_keys(made[:, t * WA + COLS : (t + 1) * WA], head_ref, k_ref, v_ref, kt_ref, rows, t, spare_k, spare_v)
-        return carry
-
-    lax.fori_loop(0, x_ref.shape[0] // 128, own_rows, 0)
+
+    blocks = [dict(rows=slice(i * QB, (i + 1) * QB)) for i in range(x_ref.shape[0] // QB)]
+    lax.fori_loop(0, x_ref.shape[0] // QB, norm, 0)
+    pltpu.make_async_copy(w_ref, w_ref, sem.at[1]).wait()
+    staged(blocks, (product, keep))
 
 
 DOCS = 48
@@ -818,7 +825,7 @@
         out_shape=shapes,
         in_specs=[VMEM, VMEM] + [FAR] * 9,
         out_specs=[VMEM] * len(shapes),
-        scratch_shapes=[pltpu.VMEM((32, EXTRA, WA), BF16), pltpu.SemaphoreType.DMA((2,))],
+        scratch_shapes=[pltpu.VMEM((32, EXTRA, WA), BF16), pltpu.VMEM((own, D), BF16), pltpu.SemaphoreType.DMA((2,))],
         compiler_params=params(6),
         cost_estimate=SMALL,
         name="project",
@@ -828,16 +835,19 @@
 def project_halo_kernel(x_ref, idc_ref, w_ref, vec_ref, head_ref, k_ref, v_ref, kt_ref, nt_ref):
     me = lax.axis_index("fsdp")
 
-    def halo_rows(i, carry):
-        rows = rows_of(i * 128, 128)
-        n1 = first_norm(x_ref[rows, :], vec_ref[...], me, nt_ref, rows)
+    def norm(one):
+        one["n1"] = first_norm(x_ref[one["rows"], :], vec_ref[...], me, nt_ref, one["rows"])
+
+    def product(one):
+        one["made"] = [dot(one["n1"], w_ref[:, t * WA + COLS : (t + 1) * WA]) for t in range(4)]
+
+    def keep(one):
+        rows = one["rows"]
         _, spare_k, spare_v = spare_lanes(idc_ref[rows, :])
-        for t in range(4):
-            made = dot(n1, w_ref[:, t * WA + COLS : (t + 1) * WA])
+        for t, made in enumerate(one.pop("made")):
             keep_keys(made, head_ref, k_ref, v_ref, kt_ref, rows, t, spare_k, spare_v)
-        return carry
-
-    lax.fori_loop(0, HALO // 128, halo_rows, 0)
+
+    staged([dict(rows=slice(i * QB, (i + 1) * QB)) for i in range(HALO // QB)], (norm, product, keep))
 
 
 def project_halo(x, id_col, w, vec, head):
@@ -993,26 +1003,26 @@
     )(q, k_halo, k, v_halo, v)
 
 
-PIECES_F = ((0, (0,)), (0, (1,)), (0, (2,)), (0, (3,)), (2, (0, 1, 2, 3)), (4, (0, 1, 2, 3)), (6, (0, 1)), (6, (2, 3)))
+PIECES_F = ((0, ALL), (2, ALL), (4, ALL), (6, ALL[0:2]), (6, ALL[2:4]))
 
 
 def central_kernel(
     rb, x_ref, oa_ref, oc_ref, teacher_ref, cot_ref, mask_ref, vec_ref, bup_ref, scale_ref,
     *rest
 ):
-    pieces = rest[:16]
+    pieces = rest[:10]
     (
     out_ref, gh_ref, ga_ref, theirs_ref, mine_ref, small_ref, gbup_ref,
     wo_ref, wup_ref, wdn_ref, slope_ref, hid_ref, gpre_ref, n2t_ref, gmlpt_ref, gattnt_ref, place_ref, o_ref,
     h1_ref, xhat_ref, n2_ref, gmlp_ref, sem
-    ) = rest[16:]
+    ) = rest[10:]
     me, place = lax.axis_index("fsdp"), lax.axis_index("tp")
     own, ff = x_ref.shape[0], 4 * FFC
     parts = ((wo_ref, 0, COLS), (wup_ref, COLS, FFC), (wdn_ref, COLS + FFC, FFC))
     for n, (dst, start, size) in enumerate(parts):
         for j, ref in enumerate(pieces):
-            mask, steps = PIECES_F[j % 8]
-            owner = lax.bitwise_xor(me, mask + j // 8)
+            mask, steps = PIECES_F[j % 5]
+            owner = lax.bitwise_xor(me, mask + j // 5)
             for i, s in enumerate(steps):
                 tp = lax.bitwise_and(place - s + 4, 3)
                 pltpu.make_async_copy(
@@ -1173,7 +1183,7 @@
     return pl.pallas_call(
         functools.partial(central_kernel, rb),
         out_shape=shapes,
-        in_specs=[VMEM] * 9 + [FAR] * 16,
+        in_specs=[VMEM] * 9 + [FAR] * 10,
         out_specs=[VMEM] * len(shapes),
         scratch_shapes=[
             pltpu.VMEM((D, D), BF16),
@@ -1583,13 +1593,14 @@
     steps_a = [shard_a] + [to_step(shard_a, s) for s in (1, 2, 3)]
     line_a = jnp.stack(steps_a)
     steps_f = [shard_f] + [to_step(shard_f, s) for s in (1, 2, 3)]
-    over_f = [to_mask(x, 1) for x in steps_f]
     near_a = [to_mask(line_a, m) for m in (2, 4, 6)]
-    halves_a = after([jnp.stack(steps_a[0:2]), jnp.stack(steps_a[2:4])], steps_f)
+    last_rows = layer_input[own - HALO :]
+    halves_a, last_rows = after(([jnp.stack(steps_a[0:2]), jnp.stack(steps_a[2:4])], last_rows), steps_f)
     over_a = [to_mask(a, 1) for a in halves_a]
     line_f = jnp.stack(after(steps_f, (over_a, near_a)))
+    over_f = to_mask(line_f, 1)
     pieces_a = [line_a] + near_a + over_a + [to_mask(a, 1) for a in near_a]
-    halo = lax.ppermute(layer_input[own - HALO :], "tp", [(i, i + 1) for i in range(3)])
+    halo = lax.ppermute(last_rows, "tp", [(i, i + 1) for i in range(3)])
     f_x, f_y = to_mask(line_f, 2), to_mask(line_f, 4)
 
     ids = segment_ids + 16 * jnp.arange(segment_ids.shape[0], dtype=jnp.int32)[:, None]
@@ -1605,7 +1616,7 @@
     k_halo, v_halo, kt_halo, nt_halo = project_halo(halo, id_col, w_all, vec, head)
     o_near, qa_near = attend_near(q, k_halo, k, v_halo, v)
     near_f = [f_x, f_y] + after(f_xy, o_near)
-    pieces_f = [x[None] for x in steps_f] + near_f + [x[None] for x in over_f] + [to_mask(a, 1) for a in near_f]
+    pieces_f = [line_f] + near_f + [over_f] + [to_mask(a, 1) for a in near_f]
     layer_out, g_h1, ga, theirs_f, mine_f, small_two, gbup = central(
         layer_input, o_near, o_far, teacher, cotangent, mask, vec, bup, scale, pieces_f
     )

time: 146 us -> 139 us (0.952)
  Pallas kernels: 61.5 us -> 58.8 us
  waiting for transfers between devices: 24.9 us -> 22.7 us
  other arithmetic: 5.18 us -> 3.44 us
    ppermute x12, waiting for transfers between devices: 9.65 us -> 7.76 us  [to_step(): return lax.ppermute(x, 'tp', [(i, (i + step) % 4) for i in range(4)])]
    another operation x1, other arithmetic: 1.81 us -> 0.09 us  [local_fast(): line_f = jnp.stack(after(steps_f, (over_a, near_a)))]
    pallas_call x1, Pallas kernels: 5.29 us -> 3.81 us  [project(): pl.pallas_call(functools.partial(project_kernel, float(tokens_all)), out_...]
    ppermute x29 -> x26, starting transfers between devices: 19.8 us -> 19 us  [to_mask(): return lax.ppermute(x, 'fsdp', [(i, i ^ mask) for i in range(8)])]
    unnamed x36 -> x28, local copies, waits for them, and re-layouts: 6.05 us -> 5.57 us
    ppermute x29 -> x26, waiting for transfers between devices: 10.9 us -> 11.2 us  [to_mask(): return lax.ppermute(x, 'fsdp', [(i, i ^ mask) for i in range(8)])]
  transfers between devices with their start and end apart: 43 -> 40, of which waited for: 18 -> 17; matrix products, arithmetic and copies ran while one was open for 4% -> 3% of each run, Pallas kernels for 27% -> 27%
where the time goes in v1:
time: 139 us
  Pallas kernels  58.8 us (42%)
  starting transfers between devices  44.7 us (32%)
  waiting for transfers between devices  22.7 us (16%)
  local copies, waits for them, and re-layouts  8.18 us (6%)
  other arithmetic  3.44 us (2%)
    ppermute x12, starting transfers between devices, to_step(): return lax.ppermute(x, 'tp', [(i, (i + step) % 4) for i in range(4)])  21 us
    pallas_call x1, Pallas kernels, central(): pl.pallas_call(functools.partial(central_kernel, rb), out_shape=shapes, i...  19.1 us
    ppermute x26, starting transfers between devices, to_mask(): return lax.ppermute(x, 'fsdp', [(i, i ^ mask) for i in range(8)])  19 us
    ppermute x26, waiting for transfers between devices, to_mask(): return lax.ppermute(x, 'fsdp', [(i, i ^ mask) for i in range(8)])  11.2 us
    pallas_call x2, Pallas kernels, pull_near(): pl.pallas_call(functools.partial(pull_near_kernel, base), out_shape=(jax....  8.99 us
    ppermute x12, waiting for transfers between devices, to_step(): return lax.ppermute(x, 'tp', [(i, (i + step) % 4) for i in range(4)])  7.76 us
    pallas_call x1, Pallas kernels, attend_near(): pl.pallas_call(attend_near_kernel, out_shape=(jax.ShapeDtypeStruct((HALO,...  6.25 us
    unnamed x28, local copies, waits for them, and re-layouts  5.57 us
  transfers between devices with their start and end apart: 40, of which 17 were waited for; matrix products, arithmetic and copies ran while one was open for 3% of the time, Pallas kernels for 27%

profile of v1, /device:TPU:0, one launch (start us, length us, event | category | flops | bytes accessed | tf_op | source)
XLA Modules:
  0.0 139.0 jit_solution(17808640762768162749)
XLA Ops:
  0.7 1.9 %pack_weights.1 = (bf16[72,384]{1,0:T(8,128)(2,1)}, bf16[64,1152]{1,0:T(8,128)(2,1)}) custom-call(bf16[64,128]{1,0:T(8,128)(2,1)} %wq_ref.1, bf16[64,128]{1,0:T(8,128)(2,1)} %wk_ref.1, bf16[64,128]{1,0:T(8,128)(2,1)} %wv_ref.1, bf16[64,128]{1,0:T(8,128)(2,1)} %bitcast.72, bf16[64,512]{1,0:T(8,128)(2,1)} %wup_ref.1, bf16[64,512]{1,0:T(8,128)(2,1)} %bitcast.71, ...), custom_call_target="tpu_custom_call" | custom-call | tf_op jit(solution)/shard_map/pack_weights/pallas_call | solution.py:677
  2.5 5.1 %collective-permute-start.5 = (bf16[72,384]{1,0:T(8,128)(2,1)}, bf16[72,384]{1,0:T(8,128)(2,1)S(1)}, u32[]{:S(2)}, u32[]{:S(2)}) collective-permute-start(bf16[72,384]{1,0:T(8,128)(2,1)} %get-tuple-element.94), channel_id=1, source_target_pairs={{0,3},{1,0},{2,1},{3,2},{4,7},{5,4},{6,5},{7,6},{8,11},{9,8},{10,9... | collective-permute-start | bytes 165896 | tf_op jit(solution)/shard_map/ppermute | solution.py:1570
  8.7 2.8 %collective-permute-start.2 = (bf16[64,1152]{1,0:T(8,128)(2,1)}, bf16[64,1152]{1,0:T(8,128)(2,1)S(1)}, u32[]{:S(2)}, u32[]{:S(2)}) collective-permute-start(bf16[64,1152]{1,0:T(8,128)(2,1)} %get-tuple-element.97), channel_id=1, source_target_pairs={{0,3},{1,0},{2,1},{3,2},{4,7},{5,4},{6,5},{7,6},{8,11},{9,8},{10,9... | collective-permute-start | bytes 442376 | tf_op jit(solution)/shard_map/ppermute | solution.py:1570
  12.6 1.9 %slice.60 = bf16[512,512]{1,0:T(8,128)(2,1)} slice(bf16[768,512]{1,0:T(8,128)(2,1)} %x_ref.6), slice={[256:768], [0:512]} | slice | bytes 1048576 | tf_op jit(solution)/shard_map/slice | solution.py:1597
  16.2 2.5 %collective-permute-start.10 = (bf16[4,72,384]{2,1,0:T(8,128)(2,1)S(1)}, bf16[4,72,384]{2,1,0:T(8,128)(2,1)S(1)}, u32[]{:S(2)}, u32[]{:S(2)}) collective-permute-start(bf16[4,72,384]{2,1,0:T(8,128)(2,1)S(1)} %pad_maximum_fusion.3.p0), channel_id=1, source_target_pairs={{0,24},{4,28},{8,16},{12,20},{16,8},{20,12},{24,0},{28,4},{1,25},{... | collective-permute-start | bytes 663560 | tf_op jit(solution)/shard_map/ppermute | solution.py:1566
  19.7 6.5 %collective-permute-done.1 = bf16[64,1152]{1,0:T(8,128)(2,1)S(1)} collective-permute-done((bf16[64,1152]{1,0:T(8,128)(2,1)}, bf16[64,1152]{1,0:T(8,128)(2,1)S(1)}, u32[]{:S(2)}, u32[]{:S(2)}) %collective-permute-start.1) | collective-permute-done | bytes 147488 | tf_op jit(solution)/shard_map/ppermute | solution.py:1570
  29.2 1.5 %collective-permute-start.17 = (bf16[4,64,1152]{2,1,0:T(8,128)(2,1)S(1)}, bf16[4,64,1152]{2,1,0:T(8,128)(2,1)S(1)}, u32[]{:S(2)}, u32[]{:S(2)}) collective-permute-start(bf16[4,64,1152]{2,1,0:T(8,128)(2,1)S(1)} %pad_maximum_fusion.rest_0_), channel_id=1, source_target_pairs={{0,16},{4,20},{8,24},{12,28},{16,0},{20,4},{24,8},{28,12},{1,17},{... | collective-permute-start | bytes 1769480 | tf_op jit(solution)/shard_map/ppermute | solution.py:1566
  30.7 1.5 %collective-permute-start.16 = (bf16[4,64,1152]{2,1,0:T(8,128)(2,1)S(1)}, bf16[4,64,1152]{2,1,0:T(8,128)(2,1)S(1)}, u32[]{:S(2)}, u32[]{:S(2)}) collective-permute-start(bf16[4,64,1152]{2,1,0:T(8,128)(2,1)S(1)} %pad_maximum_fusion.rest_0_), channel_id=1, source_target_pairs={{0,8},{4,12},{8,0},{12,4},{16,24},{20,28},{24,16},{28,20},{1,9},{5... | collective-permute-start | bytes 1769480 | tf_op jit(solution)/shard_map/ppermute | solution.py:1566
  32.2 3.5 %collective-permute-start.15 = (bf16[512,512]{1,0:T(8,128)(2,1)}, bf16[512,512]{1,0:T(8,128)(2,1)S(1)}, u32[]{:S(2)}, u32[]{:S(2)}) collective-permute-start(bf16[512,512]{1,0:T(8,128)(2,1)} %slice.60), channel_id=1, source_target_pairs={{0,1},{1,2},{2,3},{4,5},{5,6},{6,7},{8,9},{9,10},{10,11},{12,13},{... | collective-permute-start | bytes 1572872 | tf_op jit(solution)/shard_map/ppermute | solution.py:1603
  42.0 3.8 %project.1 = (bf16[768,1024]{1,0:T(8,128)(2,1)S(1)}, bf16[768,1024]{1,0:T(8,128)(2,1)S(1)}, bf16[768,1024]{1,0:T(8,128)(2,1)S(1)}, bf16[512,768]{1,0:T(8,128)(2,...) custom-call(bf16[768,512]{1,0:T(8,128)(2,1)S(1)} %copy-done, ...), custom_call_target="tpu_custom_call" | custom-call | flops 1 | bytes 1 | tf_op jit(solution)/shard_map/project/pallas_call | solution.py:823
  45.9 3.0 %attend_far.1 = (bf16[256,512]{1,0:T(8,128)(2,1)S(1)}, bf16[256,1024]{1,0:T(8,128)(2,1)S(1)}) custom-call(bf16[768,1024]{1,0:T(8,128)(2,1)S(1)} %get-tuple-element.102.q_ref, bf16[768,1024]{1,0:T(8,128)(2,1)S(1)} %get-tuple-element.104.k_ref.ko_ref, bf16[768,1024]{1,0:T(8,128)(2,1)S(1)} %get-tuple-element.105.v_ref.vo_ref), custom_call_target="tpu_custom_call" | custom-call | flops 1 | bytes 1 | tf_op jit(solution)/shard_map/attend_far/pallas_call | solution.py:958
  50.6 1.3 project_halo.1
  51.9 6.2 %attend_near.1 = (bf16[512,512]{1,0:T(8,128)(2,1)S(1)}, bf16[512,1024]{1,0:T(8,128)(2,1)S(1)}) custom-call(bf16[768,1024]{1,0:T(8,128)(2,1)S(1)} %get-tuple-element.102.q_ref, bf16[512,1024]{1,0:T(8,128)(2,1)S(1)} %get-tuple-element.111.kh_ref, bf16[768,1024]{1,0:T(8,128)(2,1)S(1)} %get-tuple-element.104.k_ref.ko_ref, ...), custom_call_target="tpu_custom_call" | custom-call | flops 1 | bytes 1 | tf_op jit(solution)/shard_map/attend_near/pallas_call | solution.py:994
  60.5 19.1 %central.1 = (bf16[768,512]{1,0:T(8,128)(2,1)}, f32[768,512]{1,0:T(8,128)S(1)}, bf16[768,1024]{1,0:T(8,128)(2,1)S(1)}, bf16[4,4,64,1152]{3,2,1,0:T(8,128)(2,1)S(...) custom-call(bf16[768,512]{1,0:T(8,128)(2,1)S(1)} %copy-done, ...), custom_call_target="tpu_custom_call" | custom-call | flops 1 | bytes 1 | tf_op jit(solution)/shard_map/central/pallas_call | solution.py:1183
  79.8 4.6 %pull_near.2 = (bf16[512,512]{1,0:T(8,128)(2,1)S(1)}, bf16[512,256]{1,0:T(8,128)(2,1)S(1)}, f32[512,512]{1,0:T(8,128)S(1)}) custom-call(bf16[512,1024]{1,0:T(8,128)(2,1)S(1)} %get-tuple-element.129.q_ref, bf16[768,1024]{1,0:T(8,128)(2,1)S(1)} %get-tuple-element.122.g_ref.go_ref, bf16[512,1024]{1,0:T(8,128)(2,1)S(1)} %get-tuple-element.111.kh_ref, ...), custom_call_target="tpu_custom_call" | custom-call | flops 1 | bytes 1 | tf_op jit(solution)/shard_map/pull_near/pallas_call | solution.py:1305
  85.3 1.4 %collective-permute-start.26 = (bf16[2,64,1152]{2,1,0:T(8,128)(2,1)S(1)}, bf16[2,64,1152]{2,1,0:T(8,128)(2,1)S(1)}, u32[]{:S(2)}, u32[]{:S(2)}) collective-permute-start(bf16[2,64,1152]{2,1,0:T(8,128)(2,1)S(1)} %get-tuple-element.171), channel_id=1, source_target_pairs={{0,16},{4,20},{8,24},{12,28},{16,0},{20,4},{24,8},{28,12},{1,17},{... | collective-permute-start | bytes 884744 | tf_op jit(solution)/shard_map/ppermute | solution.py:1566
  86.7 1.5 %collective-permute-start.25 = (bf16[2,64,1152]{2,1,0:T(8,128)(2,1)S(1)}, bf16[2,64,1152]{2,1,0:T(8,128)(2,1)S(1)}, u32[]{:S(2)}, u32[]{:S(2)}) collective-permute-start(bf16[2,64,1152]{2,1,0:T(8,128)(2,1)S(1)} %get-tuple-element.172), channel_id=1, source_target_pairs={{0,8},{4,12},{8,0},{12,4},{16,24},{20,28},{24,16},{28,20},{1,9},{5... | collective-permute-start | bytes 884744 | tf_op jit(solution)/shard_map/ppermute | solution.py:1566
  88.2 4.4 %pull_near.3 = (bf16[512,512]{1,0:T(8,128)(2,1)S(1)}, bf16[512,256]{1,0:T(8,128)(2,1)S(1)}, f32[512,512]{1,0:T(8,128)S(1)}) custom-call(bf16[512,1024]{1,0:T(8,128)(2,1)S(1)} %get-tuple-element.129.q_ref, bf16[768,1024]{1,0:T(8,128)(2,1)S(1)} %get-tuple-element.122.g_ref.go_ref, bf16[512,1024]{1,0:T(8,128)(2,1)S(1)} %get-tuple-element.111.kh_ref, ...), custom_call_target="tpu_custom_call" | custom-call | flops 1 | bytes 1 | tf_op jit(solution)/shard_map/pull_near/pallas_call | solution.py:1305
  93.4 1.3 collective-permute-start.27
  95.9 1.6 %collective-permute-start.35 = (bf16[4,64,1152]{2,1,0:T(8,128)(2,1)S(1)}, bf16[4,64,1152]{2,1,0:T(8,128)(2,1)S(1)}, u32[]{:S(2)}, u32[]{:S(2)}) collective-permute-start(bf16[4,64,1152]{2,1,0:T(8,128)(2,1)S(1)} %pad_maximum_fusion.1), channel_id=1, source_target_pairs={{0,8},{4,12},{8,0},{12,4},{16,24},{20,28},{24,16},{28,20},{1,9},{5... | collective-permute-start | bytes 1769480 | tf_op jit(solution)/shard_map/ppermute | solution.py:1566
  98.4 4.4 %pull_far.1.g_ref = bf16[768,1536]{1,0:T(8,128)(2,1)S(1)} custom-call(bf16[256,1024]{1,0:T(8,128)(2,1)S(1)} %get-tuple-element.135.q_ref, bf16[768,1024]{1,0:T(8,128)(2,1)S(1)} %get-tuple-element.122.g_ref.go_ref, bf16[768,1024]{1,0:T(8,128)(2,1)S(1)} %get-tuple-element.104.k_ref.ko_ref, bf16[768,1024]{1,0:T(8,128)(2,1)S(1)} %get-tuple-element.105.v_ref.vo_ref, ...), custom_call_target="tpu_custom_call" | custom-call | flops 1 | bytes 1 | tf_op jit(solution)/shard_map/pull_far/pallas_call | solution.py:1355
  102.8 4.7 %own_back.1 = (f32[768,512]{1,0:T(8,128)S(1)}, bf16[4,4,72,384]{3,2,1,0:T(8,128)(2,1)S(1)}, bf16[4,4,72,384]{3,2,1,0:T(8,128)(2,1)S(1)}) custom-call(bf16[768,512]{1,0:T(8,128)(2,1)S(1)} %copy-done, bf16[512,512]{1,0:T(8,128)(2,1)S(1)} %get-tuple-element.125.ga_ref, bf16[512,512]{1,0:T(8,128)(2,1)S(1)} %get-tuple-element.130.gb_ref, ...), custom_call_target="tpu_custom_call" | custom-call | flops 1 | bytes 1 | tf_op jit(solution)/shard_map/own_back/pallas_call | solution.py:1467
  107.5 3.7 %collective-permute-done.27.back_ref = bf16[512,512]{1,0:T(8,128)(2,1)S(1)} collective-permute-done((bf16[512,512]{1,0:T(8,128)(2,1)S(1)}, bf16[512,512]{1,0:T(8,128)(2,1)S(1)}, u32[]{:S(2)}, u32[]{:S(2)}) %collective-permute-start.27) | collective-permute-done | bytes 524320 | tf_op jit(solution)/shard_map/ppermute | solution.py:1632
  112.0 1.6 %collective-permute-done.28 = bf16[4,4,72,384]{3,2,1,0:T(8,128)(2,1)S(1)} collective-permute-done((bf16[4,4,72,384]{3,2,1,0:T(8,128)(2,1)S(1)}, bf16[4,4,72,384]{3,2,1,0:T(8,128)(2,1)S(1)}, u32[]{:S(2)}, u32[]{:S(2)}) %collective-permute-start.28) | collective-permute-done | bytes 884768 | tf_op jit(solution)/shard_map/ppermute | solution.py:1566
  114.0 1.3 collective-permute-start.29
  115.3 1.5 %collective-permute-start.31 = (bf16[4,72,384]{2,1,0:T(8,128)(2,1)S(1)}, bf16[4,72,384]{2,1,0:T(8,128)(2,1)S(1)}, u32[]{:S(2)}, u32[]{:S(2)}) collective-permute-start(bf16[4,72,384]{2,1,0:T(8,128)(2,1)S(1)} %get-tuple-element.175), channel_id=1, source_target_pairs={{0,24},{4,28},{8,16},{12,20},{16,8},{20,12},{24,0},{28,4},{1,25},{... | collective-permute-start | bytes 663560 | tf_op jit(solution)/shard_map/ppermute | solution.py:1566
  117.6 3.4 %collective-permute-start.39 = (bf16[64,1152]{1,0:T(8,128)(2,1)S(1)}, bf16[64,1152]{1,0:T(8,128)(2,1)S(1)}, u32[]{:S(2)}, u32[]{:S(2)}) collective-permute-start(bf16[64,1152]{1,0:T(8,128)(2,1)S(1)} %get-tuple-element.177), channel_id=1, source_target_pairs={{0,3},{1,0},{2,1},{3,2},{4,7},{5,4},{6,5},{7,6},{8,11},{9,8},{10,9... | collective-permute-start | bytes 442376 | tf_op jit(solution)/shard_map/ppermute | solution.py:1570
  122.3 2.5 %collective-permute-start.37 = (bf16[64,1152]{1,0:T(8,128)(2,1)S(1)}, bf16[64,1152]{1,0:T(8,128)(2,1)S(1)}, u32[]{:S(2)}, u32[]{:S(2)}) collective-permute-start(bf16[64,1152]{1,0:T(8,128)(2,1)S(1)} %get-tuple-element.179), channel_id=1, source_target_pairs={{0,1},{1,2},{2,3},{3,0},{4,5},{5,6},{6,7},{7,4},{8,9},{9,10},{10,1... | collective-permute-start | bytes 442376 | tf_op jit(solution)/shard_map/ppermute | solution.py:1570
  124.8 2.3 %collective-permute-done.31 = bf16[4,72,384]{2,1,0:T(8,128)(2,1)S(1)} collective-permute-done((bf16[4,72,384]{2,1,0:T(8,128)(2,1)S(1)}, bf16[4,72,384]{2,1,0:T(8,128)(2,1)S(1)}, u32[]{:S(2)}, u32[]{:S(2)}) %collective-permute-start.31) | collective-permute-done | bytes 221216 | tf_op jit(solution)/shard_map/ppermute | solution.py:1566
  127.1 1.4 collective-permute-done.30
  129.6 2.2 %collective-permute-start.33 = (bf16[72,384]{1,0:T(8,128)(2,1)S(1)}, bf16[72,384]{1,0:T(8,128)(2,1)S(1)}, u32[]{:S(2)}, u32[]{:S(2)}) collective-permute-start(bf16[72,384]{1,0:T(8,128)(2,1)S(1)} %get-tuple-element.181), channel_id=1, source_target_pairs={{0,2},{1,3},{2,0},{3,1},{4,6},{5,7},{6,4},{7,5},{8,10},{9,11},{10,... | collective-permute-start | bytes 165896 | tf_op jit(solution)/shard_map/ppermute | solution.py:1570
  133.1 3.0 %close.1 = f32[768,512]{1,0:T(8,128)} custom-call(bf16[768,512]{1,0:T(8,128)(2,1)S(1)} %copy-done, f32[768,512]{1,0:T(8,128)S(1)} %get-tuple-element.149.gn_ref, bf16[512,512]{1,0:T(8,128)(2,1)S(1)} %collective-permute-done.27.back_ref, f32[768,512]{1,0:T(8,128)S(1)} %get-tuple-element.150.gh_ref, f32[8,512]{1,0:T(8,128)S(1)} %get-tuple-element.109.vec_ref), custom_call_target="tpu_custom_call" | custom-call | flops 1 | bytes 1 | tf_op jit(solution)/shard_map/close/pallas_call | solution.py:1499
  (115 shorter events, 30.4 us)
Async XLA Ops:
  2.5 11.9 %collective-permute-start.5 = (bf16[72,384]{1,0:T(8,128)(2,1)}, bf16[72,384]{1,0:T(8,128)(2,1)S(1)}, u32[]{:S(2)}, u32[]{:S(2)}) collective-permute-start(bf16[72,384]{1,0:T(8,128)(2,1)} %get-tuple-element.94), channel_id=1, source_target_pairs={{0,3},{1,0},{2,1},{3,2},{4,7},{5,4},{6,5},{7,6},{8,11},{9,8},{10,9... | collective-permute-start | bytes 165896 | tf_op jit(solution)/shard_map/ppermute | solution.py:1570
  7.6 6.8 %collective-permute-start.4 = (bf16[72,384]{1,0:T(8,128)(2,1)}, bf16[72,384]{1,0:T(8,128)(2,1)S(1)}, u32[]{:S(2)}, u32[]{:S(2)}) collective-permute-start(bf16[72,384]{1,0:T(8,128)(2,1)} %get-tuple-element.94), channel_id=1, source_target_pairs={{0,2},{1,3},{2,0},{3,1},{4,6},{5,7},{6,4},{7,5},{8,10},{9,11},{10,... | collective-permute-start | bytes 165896 | tf_op jit(solution)/shard_map/ppermute | solution.py:1570
  7.6 6.8 %collective-permute-start.3 = (bf16[72,384]{1,0:T(8,128)(2,1)}, bf16[72,384]{1,0:T(8,128)(2,1)S(1)}, u32[]{:S(2)}, u32[]{:S(2)}) collective-permute-start(bf16[72,384]{1,0:T(8,128)(2,1)} %get-tuple-element.94), channel_id=1, source_target_pairs={{0,1},{1,2},{2,3},{3,0},{4,5},{5,6},{6,7},{7,4},{8,9},{9,10},{10,1... | collective-permute-start | bytes 165896 | tf_op jit(solution)/shard_map/ppermute | solution.py:1570
  8.7 10.5 %collective-permute-start.2 = (bf16[64,1152]{1,0:T(8,128)(2,1)}, bf16[64,1152]{1,0:T(8,128)(2,1)S(1)}, u32[]{:S(2)}, u32[]{:S(2)}) collective-permute-start(bf16[64,1152]{1,0:T(8,128)(2,1)} %get-tuple-element.97), channel_id=1, source_target_pairs={{0,3},{1,0},{2,1},{3,2},{4,7},{5,4},{6,5},{7,6},{8,11},{9,8},{10,9... | collective-permute-start | bytes 442376 | tf_op jit(solution)/shard_map/ppermute | solution.py:1570
  11.5 14.7 %collective-permute-start.1 = (bf16[64,1152]{1,0:T(8,128)(2,1)}, bf16[64,1152]{1,0:T(8,128)(2,1)S(1)}, u32[]{:S(2)}, u32[]{:S(2)}) collective-permute-start(bf16[64,1152]{1,0:T(8,128)(2,1)} %get-tuple-element.97), channel_id=1, source_target_pairs={{0,2},{1,3},{2,0},{3,1},{4,6},{5,7},{6,4},{7,5},{8,10},{9,11},{10,... | collective-permute-start | bytes 442376 | tf_op jit(solution)/shard_map/ppermute | solution.py:1570
  14.5 11.8 %collective-permute-start = (bf16[64,1152]{1,0:T(8,128)(2,1)}, bf16[64,1152]{1,0:T(8,128)(2,1)S(1)}, u32[]{:S(2)}, u32[]{:S(2)}) collective-permute-start(bf16[64,1152]{1,0:T(8,128)(2,1)} %get-tuple-element.97), channel_id=1, source_target_pairs={{0,1},{1,2},{2,3},{3,0},{4,5},{5,6},{6,7},{7,4},{8,9},{9,10},{10,1... | collective-permute-start | bytes 442376 | tf_op jit(solution)/shard_map/ppermute | solution.py:1570
  16.2 12.7 %collective-permute-start.10 = (bf16[4,72,384]{2,1,0:T(8,128)(2,1)S(1)}, bf16[4,72,384]{2,1,0:T(8,128)(2,1)S(1)}, u32[]{:S(2)}, u32[]{:S(2)}) collective-permute-start(bf16[4,72,384]{2,1,0:T(8,128)(2,1)S(1)} %pad_maximum_fusion.3.p0), channel_id=1, source_target_pairs={{0,24},{4,28},{8,16},{12,20},{16,8},{20,12},{24,0},{28,4},{1,25},{... | collective-permute-start | bytes 663560 | tf_op jit(solution)/shard_map/ppermute | solution.py:1566
  18.7 10.2 %collective-permute-start.9 = (bf16[4,72,384]{2,1,0:T(8,128)(2,1)S(1)}, bf16[4,72,384]{2,1,0:T(8,128)(2,1)}, u32[]{:S(2)}, u32[]{:S(2)}) collective-permute-start(bf16[4,72,384]{2,1,0:T(8,128)(2,1)S(1)} %pad_maximum_fusion.3.p0), channel_id=1, source_target_pairs={{0,16},{4,20},{8,24},{12,28},{16,0},{20,4},{24,8},{28,12},{1,17},{... | collective-permute-start | bytes 663560 | tf_op jit(solution)/shard_map/ppermute | solution.py:1566
  19.2 9.6 %collective-permute-start.8 = (bf16[4,72,384]{2,1,0:T(8,128)(2,1)S(1)}, bf16[4,72,384]{2,1,0:T(8,128)(2,1)}, u32[]{:S(2)}, u32[]{:S(2)}) collective-permute-start(bf16[4,72,384]{2,1,0:T(8,128)(2,1)S(1)} %pad_maximum_fusion.3.p0), channel_id=1, source_target_pairs={{0,8},{4,12},{8,0},{12,4},{16,24},{20,28},{24,16},{28,20},{1,9},{5... | collective-permute-start | bytes 663560 | tf_op jit(solution)/shard_map/ppermute | solution.py:1566
  29.0 7.7 %collective-permute-start.11 = (bf16[4,64,1152]{2,1,0:T(8,128)(2,1)S(1)}, bf16[4,64,1152]{2,1,0:T(8,128)(2,1)S(1)}, u32[]{:S(2)}, u32[]{:S(2)}) collective-permute-start(bf16[4,64,1152]{2,1,0:T(8,128)(2,1)S(1)} %pad_maximum_fusion.rest_0_), channel_id=1, source_target_pairs={{0,4},{4,0},{8,12},{12,8},{16,20},{20,16},{24,28},{28,24},{1,5},{5... | collective-permute-start | bytes 1769480 | tf_op jit(solution)/shard_map/ppermute | solution.py:1566
  29.2 19.7 %collective-permute-start.17 = (bf16[4,64,1152]{2,1,0:T(8,128)(2,1)S(1)}, bf16[4,64,1152]{2,1,0:T(8,128)(2,1)S(1)}, u32[]{:S(2)}, u32[]{:S(2)}) collective-permute-start(bf16[4,64,1152]{2,1,0:T(8,128)(2,1)S(1)} %pad_maximum_fusion.rest_0_), channel_id=1, source_target_pairs={{0,16},{4,20},{8,24},{12,28},{16,0},{20,4},{24,8},{28,12},{1,17},{... | collective-permute-start | bytes 1769480 | tf_op jit(solution)/shard_map/ppermute | solution.py:1566
  30.7 18.2 %collective-permute-start.16 = (bf16[4,64,1152]{2,1,0:T(8,128)(2,1)S(1)}, bf16[4,64,1152]{2,1,0:T(8,128)(2,1)S(1)}, u32[]{:S(2)}, u32[]{:S(2)}) collective-permute-start(bf16[4,64,1152]{2,1,0:T(8,128)(2,1)S(1)} %pad_maximum_fusion.rest_0_), channel_id=1, source_target_pairs={{0,8},{4,12},{8,0},{12,4},{16,24},{20,28},{24,16},{28,20},{1,9},{5... | collective-permute-start | bytes 1769480 | tf_op jit(solution)/shard_map/ppermute | solution.py:1566
  32.2 18.4 %collective-permute-start.15 = (bf16[512,512]{1,0:T(8,128)(2,1)}, bf16[512,512]{1,0:T(8,128)(2,1)S(1)}, u32[]{:S(2)}, u32[]{:S(2)}) collective-permute-start(bf16[512,512]{1,0:T(8,128)(2,1)} %slice.60), channel_id=1, source_target_pairs={{0,1},{1,2},{2,3},{4,5},{5,6},{6,7},{8,9},{9,10},{10,11},{12,13},{... | collective-permute-start | bytes 1572872 | tf_op jit(solution)/shard_map/ppermute | solution.py:1603
  49.0 9.3 %collective-permute-start.18 = (bf16[2,64,1152]{2,1,0:T(8,128)(2,1)S(1)}, bf16[2,64,1152]{2,1,0:T(8,128)(2,1)S(1)}, u32[]{:S(2)}, u32[]{:S(2)}) collective-permute-start(bf16[2,64,1152]{2,1,0:T(8,128)(2,1)S(1)} %slice.61), channel_id=1, source_target_pairs={{0,8},{4,12},{8,0},{12,4},{16,24},{20,28},{24,16},{28,20},{1,9},{5... | collective-permute-start | bytes 884744 | tf_op jit(solution)/shard_map/ppermute | solution.py:1566
  49.6 8.9 %collective-permute-start.19 = (bf16[2,64,1152]{2,1,0:T(8,128)(2,1)S(1)}, bf16[2,64,1152]{2,1,0:T(8,128)(2,1)S(1)}, u32[]{:S(2)}, u32[]{:S(2)}) collective-permute-start(bf16[2,64,1152]{2,1,0:T(8,128)(2,1)S(1)} %slice.62), channel_id=1, source_target_pairs={{0,16},{4,20},{8,24},{12,28},{16,0},{20,4},{24,8},{28,12},{1,17},{... | collective-permute-start | bytes 884744 | tf_op jit(solution)/shard_map/ppermute | solution.py:1566
  50.1 9.1 %collective-permute-start.20 = (bf16[4,64,1152]{2,1,0:T(8,128)(2,1)S(1)}, bf16[4,64,1152]{2,1,0:T(8,128)(2,1)S(1)}, u32[]{:S(2)}, u32[]{:S(2)}) collective-permute-start(bf16[4,64,1152]{2,1,0:T(8,128)(2,1)S(1)} %collective-permute-done.16.rest_1_), channel_id=1, source_target_pairs={{0,4},{4,0},{8,12},{12,8},{16,20},{20,16},{24,28},{28,24},{1,5},{5... | collective-permute-start | bytes 1769480 | tf_op jit(solution)/shard_map/ppermute | solution.py:1566
  50.1 9.1 %collective-permute-start.21 = (bf16[4,64,1152]{2,1,0:T(8,128)(2,1)S(1)}, bf16[4,64,1152]{2,1,0:T(8,128)(2,1)S(1)}, u32[]{:S(2)}, u32[]{:S(2)}) collective-permute-start(bf16[4,64,1152]{2,1,0:T(8,128)(2,1)S(1)} %collective-permute-done.17.rest_2_), channel_id=1, source_target_pairs={{0,4},{4,0},{8,12},{12,8},{16,20},{20,16},{24,28},{28,24},{1,5},{5... | collective-permute-start | bytes 1769480 | tf_op jit(solution)/shard_map/ppermute | solution.py:1566
  79.6 4.8 %collective-permute-start.24 = (bf16[4,4,64,1152]{3,2,1,0:T(8,128)(2,1)S(1)}, bf16[4,4,64,1152]{3,2,1,0:T(8,128)(2,1)S(1)}, u32[]{:S(2)}, u32[]{:S(2)}) collective-permute-start(bf16[4,4,64,1152]{3,2,1,0:T(8,128)(2,1)S(1)} %get-tuple-element.128), channel_id=1, source_target_pairs={{0,4},{4,0},{8,12},{12,8},{16,20},{20,16},{24,28},{28,24},{1,5},{5... | collective-permute-start | bytes 7077896 | tf_op jit(solution)/shard_map/ppermute | solution.py:1566
  85.3 9.4 %collective-permute-start.26 = (bf16[2,64,1152]{2,1,0:T(8,128)(2,1)S(1)}, bf16[2,64,1152]{2,1,0:T(8,128)(2,1)S(1)}, u32[]{:S(2)}, u32[]{:S(2)}) collective-permute-start(bf16[2,64,1152]{2,1,0:T(8,128)(2,1)S(1)} %get-tuple-element.171), channel_id=1, source_target_pairs={{0,16},{4,20},{8,24},{12,28},{16,0},{20,4},{24,8},{28,12},{1,17},{... | collective-permute-start | bytes 884744 | tf_op jit(solution)/shard_map/ppermute | solution.py:1566
  86.7 9.0 %collective-permute-start.25 = (bf16[2,64,1152]{2,1,0:T(8,128)(2,1)S(1)}, bf16[2,64,1152]{2,1,0:T(8,128)(2,1)S(1)}, u32[]{:S(2)}, u32[]{:S(2)}) collective-permute-start(bf16[2,64,1152]{2,1,0:T(8,128)(2,1)S(1)} %get-tuple-element.172), channel_id=1, source_target_pairs={{0,8},{4,12},{8,0},{12,4},{16,24},{20,28},{24,16},{28,20},{1,9},{5... | collective-permute-start | bytes 884744 | tf_op jit(solution)/shard_map/ppermute | solution.py:1566
  93.4 17.8 %collective-permute-start.27 = (bf16[512,512]{1,0:T(8,128)(2,1)S(1)}, bf16[512,512]{1,0:T(8,128)(2,1)S(1)}, u32[]{:S(2)}, u32[]{:S(2)}) collective-permute-start(bf16[512,512]{1,0:T(8,128)(2,1)S(1)} %get-tuple-element.132), channel_id=1, source_target_pairs={{1,0},{2,1},{3,2},{5,4},{6,5},{7,6},{9,8},{10,9},{11,10},{13,12},{... | collective-permute-start | bytes 1572872 | tf_op jit(solution)/shard_map/ppermute | solution.py:1632
  95.9 15.3 %collective-permute-start.35 = (bf16[4,64,1152]{2,1,0:T(8,128)(2,1)S(1)}, bf16[4,64,1152]{2,1,0:T(8,128)(2,1)S(1)}, u32[]{:S(2)}, u32[]{:S(2)}) collective-permute-start(bf16[4,64,1152]{2,1,0:T(8,128)(2,1)S(1)} %pad_maximum_fusion.1), channel_id=1, source_target_pairs={{0,8},{4,12},{8,0},{12,4},{16,24},{20,28},{24,16},{28,20},{1,9},{5... | collective-permute-start | bytes 1769480 | tf_op jit(solution)/shard_map/ppermute | solution.py:1566
  97.6 14.3 %collective-permute-start.36 = (bf16[4,64,1152]{2,1,0:T(8,128)(2,1)S(1)}, bf16[4,64,1152]{2,1,0:T(8,128)(2,1)S(1)}, u32[]{:S(2)}, u32[]{:S(2)}) collective-permute-start(bf16[4,64,1152]{2,1,0:T(8,128)(2,1)S(1)} %pad_maximum_fusion.2), channel_id=1, source_target_pairs={{0,16},{4,20},{8,24},{12,28},{16,0},{20,4},{24,8},{28,12},{1,17},{... | collective-permute-start | bytes 1769480 | tf_op jit(solution)/shard_map/ppermute | solution.py:1566
  114.0 8.3 %collective-permute-start.29 = (bf16[4,72,384]{2,1,0:T(8,128)(2,1)S(1)}, bf16[4,72,384]{2,1,0:T(8,128)(2,1)S(1)}, u32[]{:S(2)}, u32[]{:S(2)}) collective-permute-start(bf16[4,72,384]{2,1,0:T(8,128)(2,1)S(1)} %get-tuple-element.174), channel_id=1, source_target_pairs={{0,8},{4,12},{8,0},{12,4},{16,24},{20,28},{24,16},{28,20},{1,9},{5... | collective-permute-start | bytes 663560 | tf_op jit(solution)/shard_map/ppermute | solution.py:1566
  115.3 11.8 %collective-permute-start.31 = (bf16[4,72,384]{2,1,0:T(8,128)(2,1)S(1)}, bf16[4,72,384]{2,1,0:T(8,128)(2,1)S(1)}, u32[]{:S(2)}, u32[]{:S(2)}) collective-permute-start(bf16[4,72,384]{2,1,0:T(8,128)(2,1)S(1)} %get-tuple-element.175), channel_id=1, source_target_pairs={{0,24},{4,28},{8,16},{12,20},{16,8},{20,12},{24,0},{28,4},{1,25},{... | collective-permute-start | bytes 663560 | tf_op jit(solution)/shard_map/ppermute | solution.py:1566
  116.8 11.6 %collective-permute-start.30 = (bf16[4,72,384]{2,1,0:T(8,128)(2,1)S(1)}, bf16[4,72,384]{2,1,0:T(8,128)(2,1)S(1)}, u32[]{:S(2)}, u32[]{:S(2)}) collective-permute-start(bf16[4,72,384]{2,1,0:T(8,128)(2,1)S(1)} %get-tuple-element.176), channel_id=1, source_target_pairs={{0,16},{4,20},{8,24},{12,28},{16,0},{20,4},{24,8},{28,12},{1,17},{... | collective-permute-start | bytes 663560 | tf_op jit(solution)/shard_map/ppermute | solution.py:1566
  117.6 14.3 %collective-permute-start.39 = (bf16[64,1152]{1,0:T(8,128)(2,1)S(1)}, bf16[64,1152]{1,0:T(8,128)(2,1)S(1)}, u32[]{:S(2)}, u32[]{:S(2)}) collective-permute-start(bf16[64,1152]{1,0:T(8,128)(2,1)S(1)} %get-tuple-element.177), channel_id=1, source_target_pairs={{0,3},{1,0},{2,1},{3,2},{4,7},{5,4},{6,5},{7,6},{8,11},{9,8},{10,9... | collective-permute-start | bytes 442376 | tf_op jit(solution)/shard_map/ppermute | solution.py:1570
  120.9 15.4 %collective-permute-start.38 = (bf16[64,1152]{1,0:T(8,128)(2,1)S(1)}, bf16[64,1152]{1,0:T(8,128)(2,1)S(1)}, u32[]{:S(2)}, u32[]{:S(2)}) collective-permute-start(bf16[64,1152]{1,0:T(8,128)(2,1)S(1)} %get-tuple-element.178), channel_id=1, source_target_pairs={{0,2},{1,3},{2,0},{3,1},{4,6},{5,7},{6,4},{7,5},{8,10},{9,11},{10,... | collective-permute-start | bytes 442376 | tf_op jit(solution)/shard_map/ppermute | solution.py:1570
  122.3 14.0 %collective-permute-start.37 = (bf16[64,1152]{1,0:T(8,128)(2,1)S(1)}, bf16[64,1152]{1,0:T(8,128)(2,1)S(1)}, u32[]{:S(2)}, u32[]{:S(2)}) collective-permute-start(bf16[64,1152]{1,0:T(8,128)(2,1)S(1)} %get-tuple-element.179), channel_id=1, source_target_pairs={{0,1},{1,2},{2,3},{3,0},{4,5},{5,6},{6,7},{7,4},{8,9},{9,10},{10,1... | collective-permute-start | bytes 442376 | tf_op jit(solution)/shard_map/ppermute | solution.py:1570
  128.6 8.5 %collective-permute-start.34 = (bf16[72,384]{1,0:T(8,128)(2,1)S(1)}, bf16[72,384]{1,0:T(8,128)(2,1)S(1)}, u32[]{:S(2)}, u32[]{:S(2)}) collective-permute-start(bf16[72,384]{1,0:T(8,128)(2,1)S(1)} %get-tuple-element.180), channel_id=1, source_target_pairs={{0,3},{1,0},{2,1},{3,2},{4,7},{5,4},{6,5},{7,6},{8,11},{9,8},{10,9... | collective-permute-start | bytes 165896 | tf_op jit(solution)/shard_map/ppermute | solution.py:1570
  129.6 8.4 %collective-permute-start.33 = (bf16[72,384]{1,0:T(8,128)(2,1)S(1)}, bf16[72,384]{1,0:T(8,128)(2,1)S(1)}, u32[]{:S(2)}, u32[]{:S(2)}) collective-permute-start(bf16[72,384]{1,0:T(8,128)(2,1)S(1)} %get-tuple-element.181), channel_id=1, source_target_pairs={{0,2},{1,3},{2,0},{3,1},{4,6},{5,7},{6,4},{7,5},{8,10},{9,11},{10,... | collective-permute-start | bytes 165896 | tf_op jit(solution)/shard_map/ppermute | solution.py:1570
  131.8 6.2 %collective-permute-start.32 = (bf16[72,384]{1,0:T(8,128)(2,1)S(1)}, bf16[72,384]{1,0:T(8,128)(2,1)S(1)}, u32[]{:S(2)}, u32[]{:S(2)}) collective-permute-start(bf16[72,384]{1,0:T(8,128)(2,1)S(1)} %get-tuple-element.182), channel_id=1, source_target_pairs={{0,1},{1,2},{2,3},{3,0},{4,5},{5,6},{6,7},{7,4},{8,9},{9,10},{10,1... | collective-permute-start | bytes 165896 | tf_op jit(solution)/shard_map/ppermute | solution.py:1570
  (22 other events, 149.0 us)

commit v2 on v1

--- a/solution.py
+++ b/solution.py
@@ -615,7 +615,7 @@
 WF = COLS + 2 * FFC
 TALL = D + 16
 ALL = (0, 1, 2, 3)
-PIECES_A = ((0, ALL), (2, ALL), (4, ALL), (6, ALL), (1, ALL[0:2]), (1, ALL[2:4]), (3, ALL), (5, ALL), (7, ALL))
+PIECES_A = ((0, ALL), (2, ALL), (4, ALL), (6, ALL), (1, ALL), (3, ALL), (5, ALL), (7, ALL))
 SMALL = pl.CostEstimate(flops=1, bytes_accessed=1, transcendentals=0)
 
 
@@ -686,11 +686,11 @@
 
 
 def project_kernel(
-    tokens_all, x_ref, idc_ref, p0, p1, p2, p3, p4, p5, p6, p7, p8,
+    tokens_all, x_ref, idc_ref, p0, p1, p2, p3, p4,
     q_ref, k_ref, v_ref, kt_ref, nt_ref, w_ref, vec_ref, bup_ref, scale_ref, head_ref, ext_ref, n_ref, sem
 ):
     me, place = lax.axis_index("fsdp"), lax.axis_index("tp")
-    pieces = (p0, p1, p2, p3, p4, p5, p6, p7, p8)
+    pieces = (p0, p1, p2, p3) + tuple(p4.at[4 * i : 4 * i + 4] for i in range(4))
 
     def each(act):
         for ref, (mask, steps) in zip(pieces, PIECES_A):
@@ -823,7 +823,7 @@
     return pl.pallas_call(
         functools.partial(project_kernel, float(tokens_all)),
         out_shape=shapes,
-        in_specs=[VMEM, VMEM] + [FAR] * 9,
+        in_specs=[VMEM, VMEM] + [FAR] * 5,
         out_specs=[VMEM] * len(shapes),
         scratch_shapes=[pltpu.VMEM((32, EXTRA, WA), BF16), pltpu.VMEM((own, D), BF16), pltpu.SemaphoreType.DMA((2,))],
         compiler_params=params(6),
@@ -911,7 +911,7 @@
             q = jnp.where((at == DOCS + i) & ~mine, jnp.broadcast_to(term, q.shape), q)
         one["take"](one["h"], (total / weight).astype(BF16), q)
 
-    staged(heads, (score, soften, attend), 2)
+    staged(heads, (score, soften, attend), 3)
 
 
 def keep_attended(o_ref, qa_ref, rows, pair):
@@ -1599,7 +1599,7 @@
     over_a = [to_mask(a, 1) for a in halves_a]
     line_f = jnp.stack(after(steps_f, (over_a, near_a)))
     over_f = to_mask(line_f, 1)
-    pieces_a = [line_a] + near_a + over_a + [to_mask(a, 1) for a in near_a]
+    pieces_a = [line_a] + near_a + [jnp.concatenate(over_a + [to_mask(a, 1) for a in near_a])]
     halo = lax.ppermute(last_rows, "tp", [(i, i + 1) for i in range(3)])
     f_x, f_y = to_mask(line_f, 2), to_mask(line_f, 4)
 
@@ -1701,5 +1701,11 @@
         rows,
     )
     sizes = (mesh.shape["fsdp"], mesh.shape["tp"])
-    body = local_fast if sizes == (8, 4) else local
+
+    def body(*args):
+        x, ids, w_q, w_up = args[0], args[1], args[7], args[16]
+        fits = x.shape[0] == HALO + QB and 16 * ids.shape[0] <= DOCS
+        fits = fits and w_q.shape == (ROWS, COLS) and w_up.shape == (ROWS, FFC)
+        return (local_fast if fits and sizes == (8, 4) else local)(*args)
+
     return jax.shard_map(body, mesh=mesh, in_specs=placed, out_specs=given, check_vma=False)

time: 139 us -> 139 us (level)
  local copies, waits for them, and re-layouts: 8.18 us -> 1.99 us
  waiting for transfers between devices: 22.7 us -> 26 us
  starting transfers between devices: 44.7 us -> 47.4 us
    unnamed x28 -> x16, local copies, waits for them, and re-layouts: 5.57 us -> 0.14 us
    ppermute x1, waiting for transfers between devices: 0.01 us -> 2.37 us  [local_fast(): halo = lax.ppermute(last_rows, 'tp', [(i, i + 1) for i in range(3)])]
    ppermute x12, starting transfers between devices: 21 us -> 23.3 us  [to_step(): return lax.ppermute(x, 'tp', [(i, (i + step) % 4) for i in range(4)])]
  transfers between devices with their start and end apart: 40 -> 40, of which waited for: 17 -> 18; matrix products, arithmetic and copies ran while one was open for 3% -> 3% of each run, Pallas kernels for 27% -> 26%
where the time goes in v2:
time: 139 us; the launch traced here: 138 us
  Pallas kernels  58.1 us (42%)
  starting transfers between devices  47.4 us (34%)
  waiting for transfers between devices  26 us (19%)
  other arithmetic  3.44 us (2%)
  local copies, waits for them, and re-layouts  1.99 us (1%)
    ppermute x12, starting transfers between devices, to_step(): return lax.ppermute(x, 'tp', [(i, (i + step) % 4) for i in range(4)])  23.3 us
    pallas_call x1, Pallas kernels, central(): pl.pallas_call(functools.partial(central_kernel, rb), out_shape=shapes, i...  19.2 us
    ppermute x26, starting transfers between devices, to_mask(): return lax.ppermute(x, 'fsdp', [(i, i ^ mask) for i in range(8)])  18 us
    ppermute x26, waiting for transfers between devices, to_mask(): return lax.ppermute(x, 'fsdp', [(i, i ^ mask) for i in range(8)])  11.4 us
    pallas_call x2, Pallas kernels, pull_near(): pl.pallas_call(functools.partial(pull_near_kernel, base), out_shape=(jax....  9.03 us
    ppermute x12, waiting for transfers between devices, to_step(): return lax.ppermute(x, 'tp', [(i, (i + step) % 4) for i in range(4)])  8.48 us
    pallas_call x1, Pallas kernels, attend_near(): pl.pallas_call(attend_near_kernel, out_shape=(jax.ShapeDtypeStruct((HALO,...  5.96 us
    ppermute x1, starting transfers between devices, local_fast(): halo = lax.ppermute(last_rows, 'tp', [(i, i + 1) for i in range(3)])  4.8 us
  transfers between devices with their start and end apart: 40, of which 18 were waited for; matrix products, arithmetic and copies ran while one was open for 3% of the time, Pallas kernels for 26%

profile of v2, /device:TPU:0, one launch (start us, length us, event | category | flops | bytes accessed | tf_op | source)
XLA Modules:
  0.0 138.2 jit_solution(12891042153037268244)
XLA Ops:
  0.7 1.9 %pack_weights.1 = (bf16[72,384]{1,0:T(8,128)(2,1)}, bf16[64,1152]{1,0:T(8,128)(2,1)}) custom-call(bf16[64,128]{1,0:T(8,128)(2,1)} %wq_ref.1, bf16[64,128]{1,0:T(8,128)(2,1)} %wk_ref.1, bf16[64,128]{1,0:T(8,128)(2,1)} %wv_ref.1, bf16[64,128]{1,0:T(8,128)(2,1)} %bitcast.72, bf16[64,512]{1,0:T(8,128)(2,1)} %wup_ref.1, bf16[64,512]{1,0:T(8,128)(2,1)} %bitcast.71, ...), custom_call_target="tpu_custom_call" | custom-call | tf_op jit(solution)/shard_map/pack_weights/pallas_call | solution.py:677
  2.5 5.1 %collective-permute-start.5 = (bf16[72,384]{1,0:T(8,128)(2,1)}, bf16[72,384]{1,0:T(8,128)(2,1)S(1)}, u32[]{:S(2)}, u32[]{:S(2)}) collective-permute-start(bf16[72,384]{1,0:T(8,128)(2,1)} %get-tuple-element.94), channel_id=1, source_target_pairs={{0,3},{1,0},{2,1},{3,2},{4,7},{5,4},{6,5},{7,6},{8,11},{9,8},{10,9... | collective-permute-start | bytes 165896 | tf_op jit(solution)/shard_map/ppermute | solution.py:1570
  8.6 2.8 %collective-permute-start.2 = (bf16[64,1152]{1,0:T(8,128)(2,1)}, bf16[64,1152]{1,0:T(8,128)(2,1)S(1)}, u32[]{:S(2)}, u32[]{:S(2)}) collective-permute-start(bf16[64,1152]{1,0:T(8,128)(2,1)} %get-tuple-element.97), channel_id=1, source_target_pairs={{0,3},{1,0},{2,1},{3,2},{4,7},{5,4},{6,5},{7,6},{8,11},{9,8},{10,9... | collective-permute-start | bytes 442376 | tf_op jit(solution)/shard_map/ppermute | solution.py:1570
  16.1 2.5 %collective-permute-start.10 = (bf16[4,72,384]{2,1,0:T(8,128)(2,1)S(1)}, bf16[4,72,384]{2,1,0:T(8,128)(2,1)S(1)}, u32[]{:S(2)}, u32[]{:S(2)}) collective-permute-start(bf16[4,72,384]{2,1,0:T(8,128)(2,1)S(1)} %pad_maximum_fusion.3.p0), channel_id=1, source_target_pairs={{0,24},{4,28},{8,16},{12,20},{16,8},{20,12},{24,0},{28,4},{1,25},{... | collective-permute-start | bytes 663560 | tf_op jit(solution)/shard_map/ppermute | solution.py:1566
  19.8 6.4 %collective-permute-done.1 = bf16[64,1152]{1,0:T(8,128)(2,1)S(1)} collective-permute-done((bf16[64,1152]{1,0:T(8,128)(2,1)}, bf16[64,1152]{1,0:T(8,128)(2,1)S(1)}, u32[]{:S(2)}, u32[]{:S(2)}) %collective-permute-start.1) | collective-permute-done | bytes 147488 | tf_op jit(solution)/shard_map/ppermute | solution.py:1570
  27.8 1.6 %collective-permute-start.17 = (bf16[4,64,1152]{2,1,0:T(8,128)(2,1)S(1)}, bf16[4,64,1152]{2,1,0:T(8,128)(2,1)S(1)}, u32[]{:S(2)}, u32[]{:S(2)}) collective-permute-start(bf16[4,64,1152]{2,1,0:T(8,128)(2,1)S(1)} %pad_maximum_fusion.rest_0_), channel_id=1, source_target_pairs={{0,16},{4,20},{8,24},{12,28},{16,0},{20,4},{24,8},{28,12},{1,17},{... | collective-permute-start | bytes 1769480 | tf_op jit(solution)/shard_map/ppermute | solution.py:1566
  29.4 1.5 %collective-permute-start.16 = (bf16[4,64,1152]{2,1,0:T(8,128)(2,1)S(1)}, bf16[4,64,1152]{2,1,0:T(8,128)(2,1)S(1)}, u32[]{:S(2)}, u32[]{:S(2)}) collective-permute-start(bf16[4,64,1152]{2,1,0:T(8,128)(2,1)S(1)} %pad_maximum_fusion.rest_0_), channel_id=1, source_target_pairs={{0,8},{4,12},{8,0},{12,4},{16,24},{20,28},{24,16},{28,20},{1,9},{5... | collective-permute-start | bytes 1769480 | tf_op jit(solution)/shard_map/ppermute | solution.py:1566
  31.9 1.3 collective-permute-done.12
  33.5 4.8 %collective-permute-start.15 = (bf16[512,512]{1,0:T(8,128)(2,1)S(1)}, bf16[512,512]{1,0:T(8,128)(2,1)S(1)}, u32[]{:S(2)}, u32[]{:S(2)}) collective-permute-start(bf16[512,512]{1,0:T(8,128)(2,1)S(1)} %slice.60), channel_id=1, source_target_pairs={{0,1},{1,2},{2,3},{4,5},{5,6},{6,7},{8,9},{9,10},{10,11},{12,13},{... | collective-permute-start | bytes 1572872 | tf_op jit(solution)/shard_map/ppermute | solution.py:1603
  38.5 3.4 %project.1 = (bf16[768,1024]{1,0:T(8,128)(2,1)S(1)}, bf16[768,1024]{1,0:T(8,128)(2,1)S(1)}, bf16[768,1024]{1,0:T(8,128)(2,1)S(1)}, bf16[512,768]{1,0:T(8,128)(2,...) custom-call(bf16[768,512]{1,0:T(8,128)(2,1)S(1)} %copy-done, ...), custom_call_target="tpu_custom_call" | custom-call | flops 1 | bytes 1 | tf_op jit(solution)/shard_map/project/pallas_call | solution.py:823
  41.9 3.0 %attend_far.1 = (bf16[256,512]{1,0:T(8,128)(2,1)S(1)}, bf16[256,1024]{1,0:T(8,128)(2,1)S(1)}) custom-call(bf16[768,1024]{1,0:T(8,128)(2,1)S(1)} %get-tuple-element.102.q_ref, bf16[768,1024]{1,0:T(8,128)(2,1)S(1)} %get-tuple-element.104.k_ref.ko_ref, bf16[768,1024]{1,0:T(8,128)(2,1)S(1)} %get-tuple-element.105.v_ref.vo_ref), custom_call_target="tpu_custom_call" | custom-call | flops 1 | bytes 1 | tf_op jit(solution)/shard_map/attend_far/pallas_call | solution.py:958
  45.0 1.3 collective-permute-start.18
  47.4 2.4 %collective-permute-done.15.x_ref = bf16[512,512]{1,0:T(8,128)(2,1)S(1)} collective-permute-done((bf16[512,512]{1,0:T(8,128)(2,1)S(1)}, bf16[512,512]{1,0:T(8,128)(2,1)S(1)}, u32[]{:S(2)}, u32[]{:S(2)}) %collective-permute-start.15) | collective-permute-done | bytes 524320 | tf_op jit(solution)/shard_map/ppermute | solution.py:1603
  51.1 6.0 %attend_near.1 = (bf16[512,512]{1,0:T(8,128)(2,1)S(1)}, bf16[512,1024]{1,0:T(8,128)(2,1)S(1)}) custom-call(bf16[768,1024]{1,0:T(8,128)(2,1)S(1)} %get-tuple-element.102.q_ref, bf16[512,1024]{1,0:T(8,128)(2,1)S(1)} %get-tuple-element.111.kh_ref, bf16[768,1024]{1,0:T(8,128)(2,1)S(1)} %get-tuple-element.104.k_ref.ko_ref, ...), custom_call_target="tpu_custom_call" | custom-call | flops 1 | bytes 1 | tf_op jit(solution)/shard_map/attend_near/pallas_call | solution.py:994
  59.1 19.2 %central.1 = (bf16[768,512]{1,0:T(8,128)(2,1)}, f32[768,512]{1,0:T(8,128)S(1)}, bf16[768,1024]{1,0:T(8,128)(2,1)S(1)}, bf16[4,4,64,1152]{3,2,1,0:T(8,128)(2,1)S(...) custom-call(bf16[768,512]{1,0:T(8,128)(2,1)S(1)} %copy-done, ...), custom_call_target="tpu_custom_call" | custom-call | flops 1 | bytes 1 | tf_op jit(solution)/shard_map/central/pallas_call | solution.py:1183
  78.5 4.7 %pull_near.2 = (bf16[512,512]{1,0:T(8,128)(2,1)S(1)}, bf16[512,256]{1,0:T(8,128)(2,1)S(1)}, f32[512,512]{1,0:T(8,128)S(1)}) custom-call(bf16[512,1024]{1,0:T(8,128)(2,1)S(1)} %get-tuple-element.129.q_ref, bf16[768,1024]{1,0:T(8,128)(2,1)S(1)} %get-tuple-element.122.g_ref.go_ref, bf16[512,1024]{1,0:T(8,128)(2,1)S(1)} %get-tuple-element.111.kh_ref, ...), custom_call_target="tpu_custom_call" | custom-call | flops 1 | bytes 1 | tf_op jit(solution)/shard_map/pull_near/pallas_call | solution.py:1305
  85.1 4.4 %pull_near.3 = (bf16[512,512]{1,0:T(8,128)(2,1)S(1)}, bf16[512,256]{1,0:T(8,128)(2,1)S(1)}, f32[512,512]{1,0:T(8,128)S(1)}) custom-call(bf16[512,1024]{1,0:T(8,128)(2,1)S(1)} %get-tuple-element.129.q_ref, bf16[768,1024]{1,0:T(8,128)(2,1)S(1)} %get-tuple-element.122.g_ref.go_ref, bf16[512,1024]{1,0:T(8,128)(2,1)S(1)} %get-tuple-element.111.kh_ref, ...), custom_call_target="tpu_custom_call" | custom-call | flops 1 | bytes 1 | tf_op jit(solution)/shard_map/pull_near/pallas_call | solution.py:1305
  91.6 1.7 %collective-permute-done.26 = bf16[2,64,1152]{2,1,0:T(8,128)(2,1)S(1)} collective-permute-done((bf16[2,64,1152]{2,1,0:T(8,128)(2,1)S(1)}, bf16[2,64,1152]{2,1,0:T(8,128)(2,1)S(1)}, u32[]{:S(2)}, u32[]{:S(2)}) %collective-permute-start.26) | collective-permute-done | bytes 294944 | tf_op jit(solution)/shard_map/ppermute | solution.py:1566
  94.5 1.6 %collective-permute-start.36 = (bf16[4,64,1152]{2,1,0:T(8,128)(2,1)S(1)}, bf16[4,64,1152]{2,1,0:T(8,128)(2,1)S(1)}, u32[]{:S(2)}, u32[]{:S(2)}) collective-permute-start(bf16[4,64,1152]{2,1,0:T(8,128)(2,1)S(1)} %pad_maximum_fusion.2), channel_id=1, source_target_pairs={{0,16},{4,20},{8,24},{12,28},{16,0},{20,4},{24,8},{28,12},{1,17},{... | collective-permute-start | bytes 1769480 | tf_op jit(solution)/shard_map/ppermute | solution.py:1566
  96.1 4.4 %pull_far.1.g_ref = bf16[768,1536]{1,0:T(8,128)(2,1)S(1)} custom-call(bf16[256,1024]{1,0:T(8,128)(2,1)S(1)} %get-tuple-element.135.q_ref, bf16[768,1024]{1,0:T(8,128)(2,1)S(1)} %get-tuple-element.122.g_ref.go_ref, bf16[768,1024]{1,0:T(8,128)(2,1)S(1)} %get-tuple-element.104.k_ref.ko_ref, bf16[768,1024]{1,0:T(8,128)(2,1)S(1)} %get-tuple-element.105.v_ref.vo_ref, ...), custom_call_target="tpu_custom_call" | custom-call | flops 1 | bytes 1 | tf_op jit(solution)/shard_map/pull_far/pallas_call | solution.py:1355
  100.5 4.7 %own_back.1 = (f32[768,512]{1,0:T(8,128)S(1)}, bf16[4,4,72,384]{3,2,1,0:T(8,128)(2,1)S(1)}, bf16[4,4,72,384]{3,2,1,0:T(8,128)(2,1)S(1)}) custom-call(bf16[768,512]{1,0:T(8,128)(2,1)S(1)} %copy-done, bf16[512,512]{1,0:T(8,128)(2,1)S(1)} %get-tuple-element.125.ga_ref, bf16[512,512]{1,0:T(8,128)(2,1)S(1)} %get-tuple-element.130.gb_ref, ...), custom_call_target="tpu_custom_call" | custom-call | flops 1 | bytes 1 | tf_op jit(solution)/shard_map/own_back/pallas_call | solution.py:1467
  105.2 3.7 %collective-permute-done.27.back_ref = bf16[512,512]{1,0:T(8,128)(2,1)S(1)} collective-permute-done((bf16[512,512]{1,0:T(8,128)(2,1)S(1)}, bf16[512,512]{1,0:T(8,128)(2,1)S(1)}, u32[]{:S(2)}, u32[]{:S(2)}) %collective-permute-start.27) | collective-permute-done | bytes 524320 | tf_op jit(solution)/shard_map/ppermute | solution.py:1632
  109.2 2.2 %collective-permute-done.28 = bf16[4,4,72,384]{3,2,1,0:T(8,128)(2,1)S(1)} collective-permute-done((bf16[4,4,72,384]{3,2,1,0:T(8,128)(2,1)S(1)}, bf16[4,4,72,384]{3,2,1,0:T(8,128)(2,1)S(1)}, u32[]{:S(2)}, u32[]{:S(2)}) %collective-permute-start.28) | collective-permute-done | bytes 884768 | tf_op jit(solution)/shard_map/ppermute | solution.py:1566
  111.7 1.6 %collective-permute-start.29 = (bf16[4,72,384]{2,1,0:T(8,128)(2,1)S(1)}, bf16[4,72,384]{2,1,0:T(8,128)(2,1)S(1)}, u32[]{:S(2)}, u32[]{:S(2)}) collective-permute-start(bf16[4,72,384]{2,1,0:T(8,128)(2,1)S(1)} %get-tuple-element.174), channel_id=1, source_target_pairs={{0,8},{4,12},{8,0},{12,4},{16,24},{20,28},{24,16},{28,20},{1,9},{5... | collective-permute-start | bytes 663560 | tf_op jit(solution)/shard_map/ppermute | solution.py:1566
  113.3 1.4 %collective-permute-start.31 = (bf16[4,72,384]{2,1,0:T(8,128)(2,1)S(1)}, bf16[4,72,384]{2,1,0:T(8,128)(2,1)S(1)}, u32[]{:S(2)}, u32[]{:S(2)}) collective-permute-start(bf16[4,72,384]{2,1,0:T(8,128)(2,1)S(1)} %get-tuple-element.175), channel_id=1, source_target_pairs={{0,24},{4,28},{8,16},{12,20},{16,8},{20,12},{24,0},{28,4},{1,25},{... | collective-permute-start | bytes 663560 | tf_op jit(solution)/shard_map/ppermute | solution.py:1566
  115.3 5.9 %collective-permute-start.39 = (bf16[64,1152]{1,0:T(8,128)(2,1)S(1)}, bf16[64,1152]{1,0:T(8,128)(2,1)S(1)}, u32[]{:S(2)}, u32[]{:S(2)}) collective-permute-start(bf16[64,1152]{1,0:T(8,128)(2,1)S(1)} %get-tuple-element.177), channel_id=1, source_target_pairs={{0,3},{1,0},{2,1},{3,2},{4,7},{5,4},{6,5},{7,6},{8,11},{9,8},{10,9... | collective-permute-start | bytes 442376 | tf_op jit(solution)/shard_map/ppermute | solution.py:1570
  121.1 1.6 %collective-permute-start.37 = (bf16[64,1152]{1,0:T(8,128)(2,1)S(1)}, bf16[64,1152]{1,0:T(8,128)(2,1)S(1)}, u32[]{:S(2)}, u32[]{:S(2)}) collective-permute-start(bf16[64,1152]{1,0:T(8,128)(2,1)S(1)} %get-tuple-element.179), channel_id=1, source_target_pairs={{0,1},{1,2},{2,3},{3,0},{4,5},{5,6},{6,7},{7,4},{8,9},{9,10},{10,1... | collective-permute-start | bytes 442376 | tf_op jit(solution)/shard_map/ppermute | solution.py:1570
  122.7 2.2 %collective-permute-done.31 = bf16[4,72,384]{2,1,0:T(8,128)(2,1)S(1)} collective-permute-done((bf16[4,72,384]{2,1,0:T(8,128)(2,1)S(1)}, bf16[4,72,384]{2,1,0:T(8,128)(2,1)S(1)}, u32[]{:S(2)}, u32[]{:S(2)}) %collective-permute-start.31) | collective-permute-done | bytes 221216 | tf_op jit(solution)/shard_map/ppermute | solution.py:1566
  125.0 1.4 collective-permute-done.30
  126.5 3.4 %collective-permute-start.34 = (bf16[72,384]{1,0:T(8,128)(2,1)S(1)}, bf16[72,384]{1,0:T(8,128)(2,1)S(1)}, u32[]{:S(2)}, u32[]{:S(2)}) collective-permute-start(bf16[72,384]{1,0:T(8,128)(2,1)S(1)} %get-tuple-element.180), channel_id=1, source_target_pairs={{0,3},{1,0},{2,1},{3,2},{4,7},{5,4},{6,5},{7,6},{8,11},{9,8},{10,9... | collective-permute-start | bytes 165896 | tf_op jit(solution)/shard_map/ppermute | solution.py:1570
  130.5 1.7 %collective-permute-start.32 = (bf16[72,384]{1,0:T(8,128)(2,1)S(1)}, bf16[72,384]{1,0:T(8,128)(2,1)S(1)}, u32[]{:S(2)}, u32[]{:S(2)}) collective-permute-start(bf16[72,384]{1,0:T(8,128)(2,1)S(1)} %get-tuple-element.182), channel_id=1, source_target_pairs={{0,1},{1,2},{2,3},{3,0},{4,5},{5,6},{6,7},{7,4},{8,9},{9,10},{10,1... | collective-permute-start | bytes 165896 | tf_op jit(solution)/shard_map/ppermute | solution.py:1570
  132.2 3.0 %close.1 = f32[768,512]{1,0:T(8,128)} custom-call(bf16[768,512]{1,0:T(8,128)(2,1)S(1)} %copy-done, f32[768,512]{1,0:T(8,128)S(1)} %get-tuple-element.149.gn_ref, bf16[512,512]{1,0:T(8,128)(2,1)S(1)} %collective-permute-done.27.back_ref, f32[768,512]{1,0:T(8,128)S(1)} %get-tuple-element.150.gh_ref, f32[8,512]{1,0:T(8,128)S(1)} %get-tuple-element.109.vec_ref), custom_call_target="tpu_custom_call" | custom-call | flops 1 | bytes 1 | tf_op jit(solution)/shard_map/close/pallas_call | solution.py:1499
  (104 shorter events, 24.3 us)
Async XLA Ops:
  2.5 11.1 %collective-permute-start.5 = (bf16[72,384]{1,0:T(8,128)(2,1)}, bf16[72,384]{1,0:T(8,128)(2,1)S(1)}, u32[]{:S(2)}, u32[]{:S(2)}) collective-permute-start(bf16[72,384]{1,0:T(8,128)(2,1)} %get-tuple-element.94), channel_id=1, source_target_pairs={{0,3},{1,0},{2,1},{3,2},{4,7},{5,4},{6,5},{7,6},{8,11},{9,8},{10,9... | collective-permute-start | bytes 165896 | tf_op jit(solution)/shard_map/ppermute | solution.py:1570
  7.6 6.2 %collective-permute-start.4 = (bf16[72,384]{1,0:T(8,128)(2,1)}, bf16[72,384]{1,0:T(8,128)(2,1)S(1)}, u32[]{:S(2)}, u32[]{:S(2)}) collective-permute-start(bf16[72,384]{1,0:T(8,128)(2,1)} %get-tuple-element.94), channel_id=1, source_target_pairs={{0,2},{1,3},{2,0},{3,1},{4,6},{5,7},{6,4},{7,5},{8,10},{9,11},{10,... | collective-permute-start | bytes 165896 | tf_op jit(solution)/shard_map/ppermute | solution.py:1570
  7.6 6.8 %collective-permute-start.3 = (bf16[72,384]{1,0:T(8,128)(2,1)}, bf16[72,384]{1,0:T(8,128)(2,1)S(1)}, u32[]{:S(2)}, u32[]{:S(2)}) collective-permute-start(bf16[72,384]{1,0:T(8,128)(2,1)} %get-tuple-element.94), channel_id=1, source_target_pairs={{0,1},{1,2},{2,3},{3,0},{4,5},{5,6},{6,7},{7,4},{8,9},{9,10},{10,1... | collective-permute-start | bytes 165896 | tf_op jit(solution)/shard_map/ppermute | solution.py:1570
  8.6 10.5 %collective-permute-start.2 = (bf16[64,1152]{1,0:T(8,128)(2,1)}, bf16[64,1152]{1,0:T(8,128)(2,1)S(1)}, u32[]{:S(2)}, u32[]{:S(2)}) collective-permute-start(bf16[64,1152]{1,0:T(8,128)(2,1)} %get-tuple-element.97), channel_id=1, source_target_pairs={{0,3},{1,0},{2,1},{3,2},{4,7},{5,4},{6,5},{7,6},{8,11},{9,8},{10,9... | collective-permute-start | bytes 442376 | tf_op jit(solution)/shard_map/ppermute | solution.py:1570
  11.5 14.7 %collective-permute-start.1 = (bf16[64,1152]{1,0:T(8,128)(2,1)}, bf16[64,1152]{1,0:T(8,128)(2,1)S(1)}, u32[]{:S(2)}, u32[]{:S(2)}) collective-permute-start(bf16[64,1152]{1,0:T(8,128)(2,1)} %get-tuple-element.97), channel_id=1, source_target_pairs={{0,2},{1,3},{2,0},{3,1},{4,6},{5,7},{6,4},{7,5},{8,10},{9,11},{10,... | collective-permute-start | bytes 442376 | tf_op jit(solution)/shard_map/ppermute | solution.py:1570
  13.7 12.5 %collective-permute-start = (bf16[64,1152]{1,0:T(8,128)(2,1)}, bf16[64,1152]{1,0:T(8,128)(2,1)S(1)}, u32[]{:S(2)}, u32[]{:S(2)}) collective-permute-start(bf16[64,1152]{1,0:T(8,128)(2,1)} %get-tuple-element.97), channel_id=1, source_target_pairs={{0,1},{1,2},{2,3},{3,0},{4,5},{5,6},{6,7},{7,4},{8,9},{9,10},{10,1... | collective-permute-start | bytes 442376 | tf_op jit(solution)/shard_map/ppermute | solution.py:1570
  16.1 11.6 %collective-permute-start.10 = (bf16[4,72,384]{2,1,0:T(8,128)(2,1)S(1)}, bf16[4,72,384]{2,1,0:T(8,128)(2,1)S(1)}, u32[]{:S(2)}, u32[]{:S(2)}) collective-permute-start(bf16[4,72,384]{2,1,0:T(8,128)(2,1)S(1)} %pad_maximum_fusion.3.p0), channel_id=1, source_target_pairs={{0,24},{4,28},{8,16},{12,20},{16,8},{20,12},{24,0},{28,4},{1,25},{... | collective-permute-start | bytes 663560 | tf_op jit(solution)/shard_map/ppermute | solution.py:1566
  18.6 9.1 %collective-permute-start.9 = (bf16[4,72,384]{2,1,0:T(8,128)(2,1)S(1)}, bf16[4,72,384]{2,1,0:T(8,128)(2,1)S(1)}, u32[]{:S(2)}, u32[]{:S(2)}) collective-permute-start(bf16[4,72,384]{2,1,0:T(8,128)(2,1)S(1)} %pad_maximum_fusion.3.p0), channel_id=1, source_target_pairs={{0,16},{4,20},{8,24},{12,28},{16,0},{20,4},{24,8},{28,12},{1,17},{... | collective-permute-start | bytes 663560 | tf_op jit(solution)/shard_map/ppermute | solution.py:1566
  19.2 8.5 %collective-permute-start.8 = (bf16[4,72,384]{2,1,0:T(8,128)(2,1)S(1)}, bf16[4,72,384]{2,1,0:T(8,128)(2,1)S(1)}, u32[]{:S(2)}, u32[]{:S(2)}) collective-permute-start(bf16[4,72,384]{2,1,0:T(8,128)(2,1)S(1)} %pad_maximum_fusion.3.p0), channel_id=1, source_target_pairs={{0,8},{4,12},{8,0},{12,4},{16,24},{20,28},{24,16},{28,20},{1,9},{5... | collective-permute-start | bytes 663560 | tf_op jit(solution)/shard_map/ppermute | solution.py:1566
  27.8 17.1 %collective-permute-start.17 = (bf16[4,64,1152]{2,1,0:T(8,128)(2,1)S(1)}, bf16[4,64,1152]{2,1,0:T(8,128)(2,1)S(1)}, u32[]{:S(2)}, u32[]{:S(2)}) collective-permute-start(bf16[4,64,1152]{2,1,0:T(8,128)(2,1)S(1)} %pad_maximum_fusion.rest_0_), channel_id=1, source_target_pairs={{0,16},{4,20},{8,24},{12,28},{16,0},{20,4},{24,8},{28,12},{1,17},{... | collective-permute-start | bytes 1769480 | tf_op jit(solution)/shard_map/ppermute | solution.py:1566
  29.4 15.5 %collective-permute-start.16 = (bf16[4,64,1152]{2,1,0:T(8,128)(2,1)S(1)}, bf16[4,64,1152]{2,1,0:T(8,128)(2,1)S(1)}, u32[]{:S(2)}, u32[]{:S(2)}) collective-permute-start(bf16[4,64,1152]{2,1,0:T(8,128)(2,1)S(1)} %pad_maximum_fusion.rest_0_), channel_id=1, source_target_pairs={{0,8},{4,12},{8,0},{12,4},{16,24},{20,28},{24,16},{28,20},{1,9},{5... | collective-permute-start | bytes 1769480 | tf_op jit(solution)/shard_map/ppermute | solution.py:1566
  30.9 7.6 %collective-permute-start.11 = (bf16[4,64,1152]{2,1,0:T(8,128)(2,1)S(1)}, bf16[4,64,1152]{2,1,0:T(8,128)(2,1)S(1)}, u32[]{:S(2)}, u32[]{:S(2)}) collective-permute-start(bf16[4,64,1152]{2,1,0:T(8,128)(2,1)S(1)} %pad_maximum_fusion.rest_0_), channel_id=1, source_target_pairs={{0,4},{4,0},{8,12},{12,8},{16,20},{20,16},{24,28},{28,24},{1,5},{5... | collective-permute-start | bytes 1769480 | tf_op jit(solution)/shard_map/ppermute | solution.py:1566
  33.2 5.2 %collective-permute-start.14 = (bf16[4,72,384]{2,1,0:T(8,128)(2,1)S(1)}, bf16[4,72,384]{2,1,0:T(8,128)(2,1)S(1)}, u32[]{:S(2)}, u32[]{:S(2)}) collective-permute-start(bf16[4,72,384]{2,1,0:T(8,128)(2,1)S(1)} %collective-permute-done.10.p3), channel_id=1, source_target_pairs={{0,4},{4,0},{8,12},{12,8},{16,20},{20,16},{24,28},{28,24},{1,5},{5... | collective-permute-start | bytes 663560 | tf_op jit(solution)/shard_map/ppermute | solution.py:1566
  33.5 16.2 %collective-permute-start.15 = (bf16[512,512]{1,0:T(8,128)(2,1)S(1)}, bf16[512,512]{1,0:T(8,128)(2,1)S(1)}, u32[]{:S(2)}, u32[]{:S(2)}) collective-permute-start(bf16[512,512]{1,0:T(8,128)(2,1)S(1)} %slice.60), channel_id=1, source_target_pairs={{0,1},{1,2},{2,3},{4,5},{5,6},{6,7},{8,9},{9,10},{10,11},{12,13},{... | collective-permute-start | bytes 1572872 | tf_op jit(solution)/shard_map/ppermute | solution.py:1603
  45.0 12.0 %collective-permute-start.18 = (bf16[2,64,1152]{2,1,0:T(8,128)(2,1)S(1)}, bf16[2,64,1152]{2,1,0:T(8,128)(2,1)S(1)}, u32[]{:S(2)}, u32[]{:S(2)}) collective-permute-start(bf16[2,64,1152]{2,1,0:T(8,128)(2,1)S(1)} %slice.61), channel_id=1, source_target_pairs={{0,8},{4,12},{8,0},{12,4},{16,24},{20,28},{24,16},{28,20},{1,9},{5... | collective-permute-start | bytes 884744 | tf_op jit(solution)/shard_map/ppermute | solution.py:1566
  46.3 10.7 %collective-permute-start.19 = (bf16[2,64,1152]{2,1,0:T(8,128)(2,1)S(1)}, bf16[2,64,1152]{2,1,0:T(8,128)(2,1)S(1)}, u32[]{:S(2)}, u32[]{:S(2)}) collective-permute-start(bf16[2,64,1152]{2,1,0:T(8,128)(2,1)S(1)} %slice.62), channel_id=1, source_target_pairs={{0,16},{4,20},{8,24},{12,28},{16,0},{20,4},{24,8},{28,12},{1,17},{... | collective-permute-start | bytes 884744 | tf_op jit(solution)/shard_map/ppermute | solution.py:1566
  46.8 10.9 %collective-permute-start.20 = (bf16[4,64,1152]{2,1,0:T(8,128)(2,1)S(1)}, bf16[4,64,1152]{2,1,0:T(8,128)(2,1)S(1)}, u32[]{:S(2)}, u32[]{:S(2)}) collective-permute-start(bf16[4,64,1152]{2,1,0:T(8,128)(2,1)S(1)} %collective-permute-done.16.rest_1_), channel_id=1, source_target_pairs={{0,4},{4,0},{8,12},{12,8},{16,20},{20,16},{24,28},{28,24},{1,5},{5... | collective-permute-start | bytes 1769480 | tf_op jit(solution)/shard_map/ppermute | solution.py:1566
  46.8 11.0 %collective-permute-start.21 = (bf16[4,64,1152]{2,1,0:T(8,128)(2,1)S(1)}, bf16[4,64,1152]{2,1,0:T(8,128)(2,1)S(1)}, u32[]{:S(2)}, u32[]{:S(2)}) collective-permute-start(bf16[4,64,1152]{2,1,0:T(8,128)(2,1)S(1)} %collective-permute-done.17.rest_2_), channel_id=1, source_target_pairs={{0,4},{4,0},{8,12},{12,8},{16,20},{20,16},{24,28},{28,24},{1,5},{5... | collective-permute-start | bytes 1769480 | tf_op jit(solution)/shard_map/ppermute | solution.py:1566
  84.0 9.3 %collective-permute-start.26 = (bf16[2,64,1152]{2,1,0:T(8,128)(2,1)S(1)}, bf16[2,64,1152]{2,1,0:T(8,128)(2,1)S(1)}, u32[]{:S(2)}, u32[]{:S(2)}) collective-permute-start(bf16[2,64,1152]{2,1,0:T(8,128)(2,1)S(1)} %get-tuple-element.171), channel_id=1, source_target_pairs={{0,16},{4,20},{8,24},{12,28},{16,0},{20,4},{24,8},{28,12},{1,17},{... | collective-permute-start | bytes 884744 | tf_op jit(solution)/shard_map/ppermute | solution.py:1566
  84.6 9.0 %collective-permute-start.25 = (bf16[2,64,1152]{2,1,0:T(8,128)(2,1)S(1)}, bf16[2,64,1152]{2,1,0:T(8,128)(2,1)S(1)}, u32[]{:S(2)}, u32[]{:S(2)}) collective-permute-start(bf16[2,64,1152]{2,1,0:T(8,128)(2,1)S(1)} %get-tuple-element.172), channel_id=1, source_target_pairs={{0,8},{4,12},{8,0},{12,4},{16,24},{20,28},{24,16},{28,20},{1,9},{5... | collective-permute-start | bytes 884744 | tf_op jit(solution)/shard_map/ppermute | solution.py:1566
  90.3 18.6 %collective-permute-start.27 = (bf16[512,512]{1,0:T(8,128)(2,1)S(1)}, bf16[512,512]{1,0:T(8,128)(2,1)S(1)}, u32[]{:S(2)}, u32[]{:S(2)}) collective-permute-start(bf16[512,512]{1,0:T(8,128)(2,1)S(1)} %get-tuple-element.132), channel_id=1, source_target_pairs={{1,0},{2,1},{3,2},{5,4},{6,5},{7,6},{9,8},{10,9},{11,10},{13,12},{... | collective-permute-start | bytes 1572872 | tf_op jit(solution)/shard_map/ppermute | solution.py:1632
  93.8 15.1 %collective-permute-start.35 = (bf16[4,64,1152]{2,1,0:T(8,128)(2,1)S(1)}, bf16[4,64,1152]{2,1,0:T(8,128)(2,1)S(1)}, u32[]{:S(2)}, u32[]{:S(2)}) collective-permute-start(bf16[4,64,1152]{2,1,0:T(8,128)(2,1)S(1)} %pad_maximum_fusion.1), channel_id=1, source_target_pairs={{0,8},{4,12},{8,0},{12,4},{16,24},{20,28},{24,16},{28,20},{1,9},{5... | collective-permute-start | bytes 1769480 | tf_op jit(solution)/shard_map/ppermute | solution.py:1566
  94.5 14.5 %collective-permute-start.36 = (bf16[4,64,1152]{2,1,0:T(8,128)(2,1)S(1)}, bf16[4,64,1152]{2,1,0:T(8,128)(2,1)S(1)}, u32[]{:S(2)}, u32[]{:S(2)}) collective-permute-start(bf16[4,64,1152]{2,1,0:T(8,128)(2,1)S(1)} %pad_maximum_fusion.2), channel_id=1, source_target_pairs={{0,16},{4,20},{8,24},{12,28},{16,0},{20,4},{24,8},{28,12},{1,17},{... | collective-permute-start | bytes 1769480 | tf_op jit(solution)/shard_map/ppermute | solution.py:1566
  111.7 9.5 %collective-permute-start.29 = (bf16[4,72,384]{2,1,0:T(8,128)(2,1)S(1)}, bf16[4,72,384]{2,1,0:T(8,128)(2,1)S(1)}, u32[]{:S(2)}, u32[]{:S(2)}) collective-permute-start(bf16[4,72,384]{2,1,0:T(8,128)(2,1)S(1)} %get-tuple-element.174), channel_id=1, source_target_pairs={{0,8},{4,12},{8,0},{12,4},{16,24},{20,28},{24,16},{28,20},{1,9},{5... | collective-permute-start | bytes 663560 | tf_op jit(solution)/shard_map/ppermute | solution.py:1566
  113.3 11.7 %collective-permute-start.31 = (bf16[4,72,384]{2,1,0:T(8,128)(2,1)S(1)}, bf16[4,72,384]{2,1,0:T(8,128)(2,1)S(1)}, u32[]{:S(2)}, u32[]{:S(2)}) collective-permute-start(bf16[4,72,384]{2,1,0:T(8,128)(2,1)S(1)} %get-tuple-element.175), channel_id=1, source_target_pairs={{0,24},{4,28},{8,16},{12,20},{16,8},{20,12},{24,0},{28,4},{1,25},{... | collective-permute-start | bytes 663560 | tf_op jit(solution)/shard_map/ppermute | solution.py:1566
  114.7 11.6 %collective-permute-start.30 = (bf16[4,72,384]{2,1,0:T(8,128)(2,1)S(1)}, bf16[4,72,384]{2,1,0:T(8,128)(2,1)S(1)}, u32[]{:S(2)}, u32[]{:S(2)}) collective-permute-start(bf16[4,72,384]{2,1,0:T(8,128)(2,1)S(1)} %get-tuple-element.176), channel_id=1, source_target_pairs={{0,16},{4,20},{8,24},{12,28},{16,0},{20,4},{24,8},{28,12},{1,17},{... | collective-permute-start | bytes 663560 | tf_op jit(solution)/shard_map/ppermute | solution.py:1566
  115.3 15.2 %collective-permute-start.39 = (bf16[64,1152]{1,0:T(8,128)(2,1)S(1)}, bf16[64,1152]{1,0:T(8,128)(2,1)S(1)}, u32[]{:S(2)}, u32[]{:S(2)}) collective-permute-start(bf16[64,1152]{1,0:T(8,128)(2,1)S(1)} %get-tuple-element.177), channel_id=1, source_target_pairs={{0,3},{1,0},{2,1},{3,2},{4,7},{5,4},{6,5},{7,6},{8,11},{9,8},{10,9... | collective-permute-start | bytes 442376 | tf_op jit(solution)/shard_map/ppermute | solution.py:1570
  121.1 14.4 %collective-permute-start.38 = (bf16[64,1152]{1,0:T(8,128)(2,1)S(1)}, bf16[64,1152]{1,0:T(8,128)(2,1)S(1)}, u32[]{:S(2)}, u32[]{:S(2)}) collective-permute-start(bf16[64,1152]{1,0:T(8,128)(2,1)S(1)} %get-tuple-element.178), channel_id=1, source_target_pairs={{0,2},{1,3},{2,0},{3,1},{4,6},{5,7},{6,4},{7,5},{8,10},{9,11},{10,... | collective-permute-start | bytes 442376 | tf_op jit(solution)/shard_map/ppermute | solution.py:1570
  121.1 14.4 %collective-permute-start.37 = (bf16[64,1152]{1,0:T(8,128)(2,1)S(1)}, bf16[64,1152]{1,0:T(8,128)(2,1)S(1)}, u32[]{:S(2)}, u32[]{:S(2)}) collective-permute-start(bf16[64,1152]{1,0:T(8,128)(2,1)S(1)} %get-tuple-element.179), channel_id=1, source_target_pairs={{0,1},{1,2},{2,3},{3,0},{4,5},{5,6},{6,7},{7,4},{8,9},{9,10},{10,1... | collective-permute-start | bytes 442376 | tf_op jit(solution)/shard_map/ppermute | solution.py:1570
  126.5 9.8 %collective-permute-start.34 = (bf16[72,384]{1,0:T(8,128)(2,1)S(1)}, bf16[72,384]{1,0:T(8,128)(2,1)S(1)}, u32[]{:S(2)}, u32[]{:S(2)}) collective-permute-start(bf16[72,384]{1,0:T(8,128)(2,1)S(1)} %get-tuple-element.180), channel_id=1, source_target_pairs={{0,3},{1,0},{2,1},{3,2},{4,7},{5,4},{6,5},{7,6},{8,11},{9,8},{10,9... | collective-permute-start | bytes 165896 | tf_op jit(solution)/shard_map/ppermute | solution.py:1570
  129.8 7.4 %collective-permute-start.33 = (bf16[72,384]{1,0:T(8,128)(2,1)S(1)}, bf16[72,384]{1,0:T(8,128)(2,1)S(1)}, u32[]{:S(2)}, u32[]{:S(2)}) collective-permute-start(bf16[72,384]{1,0:T(8,128)(2,1)S(1)} %get-tuple-element.181), channel_id=1, source_target_pairs={{0,2},{1,3},{2,0},{3,1},{4,6},{5,7},{6,4},{7,5},{8,10},{9,11},{10,... | collective-permute-start | bytes 165896 | tf_op jit(solution)/shard_map/ppermute | solution.py:1570
  130.5 6.8 %collective-permute-start.32 = (bf16[72,384]{1,0:T(8,128)(2,1)S(1)}, bf16[72,384]{1,0:T(8,128)(2,1)S(1)}, u32[]{:S(2)}, u32[]{:S(2)}) collective-permute-start(bf16[72,384]{1,0:T(8,128)(2,1)S(1)} %get-tuple-element.182), channel_id=1, source_target_pairs={{0,1},{1,2},{2,3},{3,0},{4,5},{5,6},{6,7},{7,4},{8,9},{9,10},{10,1... | collective-permute-start | bytes 165896 | tf_op jit(solution)/shard_map/ppermute | solution.py:1570
  (14 other events, 102.2 us)
